TPU v7x, 32 devices: a whole 2x2x4 slice. The times are simulated.
32 devices in a mesh: dp: 4 (over z), mp: 8 (over y, x, core).
Axes of the slice: x: 2, y: 2, z: 4, core: 2. Of those that a mesh axis runs over, the one named last changes fastest.
Arguments:
- tokens: bfloat16 [16384, 2048], P('dp', 'mp'), may hold values from -6 to 6
- norm_gains: float32 [2, 2048], replicated, may hold values from 0.5 to 1.5
- query_key_value_weight: bfloat16 [3, 2048, 2048], P(None, None, 'mp'), may hold values from -0.125 to 0.125
- output_weight: bfloat16 [2048, 2048], P('mp'), may hold values from -0.125 to 0.125
- gate_up_weight: bfloat16 [2, 2048, 5632], P(None, None, 'mp'), may hold values from -0.125 to 0.125
- down_weight: bfloat16 [5632, 2048], P('mp'), may hold values from -0.078125 to 0.078125
- a_in: float32 [6, 2048, 16], P(None, ('dp', 'mp')), may hold values from -0.125 to 0.125
- a_down: float32 [5632, 16], P(('dp', 'mp')), may hold values from -0.078125 to 0.078125
- b_dmodel: float32 [5, 16, 2048], P(None, None, ('dp', 'mp')), may hold values from -0.375 to 0.375
- b_hidden: float32 [2, 16, 5632], P(None, None, ('dp', 'mp')), may hold values from -0.375 to 0.375
- m_dmodel: float32 [5, 2048], P(None, ('dp', 'mp')), may hold values from 0.8 to 8, as said below
- m_hidden: float32 [2, 5632], P(None, ('dp', 'mp')), may hold values from 0.7 to 1.6
- segment_ids: int32 [8, 2048], P('dp'), may hold values from 0 to 7, as said below
- valid_mask: int32 [8, 2048], P('dp'), may hold values from 0 to 1, as said below
- cotangent: bfloat16 [16384, 2048], P('dp', 'mp'), may hold values from -6 to 6
Outputs:
- activations: bfloat16 [16384, 2048], P('dp', 'mp')
- input_grad: bfloat16 [16384, 2048], P('dp', 'mp')
- grad_a_in: float32 [6, 2048, 16], P(None, ('dp', 'mp'))
- grad_a_down: float32 [5632, 16], P(('dp', 'mp'))
- grad_b_dmodel: float32 [5, 16, 2048], P(None, None, ('dp', 'mp'))
- grad_b_hidden: float32 [2, 16, 5632], P(None, None, ('dp', 'mp'))
- grad_m_dmodel: float32 [5, 2048], P(None, ('dp', 'mp'))
- grad_m_hidden: float32 [2, 5632], P(None, ('dp', 'mp'))
Inputs may be any that keep to these rules, and one draw needn't show every extreme that they name: `segment_ids`: in each row the segment numbers never fall, begin at 0 and take every value up to 7. `valid_mask`: in each row the ones come first, followed by 1 to 256 zeros. `m_dmodel`: magnitudes of q, k and v lie in 0.8 to 1.6, of o in 3 to 8, of down in 1.2 to 3.
All inputs are finite; a program needn't handle non-finite values.
Results may differ from a plain program's by a relative error of at most 0.025.
Values may be sent and summed in bfloat16 or wider, within the bound.
No kernel may reach another device: no remote copies, remote signals or barrier semaphores. Data moves between devices by JAX's collectives and lax.ppermute only.
A program may use at most 384 MiB of HBM per device.

v0:
```python
import jax
import jax.numpy as jnp
from jax import lax
from jax.sharding import PartitionSpec as P

D = 2048
HEAD = 128
FF = 5632


EPSILON = 1e-05
ADAPTER_SCALE = 2.0
ROPE_BASE = 10000.0
MASKED = -1e30
HIGHEST = lax.Precision.HIGHEST


def own_block(values, block_width, along):
    return lax.dynamic_slice_in_dim(values, lax.axis_index("mp") * block_width, block_width, along)


def embedding_block(values, length, along):
    dims_out = list(values.shape)
    dims_out[along] = length
    holder = jnp.zeros(dims_out, jnp.float32)
    return lax.dynamic_update_slice_in_dim(
        holder, values, lax.axis_index("mp") * values.shape[along], along
    )


def token_sums(values):
    return lax.psum(values, "mp")


def lowrank_sums(values):
    return lax.psum(values.astype(jnp.bfloat16), "mp").astype(jnp.float32)


def gather_features(values):
    return lax.all_gather(values, "mp", axis=1, tiled=True)


def scatter_inputs(values):
    return lax.psum_scatter(
        values.astype(jnp.bfloat16), "mp", scatter_dimension=1, tiled=True
    ).astype(jnp.float32)


def positions(segments):
    index = jnp.broadcast_to(
        jnp.arange(segments.shape[1], dtype=jnp.int32)[None, :], segments.shape
    )
    earlier = jnp.concatenate([segments[:, :1] - 1, segments[:, :-1]], axis=1)
    starts = lax.cummax(jnp.where(segments != earlier, index, 0), axis=1)
    return index - starts


def rope_tables(segments):
    half_size = HEAD // 2
    frequency = ROPE_BASE ** (-(jnp.arange(half_size, dtype=jnp.float32) * (2.0 / HEAD)))
    angles = positions(segments).astype(jnp.float32)[..., None] * frequency
    angles = jnp.concatenate([angles, angles], axis=-1)
    return (jnp.cos(angles)[:, :, None, :], jnp.sin(angles)[:, :, None, :])


def rotate(values):
    half_size = values.shape[-1] // 2
    return jnp.concatenate([-values[..., half_size:], values[..., :half_size]], axis=-1)


def rotate_back(values):
    half_size = values.shape[-1] // 2
    return jnp.concatenate([values[..., half_size:], -values[..., :half_size]], axis=-1)


def visible(segment_block, query_index, segments, valid, key_index):
    same_segment = segment_block[:, :, None] == segments[:, None, :]
    causal = key_index[None, None, :] <= query_index[None, :, None]
    keep_key = (valid[:, None, :] > 0) | (key_index[None, None, :] == query_index[None, :, None])
    return (same_segment & causal & keep_key)[:, None, :, :]


def attention_forward(query, keys, values, segments, valid):
    row_count, length, head_count, head_size = query.shape
    block_rows = min(512, length)
    factor = head_size ** (-0.5)
    key_index = jnp.arange(length, dtype=jnp.int32)

    def one_block(start):
        query_block = lax.dynamic_slice_in_dim(query, start, block_rows, 1)
        allowed = visible(
            lax.dynamic_slice_in_dim(segments, start, block_rows, 1),
            start + jnp.arange(block_rows, dtype=jnp.int32),
            segments,
            valid,
            key_index,
        )
        scores = (
            jnp.einsum("rqhe,rkhe->rhqk", query_block, keys, preferred_element_type=jnp.float32)
            * factor
        )
        masked = jnp.where(allowed, scores, MASKED)
        maxima = jnp.max(masked, axis=-1, keepdims=True)
        weights = jnp.exp(masked - maxima)
        denominator = jnp.sum(weights, axis=-1, keepdims=True)
        weights_low = (weights / denominator).astype(jnp.bfloat16)
        attended = jnp.einsum(
            "rhqk,rkhe->rqhe", weights_low, values, preferred_element_type=jnp.float32
        )
        return (attended, (maxima + jnp.log(denominator))[..., 0])

    starts = jnp.arange(length // block_rows, dtype=jnp.int32) * block_rows
    attended, log_total = lax.map(one_block, starts)
    attended = jnp.moveaxis(attended, 0, 1).reshape(row_count, length, head_count, head_size)
    log_total = jnp.transpose(log_total, (1, 2, 0, 3)).reshape(row_count, head_count, length)
    return (attended, log_total)


def attention_backward(query, keys, values, segments, valid, log_total, grad_attended):
    row_count, length, head_count, head_size = query.shape
    block_rows = min(512, length)
    factor = head_size ** (-0.5)
    key_index = jnp.arange(length, dtype=jnp.int32)

    def one_block(carry, start):
        grad_keys, grad_values = carry
        query_block = lax.dynamic_slice_in_dim(query, start, block_rows, 1)
        grad_block = lax.dynamic_slice_in_dim(grad_attended, start, block_rows, 1)
        allowed = visible(
            lax.dynamic_slice_in_dim(segments, start, block_rows, 1),
            start + jnp.arange(block_rows, dtype=jnp.int32),
            segments,
            valid,
            key_index,
        )
        scores = (
            jnp.einsum("rqhe,rkhe->rhqk", query_block, keys, preferred_element_type=jnp.float32)
            * factor
        )
        shifted = scores - lax.dynamic_slice_in_dim(log_total, start, block_rows, 2)[..., None]
        weights = jnp.exp(jnp.where(allowed, shifted, MASKED))
        grad_weights = jnp.einsum(
            "rqhe,rkhe->rhqk", grad_block, values, preferred_element_type=jnp.float32
        )
        inner = jnp.sum(weights * grad_weights, axis=-1, keepdims=True)
        grad_scores = (weights * (grad_weights - inner)).astype(jnp.bfloat16)
        grad_query = (
            jnp.einsum("rhqk,rkhe->rqhe", grad_scores, keys, preferred_element_type=jnp.float32)
            * factor
        )
        grad_keys = (
            grad_keys
            + jnp.einsum(
                "rhqk,rqhe->rkhe", grad_scores, query_block, preferred_element_type=jnp.float32
            )
            * factor
        )
        grad_values = grad_values + jnp.einsum(
            "rhqk,rqhe->rkhe",
            weights.astype(jnp.bfloat16),
            grad_block,
            preferred_element_type=jnp.float32,
        )
        return ((grad_keys, grad_values), grad_query)

    starts = jnp.arange(length // block_rows, dtype=jnp.int32) * block_rows
    empty = jnp.zeros(query.shape, jnp.float32)
    (grad_keys, grad_values), grad_query = lax.scan(one_block, (empty, empty), starts)
    grad_query = jnp.moveaxis(grad_query, 0, 1).reshape(row_count, length, head_count, head_size)
    return (grad_query, grad_keys, grad_values)


def column_forward(normed_input, weights, adapters_a, adapters_b, magnitudes, norms):
    adapter_product = jnp.einsum(
        "td,kdr->ktr", normed_input, adapters_a, preferred_element_type=jnp.float32
    ).astype(jnp.bfloat16)
    frozen_product = jnp.einsum(
        "td,kdc->ktc", normed_input, weights, preferred_element_type=jnp.float32
    )
    unscaled_output = frozen_product + ADAPTER_SCALE * jnp.einsum(
        "ktr,krc->ktc", adapter_product, adapters_b, preferred_element_type=jnp.float32
    )
    return (unscaled_output, adapter_product, unscaled_output * (magnitudes / norms)[:, None, :])


def column_backward(
    grad_y,
    unscaled_output,
    adapter_product,
    merged_weight,
    norms,
    magnitudes,
    normed_input,
    weights,
    adapters_a,
    adapters_b,
    feature_own,
):
    grad_scale = jnp.sum(grad_y * unscaled_output, axis=1)
    grad_mag = grad_scale / norms
    coeffs = grad_scale * magnitudes / (norms * norms * norms)
    grad_pre = (grad_y * (magnitudes / norms)[:, None, :]).astype(jnp.bfloat16)
    grad_low = lowrank_sums(
        ADAPTER_SCALE
        * jnp.einsum("ktc,krc->ktr", grad_pre, adapters_b, preferred_element_type=jnp.float32)
    ).astype(jnp.bfloat16)
    partial_in = jnp.einsum("ktc,kdc->td", grad_pre, weights, preferred_element_type=jnp.float32)
    grad_in = scatter_inputs(partial_in)
    grad_in = grad_in + jnp.einsum(
        "ktr,kdr->td",
        grad_low,
        own_block(adapters_a, feature_own, 1),
        preferred_element_type=jnp.float32,
    )
    weighted = merged_weight * coeffs[:, None, :]
    local_contribution = jnp.einsum(
        "td,ktr->kdr",
        own_block(normed_input, feature_own, 1),
        grad_low,
        preferred_element_type=jnp.float32,
    )
    first_adapter_gradient = embedding_block(
        local_contribution, normed_input.shape[1], 1
    ) - ADAPTER_SCALE * jnp.einsum(
        "kdc,krc->kdr", weighted, adapters_b.astype(jnp.float32), precision=HIGHEST
    )
    second_adapter_gradient = ADAPTER_SCALE * (
        jnp.einsum("ktr,ktc->krc", adapter_product, grad_pre, preferred_element_type=jnp.float32)
        - jnp.einsum("kdr,kdc->krc", adapters_a.astype(jnp.float32), weighted, precision=HIGHEST)
    )
    return (grad_in, first_adapter_gradient, second_adapter_gradient, grad_mag)


def row_forward(inputs, weight_matrix, first_adapter, second_adapter, magnitude, norm_full):
    partial_value = jnp.dot(inputs, weight_matrix, preferred_element_type=jnp.float32)
    local_portion = lax.psum_scatter(
        partial_value.astype(jnp.bfloat16), "mp", scatter_dimension=1, tiled=True
    ).astype(jnp.float32)
    width_own = local_portion.shape[1]
    adapter_product = lowrank_sums(
        jnp.dot(inputs, first_adapter, preferred_element_type=jnp.float32)
    ).astype(jnp.bfloat16)
    unscaled_output = local_portion + ADAPTER_SCALE * jnp.dot(
        adapter_product, own_block(second_adapter, width_own, 1), preferred_element_type=jnp.float32
    )
    return (
        unscaled_output,
        adapter_product,
        unscaled_output * own_block(magnitude / norm_full, width_own, 0),
    )


def row_backward(
    grad_y,
    unscaled_output,
    adapter_product,
    merged_weight,
    norm_full,
    magnitude,
    inputs,
    weight_matrix,
    first_adapter,
    second_adapter,
):
    width_own = grad_y.shape[1]
    norm_own = own_block(norm_full, width_own, 0)
    mag_own = own_block(magnitude, width_own, 0)
    grad_scale = jnp.sum(grad_y * unscaled_output, axis=0)
    grad_mag = grad_scale / norm_own
    coef_own = grad_scale * mag_own / (norm_own * norm_own * norm_own)
    grad_pre = (grad_y * (mag_own / norm_own)).astype(jnp.bfloat16)
    pre_whole, coef_whole = (
        lax.all_gather(grad_pre, "mp", axis=1, tiled=True),
        lax.all_gather(coef_own.astype(jnp.bfloat16), "mp", axis=0, tiled=True).astype(
            coef_own.dtype
        ),
    )
    grad_low = (
        ADAPTER_SCALE
        * jnp.einsum("td,rd->tr", pre_whole, second_adapter, preferred_element_type=jnp.float32)
    ).astype(jnp.bfloat16)
    grad_in = jnp.einsum("td,id->ti", pre_whole, weight_matrix, preferred_element_type=jnp.float32)
    grad_in = grad_in + jnp.einsum(
        "tr,ir->ti", grad_low, first_adapter, preferred_element_type=jnp.float32
    )
    weighted = merged_weight * coef_whole
    first_adapter_gradient = jnp.einsum(
        "ti,tr->ir", inputs, grad_low, preferred_element_type=jnp.float32
    ) - ADAPTER_SCALE * jnp.einsum(
        "id,rd->ir", weighted, second_adapter.astype(jnp.float32), precision=HIGHEST
    )
    local_contribution = jnp.einsum(
        "tr,tc->rc", adapter_product, grad_pre, preferred_element_type=jnp.float32
    )
    second_adapter_gradient = ADAPTER_SCALE * (
        embedding_block(local_contribution, D, 1)
        - jnp.einsum("ir,id->rd", first_adapter.astype(jnp.float32), weighted, precision=HIGHEST)
    )
    return (
        grad_in,
        first_adapter_gradient,
        second_adapter_gradient,
        embedding_block(grad_mag, D, 0),
    )


def norm_backward(grad_normed, stream_own, inverse_rms, gain_own):
    inner = token_sums(jnp.sum(stream_own * gain_own * grad_normed, axis=1))
    cubed = inverse_rms * inverse_rms * inverse_rms
    return inverse_rms[:, None] * gain_own * grad_normed - stream_own * (cubed * inner / D)[:, None]


def local(
    tokens,
    norm_gains,
    query_key_value_weight,
    output_weight,
    gate_up_weight,
    down_weight,
    a_in,
    a_down,
    b_dmodel,
    b_hidden,
    m_dmodel,
    m_hidden,
    segment_ids,
    valid_mask,
    cotangent,
):
    width_own = tokens.shape[1]
    hidden_own = gate_up_weight.shape[2]
    (
        gathered_input,
        gathered_down,
        gathered_b_model,
        gathered_b_hidden,
        gathered_mag_model,
        gathered_mag_hidden,
    ) = (
        lax.all_gather(a_in.astype(jnp.bfloat16), ("dp", "mp"), axis=1, tiled=True),
        lax.all_gather(a_down.astype(jnp.bfloat16), ("dp", "mp"), axis=0, tiled=True),
        lax.all_gather(b_dmodel.astype(jnp.bfloat16), ("dp", "mp"), axis=2, tiled=True),
        lax.all_gather(b_hidden.astype(jnp.bfloat16), ("dp", "mp"), axis=2, tiled=True),
        lax.all_gather(m_dmodel.astype(jnp.bfloat16), ("dp", "mp"), axis=1, tiled=True),
        lax.all_gather(m_hidden.astype(jnp.bfloat16), ("dp", "mp"), axis=1, tiled=True),
    )
    mag_dm = gathered_mag_model.astype(jnp.float32)
    hidden_magnitude = gathered_mag_hidden.astype(jnp.float32)
    out_a = own_block(gathered_input[3], width_own, 0)
    down_a = own_block(gathered_down, hidden_own, 0)
    output_merged = output_weight.astype(jnp.float32) + ADAPTER_SCALE * jnp.dot(
        out_a, gathered_b_model[3], preferred_element_type=jnp.float32
    )
    down_merged = down_weight.astype(jnp.float32) + ADAPTER_SCALE * jnp.dot(
        down_a, gathered_b_model[4], preferred_element_type=jnp.float32
    )
    out_sq, down_sq = lax.psum(
        (
            jnp.sum(output_merged * output_merged, axis=0),
            jnp.sum(down_merged * down_merged, axis=0),
        ),
        "mp",
    )
    out_norm = jnp.sqrt(out_sq)
    down_norm = jnp.sqrt(down_sq)
    qkv_b = own_block(gathered_b_model[0:3], width_own, 2)
    qkv_mag = own_block(mag_dm[0:3], width_own, 1)
    query_key_value_merged = query_key_value_weight.astype(
        jnp.float32
    ) + ADAPTER_SCALE * jnp.einsum(
        "kdr,krc->kdc", gathered_input[0:3], qkv_b, preferred_element_type=jnp.float32
    )
    qkv_norm = jnp.sqrt(jnp.sum(query_key_value_merged * query_key_value_merged, axis=1))
    gu_b = own_block(gathered_b_hidden, hidden_own, 2)
    gu_mag = own_block(hidden_magnitude, hidden_own, 1)
    gate_up_merged = gate_up_weight.astype(jnp.float32) + ADAPTER_SCALE * jnp.einsum(
        "kdr,krc->kdc", gathered_input[4:6], gu_b, preferred_element_type=jnp.float32
    )
    gu_norm = jnp.sqrt(jnp.sum(gate_up_merged * gate_up_merged, axis=1))
    stream = tokens.astype(jnp.float32)
    gains_own = own_block(norm_gains, width_own, 1)
    first_rms = lax.rsqrt(token_sums(jnp.sum(stream * stream, axis=1)) / D + EPSILON)
    normed_first = gather_features(
        (stream * first_rms[:, None] * gains_own[0]).astype(jnp.bfloat16)
    )
    row_count = segment_ids.shape[0]
    length = segment_ids.shape[1]
    shape_four = (row_count, length, width_own // HEAD, HEAD)
    cosine, sine = rope_tables(segment_ids)
    qkv_pre, qkv_low, qkv_out = column_forward(
        normed_first, query_key_value_weight, gathered_input[0:3], qkv_b, qkv_mag, qkv_norm
    )
    query = (
        qkv_out[0].reshape(shape_four) * cosine + rotate(qkv_out[0].reshape(shape_four)) * sine
    ).astype(jnp.bfloat16)
    keys = (
        qkv_out[1].reshape(shape_four) * cosine + rotate(qkv_out[1].reshape(shape_four)) * sine
    ).astype(jnp.bfloat16)
    values = qkv_out[2].reshape(shape_four).astype(jnp.bfloat16)
    attended, log_total = attention_forward(query, keys, values, segment_ids, valid_mask)
    attended_low = attended.reshape(row_count * length, width_own).astype(jnp.bfloat16)
    out_pre, out_low, out_y = row_forward(
        attended_low, output_weight, out_a, gathered_b_model[3], mag_dm[3], out_norm
    )
    middle = stream + out_y
    second_rms = lax.rsqrt(token_sums(jnp.sum(middle * middle, axis=1)) / D + EPSILON)
    normed_second = gather_features(
        (middle * second_rms[:, None] * gains_own[1]).astype(jnp.bfloat16)
    )
    gu_pre, gu_low, gu_out = column_forward(
        normed_second, gate_up_weight, gathered_input[4:6], gu_b, gu_mag, gu_norm
    )
    gate_sig = jax.nn.sigmoid(gu_out[0])
    hidden = (gu_out[0] * gate_sig * gu_out[1]).astype(jnp.bfloat16)
    down_pre, down_low, down_y = row_forward(
        hidden, down_weight, down_a, gathered_b_model[4], mag_dm[4], down_norm
    )
    activations = (middle + down_y).astype(jnp.bfloat16)
    grad_output = cotangent.astype(jnp.float32)
    grad_hidden, down_ga, down_gb, down_gm = row_backward(
        grad_output,
        down_pre,
        down_low,
        down_merged,
        down_norm,
        mag_dm[4],
        hidden,
        down_weight,
        down_a,
        gathered_b_model[4],
    )
    silu_slope = gate_sig * (1.0 + gu_out[0] * (1.0 - gate_sig))
    grad_gu = jnp.stack([grad_hidden * gu_out[1] * silu_slope, grad_hidden * gu_out[0] * gate_sig])
    grad_second, gu_ga, gu_gb, gu_gm = column_backward(
        grad_gu,
        gu_pre,
        gu_low,
        gate_up_merged,
        gu_norm,
        gu_mag,
        normed_second,
        gate_up_weight,
        gathered_input[4:6],
        gu_b,
        width_own,
    )
    grad_middle = grad_output + norm_backward(grad_second, middle, second_rms, gains_own[1])
    grad_att, out_ga, out_gb, out_gm = row_backward(
        grad_middle,
        out_pre,
        out_low,
        output_merged,
        out_norm,
        mag_dm[3],
        attended_low,
        output_weight,
        out_a,
        gathered_b_model[3],
    )
    grad_att = grad_att.astype(jnp.bfloat16).reshape(shape_four)
    grad_query, grad_keys, grad_values = attention_backward(
        query, keys, values, segment_ids, valid_mask, log_total, grad_att
    )
    grad_qkv = jnp.stack(
        [
            (grad_query * cosine + rotate_back(grad_query * sine)).reshape(
                row_count * length, width_own
            ),
            (grad_keys * cosine + rotate_back(grad_keys * sine)).reshape(
                row_count * length, width_own
            ),
            grad_values.reshape(row_count * length, width_own),
        ]
    )
    grad_first, qkv_ga, qkv_gb, qkv_gm = column_backward(
        grad_qkv,
        qkv_pre,
        qkv_low,
        query_key_value_merged,
        qkv_norm,
        qkv_mag,
        normed_first,
        query_key_value_weight,
        gathered_input[0:3],
        qkv_b,
        width_own,
    )
    input_grad = (grad_middle + norm_backward(grad_first, stream, first_rms, gains_own[0])).astype(
        jnp.bfloat16
    )
    term_a_in = jnp.concatenate([qkv_ga, embedding_block(out_ga, D, 0)[None], gu_ga], axis=0)
    term_a_down = embedding_block(down_ga, FF, 0)
    term_b_dmodel = jnp.concatenate(
        [embedding_block(qkv_gb, D, 2), out_gb[None], down_gb[None]], axis=0
    )
    term_b_hidden = embedding_block(gu_gb, FF, 2)
    term_m_dmodel = jnp.concatenate(
        [embedding_block(qkv_gm, D, 1), out_gm[None], down_gm[None]], axis=0
    )
    term_m_hidden = embedding_block(gu_gm, FF, 1)
    grad_a_in, grad_a_down, grad_b_dmodel, grad_b_hidden, grad_m_dmodel, grad_m_hidden = (
        lax.psum_scatter(term_a_in, ("dp", "mp"), scatter_dimension=1, tiled=True),
        lax.psum_scatter(term_a_down, ("dp", "mp"), scatter_dimension=0, tiled=True),
        lax.psum_scatter(term_b_dmodel, ("dp", "mp"), scatter_dimension=2, tiled=True),
        lax.psum_scatter(term_b_hidden, ("dp", "mp"), scatter_dimension=2, tiled=True),
        lax.psum_scatter(term_m_dmodel, ("dp", "mp"), scatter_dimension=1, tiled=True),
        lax.psum_scatter(term_m_hidden, ("dp", "mp"), scatter_dimension=1, tiled=True),
    )
    return (
        activations,
        input_grad,
        grad_a_in,
        grad_a_down,
        grad_b_dmodel,
        grad_b_hidden,
        grad_m_dmodel,
        grad_m_hidden,
    )


def solution(mesh):
    in_specs = (
        P("dp", "mp"),
        P(),
        P(None, None, "mp"),
        P("mp", None),
        P(None, None, "mp"),
        P("mp", None),
        P(None, ("dp", "mp"), None),
        P(("dp", "mp"), None),
        P(None, None, ("dp", "mp")),
        P(None, None, ("dp", "mp")),
        P(None, ("dp", "mp")),
        P(None, ("dp", "mp")),
        P("dp", None),
        P("dp", None),
        P("dp", "mp"),
    )
    out_specs = (
        P("dp", "mp"),
        P("dp", "mp"),
        P(None, ("dp", "mp"), None),
        P(("dp", "mp"), None),
        P(None, None, ("dp", "mp")),
        P(None, None, ("dp", "mp")),
        P(None, ("dp", "mp")),
        P(None, ("dp", "mp")),
    )
    return jax.shard_map(local, mesh=mesh, in_specs=in_specs, out_specs=out_specs, check_vma=False)
```

profile of v0, /device:TPU:0, one launch (start us, length us, event | category | flops | bytes accessed | tf_op | source)
XLA Modules:
  0.0 2742.1 jit_solution(5464512786599498084)
XLA Ops:
  8.2 58.2 %all_gather.37 = bf16[6,2048,16]{2,0,1:T(8,128)(2,1)S(1)} all-gather(bf16[6,64,16]{2,0,1:T(8,128)(2,1)S(1)} %copy.155), channel_id=1, replica_groups=mesh['dp'=4,'mp'=8] {'dp','mp'}, dimensions={1}, use_global_device_ids=true | all-gather | bytes 405504 | tf_op jit(solution)/shard_map/all_gather | solution.py:340
  69.9 60.4 %all_gather.38 = bf16[5,16,2048]{1,0,2:T(8,128)(2,1)S(1)} all-gather(bf16[5,16,64]{1,0,2:T(8,128)(2,1)S(1)} %copy.157), channel_id=1, replica_groups=mesh['dp'=4,'mp'=8] {'dp','mp'}, dimensions={2}, use_global_device_ids=true | all-gather | bytes 337920 | tf_op jit(solution)/shard_map/all_gather | solution.py:342
  139.9 23.8 all-reduce.1
  178.1 37.6 %all-gather = bf16[32,64,5]{1,2,0:T(8,128)(2,1)S(1)} all-gather(bf16[1,64,5]{1,2,0:T(8,128)(2,1)S(1)} %convert_bitcast_fusion.2), channel_id=1, replica_groups=mesh['dp'=4,'mp'=8] {'dp','mp'}, dimensions={0}, use_global_device_ids=true | all-gather | bytes 21120 | tf_op jit(solution)/shard_map/all_gather | solution.py:344
  232.1 28.7 %all-gather.10.cloned.1.call-done = bf16[4096,2048]{1,0:T(8,128)(2,1)} async-done(((bf16[4096,256]{1,0:T(8,128)(2,1)}), bf16[4096,2048]{1,0:T(8,128)(2,1)}) %all-gather.10.cloned.1.call-update) | async-done | bytes 16777232 | tf_op jit(solution)/shard_map/all_gather | solution.py:40
  279.0 25.5 broadcast_multiply_fusion.1
  340.1 11.6 slice_negate_fusion.2
  360.1 111.9 %while.32 = (s32[]{:T(128)}, bf16[4,2,512,2,128]{4,2,3,1,0:T(8,128)(2,1)}, f32[4,2,2,512]{3,2,1,0:T(2,128)}, s32[4]{0:T(128)S(1)}, s32[2,2048]{1,0:T(2,128)S(1)}...) while((s32[]{:T(128)}, ...), condition=%wide.region_8.9_spmd.clone.clone.clone, body=%wide.region_5.8_spmd.clone.clone.sunk.clone | while | flops 2208303616 | bytes 77194416 | solution.py:113
  491.4 41.3 %all-gather.2 = bf16[32,176,16]{1,2,0:T(8,128)(2,1)S(1)} all-gather(bf16[1,176,16]{1,2,0:T(8,128)(2,1)S(1)} %convert_bitcast_fusion.1), channel_id=1, replica_groups=mesh['dp'=4,'mp'=8] {'dp','mp'}, dimensions={0}, use_global_device_ids=true | all-gather | bytes 185856 | tf_op jit(solution)/shard_map/all_gather | solution.py:341
  540.3 111.3 %reduce-scatter.23.cloned.1.call-done = bf16[4096,256]{1,0:T(8,128)(2,1)} async-done(((bf16[4096,2048]{1,0:T(8,128)(2,1)}), bf16[4096,256]{1,0:T(8,128)(2,1)}) %reduce-scatter.23.cloned.1.call-update) | async-done | bytes 2097168 | tf_op jit(solution)/shard_map/reduce_scatter | solution.py:236
  657.9 23.1 all-reduce
  691.0 62.1 %all_gather.41 = bf16[2,16,5632]{1,0,2:T(2,128)(2,1)S(1)} all-gather(bf16[2,16,176]{1,0,2:T(2,128)(2,1)S(1)} %copy.173), channel_id=1, replica_groups=mesh['dp'=4,'mp'=8] {'dp','mp'}, dimensions={2}, use_global_device_ids=true | all-gather | bytes 371712 | tf_op jit(solution)/shard_map/all_gather | solution.py:343
  753.5 40.7 %all-gather.1 = bf16[32,176,2]{1,2,0:T(2,128)(2,1)S(1)} all-gather(bf16[1,176,2]{1,2,0:T(2,128)(2,1)S(1)} %convert_bitcast_fusion.3), channel_id=1, replica_groups=mesh['dp'=4,'mp'=8] {'dp','mp'}, dimensions={0}, use_global_device_ids=true | all-gather | bytes 23232 | tf_op jit(solution)/shard_map/all_gather | solution.py:345
  802.4 11.2 fusion.226
  823.8 70.6 %all-gather.14.cloned.1.call-done = bf16[4096,2048]{1,0:T(8,128)(2,1)} async-done(((bf16[4096,256]{1,0:T(8,128)(2,1)}), bf16[4096,2048]{1,0:T(8,128)(2,1)}) %all-gather.14.cloned.1.call-update) | async-done | bytes 16777232 | tf_op jit(solution)/shard_map/all_gather | solution.py:273
  894.4 20.5 fusion.227
  919.3 38.2 %broadcast_multiply_fusion = (f32[2,4096,704]{1,2,0:T(8,128)}, f32[2,4096,704]{1,2,0:T(8,128)}) fusion(f32[2,704]{1,0:T(2,128)S(1)} %bitcast_divide_fusion, f32[2,4096,704]{1,2,0:T(8,128)} %fusion.168, bf16[2,2048,704]{1,2,0:T(8,128)(2,1)} %param.23, bf16[4096,2048]{1,0:T(8,128)(2,1)} %all-gather.12.cloned.1.call-done), kind=kOutput, calls=%fused_computation.74 | convolution fusion | flops 23639621632 | bytes 91756032 | tf_op jit(solution)/shard_map/td,kdc->ktc/dot_general | solution.py:177
  957.5 18.4 multiply_bitcast_fusion.1
  975.9 12.2 multiply_reduce_fusion.1
  994.7 32.7 %bitcast_convert_fusion.1 = bf16[4096,2048]{1,0:T(8,128)(2,1)} fusion(bf16[2,4096,704]{1,2,0:T(8,128)(2,1)} %copy-done.6, bf16[2,2048,704]{1,2,0:T(8,128)(2,1)} %param.23), kind=kOutput, calls=%fused_computation.52 | convolution fusion | flops 23630708736 | bytes 34078720 | tf_op jit(solution)/shard_map/ktc,kdc->td/dot_general | solution.py:207
  1028.1 20.2 all-reduce.9.cloned.1.call-done
  1048.4 119.0 %reduce-scatter.27.cloned.1.call-done = bf16[4096,256]{1,0:T(8,128)(2,1)} async-done(((bf16[4096,2048]{1,0:T(8,128)(2,1)}), bf16[4096,256]{1,0:T(8,128)(2,1)}) %reduce-scatter.27.cloned.1.call-update) | async-done | bytes 2097168 | tf_op jit(solution)/shard_map/reduce_scatter | solution.py:44
  1173.3 23.0 psum.77
  1222.2 18.7 convolution_convert_fusion
  1252.0 46.6 %all-gather.16.cloned.1.call-done = bf16[4096,2048]{1,0:T(8,128)(2,1)} async-done(((bf16[4096,256]{1,0:T(8,128)(2,1)}), bf16[4096,2048]{1,0:T(8,128)(2,1)}) %all-gather.16.cloned.1.call-update) | async-done | bytes 16777232 | tf_op jit(solution)/shard_map/all_gather | solution.py:273
  1320.9 278.7 %while.33 = (s32[]{:T(128)}, f32[2,2048,2,128]{1,3,2,0:T(8,128)}, f32[2,2048,2,128]{1,3,2,0:T(8,128)}, f32[4,2,512,2,128]{4,2,3,1,0:T(8,128)}, s32[4]{0:T(128)S(...) while((s32[]{:T(128)}, f32[2,2048,2,128]{1,3,2,0:T(8,128)}, ...), condition=%wide.region_26.27_spmd.clone.clone.clone, body=%wide.region_24.26_spmd.clone.clone.sunk.clone | while | flops 5447617024 | bytes 224510800 | solution.py:168
  1340.5 12.6 multiply_reduce_fusion.12
  1353.1 16.3 multiply_convert_fusion.8
  1410.0 12.7 multiply_reduce_fusion.12
  1422.7 14.8 multiply_convert_fusion.8
  1449.6 11.0 bitcast_add_fusion.11
  1479.4 12.6 multiply_reduce_fusion.12
  1492.0 14.8 multiply_convert_fusion.8
  1518.9 11.0 bitcast_add_fusion.11
  1548.7 12.6 multiply_reduce_fusion.12
  1561.4 14.8 multiply_convert_fusion.8
  1588.2 11.0 bitcast_add_fusion.11
  1618.6 16.2 copy.184
  1665.8 16.1 copy.187
  1837.5 20.1 bitcast_convert_fusion
  1857.7 57.2 %reduce-scatter.41.cloned.1.call-done = f32[176,2]{1,0:T(8,128)} async-done(((f32[5632,2]{1,0:T(8,128)}), f32[176,2]{1,0:T(8,128)}) %reduce-scatter.41.cloned.1.call-update) | async-done | bytes 1424
  1916.4 134.9 %reduce-scatter.37.cloned.1.call-done = f32[176,32]{1,0:T(8,128)} async-done(((f32[5632,32]{1,0:T(8,128)}), f32[176,32]{1,0:T(8,128)}) %reduce-scatter.37.cloned.1.call-update) | async-done | bytes 22544
  2053.1 131.4 %reduce-scatter.39.cloned.1.call-done = f32[64,5]{1,0:T(8,128)} async-done(((f32[2048,5]{1,0:T(8,128)}), f32[64,5]{1,0:T(8,128)}) %reduce-scatter.39.cloned.1.call-update) | async-done | bytes 1296
  2185.9 134.8 %reduce-scatter.33.cloned.1.call-done = f32[176,16]{1,0:T(8,128)} async-done(((f32[5632,16]{1,0:T(8,128)}), f32[176,16]{1,0:T(8,128)}) %reduce-scatter.33.cloned.1.call-update) | async-done | bytes 11280
  2322.3 131.2 %reduce-scatter.35.cloned.1.call-done = f32[64,80]{1,0:T(8,128)} async-done(((f32[2048,80]{1,0:T(8,128)}), f32[64,80]{1,0:T(8,128)}) %reduce-scatter.35.cloned.1.call-update) | async-done | bytes 20496
  2455.1 131.9 %reduce-scatter.31.cloned.1.call-done = f32[64,96]{1,0:T(8,128)} async-done(((f32[2048,96]{1,0:T(8,128)}), f32[64,96]{1,0:T(8,128)}) %reduce-scatter.31.cloned.1.call-update) | async-done | bytes 24592
  2588.7 113.7 %reduce-scatter.29.cloned.1.call-done = bf16[4096,256]{1,0:T(8,128)(2,1)} async-done(((bf16[4096,2048]{1,0:T(8,128)(2,1)}), bf16[4096,256]{1,0:T(8,128)(2,1)}) %reduce-scatter.29.cloned.1.call-update) | async-done | bytes 2097168 | tf_op jit(solution)/shard_map/reduce_scatter | solution.py:44
  2707.2 23.1 psum.79
  (586 shorter events, 697.8 us)
Async XLA Ops:
  7.2 62.6 %copy-start.95 = (f32[5,16,64]{2,1,0:T(8,128)S(1)}, f32[5,16,64]{2,1,0:T(8,128)}, u32[]{:S(2)}) copy-start(f32[5,16,64]{2,1,0:T(8,128)} %param.27) | copy-start | bytes 61444
  7.2 253.6 %all-gather.10.cloned.1.call-start = ((), (), s32[]{:S(2)}) async-start(), calls=%async_computation.10 | async-start | bytes 18874368 | tf_op jit(solution)/shard_map/all_gather | solution.py:40
  69.7 68.4 %copy-start.81 = (bf16[1,256,16]{1,2,0:T(8,128)(2,1)}, bf16[1,256,16]{1,2,0:T(8,128)(2,1)S(1)}, u32[]{:S(2)}) copy-start(bf16[1,256,16]{1,2,0:T(8,128)(2,1)S(1)} %copy.217) | copy-start | bytes 24580
  69.9 67.6 %copy-start.9 = (bf16[4096,256]{1,0:T(8,128)(2,1)S(1)}, bf16[4096,256]{1,0:T(8,128)(2,1)}, u32[]{:S(2)}) copy-start(bf16[4096,256]{1,0:T(8,128)(2,1)} %param.19) | copy-start | bytes 6291460
  137.4 29.5 %copy-start.63 = (bf16[1,16,2048]{2,1,0:T(8,128)(2,1)}, bf16[1,16,2048]{2,1,0:T(8,128)(2,1)S(1)}, u32[]{:S(2)}) copy-start(bf16[1,16,2048]{2,1,0:T(8,128)(2,1)S(1)} %copy.218) | copy-start | bytes 196612
  166.9 373.4 %all-reduce.7.cloned.1.call-start = ((), (), s32[]{:S(2)}) async-start(), calls=%async_computation.12 | async-start | bytes 262144 | tf_op jit(solution)/shard_map/psum | solution.py:36
  173.1 87.6 %copy-start.47 = (bf16[3,2048,16]{1,2,0:T(8,128)(2,1)}, bf16[3,2048,16]{1,2,0:T(8,128)(2,1)S(1)}, u32[]{:S(2)}) copy-start(bf16[3,2048,16]{1,2,0:T(8,128)(2,1)S(1)} %copy.213) | copy-start | bytes 589828
  173.2 42.6 %copy-start.45 = (s32[2,2048]{1,0:T(2,128)S(1)}, s32[2,2048]{1,0:T(2,128)}, u32[]{:S(2)}) copy-start(s32[2,2048]{1,0:T(2,128)} %param.31) | copy-start | bytes 49156
  174.5 97.2 %copy-start.68 = (bf16[3,16,256]{2,1,0:T(8,128)(2,1)}, bf16[3,16,256]{2,1,0:T(8,128)(2,1)S(1)}, u32[]{:S(2)}) copy-start(bf16[3,16,256]{2,1,0:T(8,128)(2,1)S(1)} %copy.215) | copy-start | bytes 73732
  222.5 56.6 %copy-start.102 = (f32[3,256]{1,0:T(4,128)}, f32[3,256]{1,0:T(4,128)S(1)}, u32[]{:S(2)}) copy-start(f32[3,256]{1,0:T(4,128)S(1)} %fusion.212) | copy-start | bytes 9220
  479.2 172.4 %reduce-scatter.23.cloned.1.call-start = ((), (), s32[]{:S(2)}) async-start(), calls=%async_computation.11 | async-start | bytes 18874368 | tf_op jit(solution)/shard_map/reduce_scatter | solution.py:236
  489.7 312.7 %all-gather.12.cloned.1.call-start = ((), (), s32[]{:S(2)}) async-start(), calls=%async_computation.13 | async-start | bytes 18874368 | tf_op jit(solution)/shard_map/all_gather | solution.py:40
  490.3 43.7 %copy-start.108 = (f32[2048]{0:T(1024)}, f32[2048]{0:T(1024)S(1)}, u32[]{:S(2)}) copy-start(f32[2048]{0:T(1024)S(1)} %sqrt.13) | copy-start | bytes 24580
  491.4 423.5 %copy-start.61 = (bf16[1,16,2048]{2,1,0:T(8,128)(2,1)}, bf16[1,16,2048]{2,1,0:T(8,128)(2,1)S(1)}, u32[]{:S(2)}) copy-start(bf16[1,16,2048]{2,1,0:T(8,128)(2,1)S(1)} %copy.221) | copy-start | bytes 196612
  533.1 684.7 %copy-start.75 = (bf16[5632,16]{0,1:T(8,128)(2,1)}, bf16[5632,16]{0,1:T(8,128)(2,1)S(1)}, u32[]{:S(2)}) copy-start(bf16[5632,16]{0,1:T(8,128)(2,1)S(1)} %reshape.322) | copy-start | bytes 540676
  534.7 116.9 %copy-start.10 = (bf16[4096,256]{1,0:T(8,128)(2,1)S(1)}, bf16[4096,256]{1,0:T(8,128)(2,1)}, u32[]{:S(2)}) copy-start(bf16[4096,256]{1,0:T(8,128)(2,1)} %param.19) | copy-start | bytes 6291460
  540.3 140.7 %copy-start.105 = (f32[1,256]{1,0:T(1,128)S(1)}, f32[1,256]{1,0:T(1,128)}, u32[]{:S(2)}) copy-start(f32[1,256]{1,0:T(1,128)} %get-tuple-element.450) | copy-start | bytes 3076
  684.7 209.6 %all-gather.14.cloned.1.call-start = ((), (), s32[]{:S(2)}) async-start(), calls=%async_computation.15 | async-start | bytes 18874368 | tf_op jit(solution)/shard_map/all_gather | solution.py:273
  687.3 66.1 %copy-start.116 = (f32[2,176]{1,0:T(2,128)S(1)}, f32[2,176]{1,0:T(2,128)}, u32[]{:S(2)}) copy-start(f32[2,176]{1,0:T(2,128)} %param.30) | copy-start | bytes 4228
  687.3 361.0 %all-reduce.9.cloned.1.call-start = ((), (), s32[]{:S(2)}) async-start(), calls=%async_computation.17 | async-start | bytes 524288 | tf_op jit(solution)/shard_map/psum | solution.py:36
  690.9 111.6 %copy-start.52 = (bf16[2,2048,16]{1,2,0:T(8,128)(2,1)}, bf16[2,2048,16]{1,2,0:T(8,128)(2,1)S(1)}, u32[]{:S(2)}) copy-start(bf16[2,2048,16]{1,2,0:T(8,128)(2,1)S(1)} %copy.219) | copy-start | bytes 393220
  753.5 234.6 %copy-start.54 = (bf16[2,16,704]{2,1,0:T(8,128)(2,1)}, bf16[2,16,704]{2,1,0:T(8,128)(2,1)S(1)}, u32[]{:S(2)}) copy-start(bf16[2,16,704]{2,1,0:T(8,128)(2,1)S(1)} %copy.220) | copy-start | bytes 135172
  814.5 79.9 %copy-start.50 = (bf16[704,2048]{1,0:T(8,128)(2,1)S(1)}, bf16[704,2048]{1,0:T(8,128)(2,1)}, u32[]{:S(2)}) copy-start(bf16[704,2048]{1,0:T(8,128)(2,1)} %param.24) | copy-start | bytes 8650756
  919.3 38.2 %copy-start.70 = (bf16[4096,16]{0,1:T(8,128)(2,1)}, bf16[4096,16]{0,1:T(8,128)(2,1)S(1)}, u32[]{:S(2)}) copy-start(bf16[4096,16]{0,1:T(8,128)(2,1)S(1)} %fusion.61) | copy-start | bytes 393220
  994.7 172.7 %reduce-scatter.27.cloned.1.call-start = ((), (), s32[]{:S(2)}) async-start(), calls=%async_computation.16 | async-start | bytes 18874368 | tf_op jit(solution)/shard_map/reduce_scatter | solution.py:44
  1027.4 139.9 %copy-start.53 = (bf16[2,2048,16]{1,2,0:T(8,128)(2,1)S(1)}, bf16[2,2048,16]{1,2,0:T(8,128)(2,1)}, u32[]{:S(2)}) copy-start(bf16[2,2048,16]{1,2,0:T(8,128)(2,1)} %copy-done.52) | copy-start | bytes 393220
  1027.4 139.9 %copy-start.106 = (f32[1,256]{1,0:T(1,128)S(1)}, f32[1,256]{1,0:T(1,128)}, u32[]{:S(2)}) copy-start(f32[1,256]{1,0:T(1,128)} %get-tuple-element.450) | copy-start | bytes 3076
  1027.5 271.2 %all-gather.16.cloned.1.call-start = ((), (), s32[]{:S(2)}) async-start(), calls=%async_computation.18 | async-start | bytes 18874368 | tf_op jit(solution)/shard_map/all_gather | solution.py:273
  1028.1 168.2 %copy-start.89 = (f32[4096]{0:T(1024)S(1)}, f32[4096]{0:T(1024)}, u32[]{:S(2)}) copy-start(f32[4096]{0:T(1024)} %copy-done.88) | copy-start | bytes 49156
  1028.1 168.2 %copy-start.23 = (bf16[4096,256]{1,0:T(8,128)(2,1)S(1)}, bf16[4096,256]{1,0:T(8,128)(2,1)}, u32[]{:S(2)}) copy-start(bf16[4096,256]{1,0:T(8,128)(2,1)} %param.33) | copy-start | bytes 6291460
  1028.1 168.2 %copy-start.80 = (f32[4096]{0:T(1024)S(1)}, f32[4096]{0:T(1024)}, u32[]{:S(2)}) copy-start(f32[4096]{0:T(1024)} %copy-done.79) | copy-start | bytes 49156
  1205.4 568.9 %reduce-scatter.25.cloned.1.call-start = ((), (), s32[]{:S(2)}) async-start(), calls=%async_computation.14 | async-start | bytes 18874368 | tf_op jit(solution)/shard_map/reduce_scatter | solution.py:236
  1240.9 534.2 %all-reduce.11.cloned.1.call-start = ((), (), s32[]{:S(2)}) async-start(), calls=%async_computation.26 | async-start | bytes 1048576 | tf_op jit(solution)/shard_map/psum | solution.py:36
  1241.4 57.3 %copy-start.64 = (bf16[1,16,2048]{2,1,0:T(8,128)(2,1)S(1)}, bf16[1,16,2048]{2,1,0:T(8,128)(2,1)}, u32[]{:S(2)}) copy-start(bf16[1,16,2048]{2,1,0:T(8,128)(2,1)} %copy-done.63) | copy-start | bytes 196612
  1241.4 67.6 %copy-start.43 = (bf16[256,2048]{1,0:T(8,128)(2,1)S(1)}, bf16[256,2048]{1,0:T(8,128)(2,1)}, u32[]{:S(2)}) copy-start(bf16[256,2048]{1,0:T(8,128)(2,1)} %param.22) | copy-start | bytes 3145732
  1328.7 24.4 copy-start.3
  1720.4 194.5 %reduce-scatter.41.cloned.1.call-start = ((), (), s32[]{:S(2)}) async-start(), calls=%async_computation.25 | async-start | bytes 2973696
  1730.6 320.7 %reduce-scatter.37.cloned.1.call-start = ((), (), s32[]{:S(2)}) async-start(), calls=%async_computation.23 | async-start | bytes 2973696
  1747.8 436.7 %reduce-scatter.39.cloned.1.call-start = ((), (), s32[]{:S(2)}) async-start(), calls=%async_computation.24 | async-start | bytes 1081344
  1747.9 25.4 slice-start.2
  1791.1 529.6 %reduce-scatter.33.cloned.1.call-start = ((), (), s32[]{:S(2)}) async-start(), calls=%async_computation.21 | async-start | bytes 2973696
  1799.3 654.2 %reduce-scatter.35.cloned.1.call-start = ((), (), s32[]{:S(2)}) async-start(), calls=%async_computation.22 | async-start | bytes 1081344
  1815.7 771.4 %reduce-scatter.31.cloned.1.call-start = ((), (), s32[]{:S(2)}) async-start(), calls=%async_computation.20 | async-start | bytes 1081344
  1837.2 865.2 %reduce-scatter.29.cloned.1.call-start = ((), (), s32[]{:S(2)}) async-start(), calls=%async_computation.19 | async-start | bytes 18874368 | tf_op jit(solution)/shard_map/reduce_scatter | solution.py:44
  1857.6 844.8 %copy-start.11 = (bf16[4096,256]{1,0:T(8,128)(2,1)S(1)}, bf16[4096,256]{1,0:T(8,128)(2,1)}, u32[]{:S(2)}) copy-start(bf16[4096,256]{1,0:T(8,128)(2,1)} %param.19) | copy-start | bytes 6291460
  1857.6 844.8 %copy-start.101 = (f32[1,256]{1,0:T(1,128)S(1)}, f32[1,256]{1,0:T(1,128)}, u32[]{:S(2)}) copy-start(f32[1,256]{1,0:T(1,128)} %copy-done.100) | copy-start | bytes 3076
  2588.7 141.5 %copy-start.87 = (f32[4096]{0:T(1024)S(1)}, f32[4096]{0:T(1024)}, u32[]{:S(2)}) copy-start(f32[4096]{0:T(1024)} %copy-done.86) | copy-start | bytes 49156
  2588.7 141.5 %copy-start.78 = (f32[4096]{0:T(1024)S(1)}, f32[4096]{0:T(1024)}, u32[]{:S(2)}) copy-start(f32[4096]{0:T(1024)} %copy-done.77) | copy-start | bytes 49156
  (108 other events, 849.1 us)
Sparse Core Ops, SparseCore 0:
  167.0 93.6 all-gather.9
  479.4 52.9 all-reduce.6
  536.3 115.2 reduce-scatter.22
  684.8 115.5 all-gather.11
  802.3 92.0 all-gather.13
  994.8 53.5 all-reduce.8
  1051.9 115.3 reduce-scatter.26
  1205.5 93.0 all-gather.15
  1302.2 115.9 reduce-scatter.24
  1720.5 54.5 all-reduce.10
  1777.5 137.3 reduce-scatter.40
  1917.1 134.1 reduce-scatter.36
  2053.6 130.8 reduce-scatter.38
  2186.6 134.0 reduce-scatter.32
  2322.8 130.6 reduce-scatter.34
  2456.3 130.7 reduce-scatter.30
  2590.5 111.8 reduce-scatter.28
where the time goes:
time: 2750 us; the launch traced here: 2740 us
  waiting for transfers between devices  1230 us (45%)
  matrix products  586 us (21%)
  blocking collectives  411 us (15%)
  local copies, waits for them, and re-layouts  246 us (9%)
  other arithmetic  232 us (8%)
    unnamed x23, waiting for transfers between devices  722 us
    reduce_scatter x2, waiting for transfers between devices, scatter_inputs(): lax.psum_scatter(values.astype(jnp.bfloat16), 'mp', scatter_dimension=1,...  233 us
    all_gather x2, waiting for transfers between devices, row_backward(): lax.all_gather(grad_pre, 'mp', axis=1, tiled=True)  117 us
    reduce_scatter x2, waiting for transfers between devices, row_forward(): lax.psum_scatter(partial_value.astype(jnp.bfloat16), 'mp', scatter_dimens...  111 us
    psum x4, blocking collectives, token_sums(): return lax.psum(values, 'mp')  93 us
    unnamed x269, local copies, waits for them, and re-layouts  80.6 us
    dot_general x2, matrix products, column_forward(): jnp.einsum('td,kdc->ktc', normed_input, weights, preferred_element_type=j...  63.7 us
    dot_general x8, matrix products, one_block(): jnp.einsum('rqhe,rkhe->rhqk', query_block, keys, preferred_element_type=j...  62.1 us
  transfers between devices with their start and end apart: 17, of which 14 were waited for; matrix products, arithmetic and copies ran while one was open for 25% of the time, Pallas kernels for 0%

commit v1 on v0

v1 whole, which is shorter than its diff:
```python
import functools

import jax
import jax.numpy as jnp
from jax import lax
from jax.experimental import pallas as pl
from jax.experimental.pallas import tpu as pltpu
from jax.sharding import PartitionSpec as P

D = 2048
HEAD = 128
FF = 5632
RANK = 16
SEGMENTS = 8
EPSILON = 1e-05
ROPE_BASE = 10000.0
MASKED = -1e30
ROW = 2
CHUNKS = 2
BQ = 256
BK = 256
F32 = jnp.float32
BF16 = jnp.bfloat16

NN = (((1,), (0,)), ((), ()))
NT = (((1,), (1,)), ((), ()))
TN = (((0,), (0,)), ((), ()))


def dot(a, b, dims=NN):
    return lax.dot_general(a, b, dims, preferred_element_type=F32)


def params(rank):
    return pltpu.CompilerParams(
        dimension_semantics=("arbitrary",) * rank, vmem_limit_bytes=56 * 2**20
    )


def cost(flops, moved, exps=0):
    return pl.CostEstimate(flops=int(flops), bytes_accessed=int(moved), transcendentals=int(exps))


def bytes_of(arrays):
    return sum(a.size * a.dtype.itemsize for a in arrays)


def fixed(shape):
    rank = len(shape)
    return pl.BlockSpec(shape, lambda *_: (0,) * rank, pipeline_mode=pl.Buffered(1))


def tiles(width, step=512):
    return [(at, min(step, width - at)) for at in range(0, width, step)]


def merge_columns(perm, own, other, adapter_a, adapter_b, gain, first):
    count, rows, width = own.shape
    blocks = perm.shape[0]
    size = rows // blocks
    local = adapter_b.shape[2]

    def body(perm_ref, own_ref, other_ref, a_ref, b_ref, gain_ref, v_ref, sq_ref):
        @pl.when(pl.program_id(0) == 0)
        def _():
            sq_ref[...] = jnp.zeros_like(sq_ref)

        for k in range(count):
            low = (first + k) * RANK
            product = dot(a_ref[:, low : low + RANK], b_ref[k])
            weight = jnp.concatenate([own_ref[k].astype(F32), other_ref[k].astype(F32)], axis=1)
            merged = weight + 2.0 * product
            sq_ref[k] += jnp.sum(merged * merged, axis=0, keepdims=True)
            v_ref[k] = (merged * gain_ref[...]).astype(BF16)

    return pl.pallas_call(
        body,
        out_shape=(
            jax.ShapeDtypeStruct((count, rows, local), BF16),
            jax.ShapeDtypeStruct((count, 1, local), F32),
        ),
        grid_spec=pltpu.PrefetchScalarGridSpec(
            num_scalar_prefetch=1,
            grid=(blocks,),
            in_specs=[
                pl.BlockSpec((count, size, width), lambda i, p: (0, p[i], 0)),
                pl.BlockSpec((count, size, width), lambda i, p: (0, p[i], 0)),
                pl.BlockSpec((size, adapter_a.shape[1]), lambda i, p: (i, 0)),
                fixed(adapter_b.shape),
                pl.BlockSpec((size, 1), lambda i, p: (i, 0)),
            ],
            out_specs=[
                pl.BlockSpec((count, size, local), lambda i, p: (0, i, 0)),
                pl.BlockSpec((count, 1, local), lambda i, p: (0, 0, 0)),
            ],
        ),
        compiler_params=params(1),
        cost_estimate=cost(4 * own.size * 64, 4 * bytes_of([own])),
        name="merge_columns",
    )(perm, own, other, adapter_a, adapter_b, gain)


def merge_rows(perm, own, other, adapter_a, adapter_b):
    height, columns = own.shape
    blocks = perm.shape[0]
    size = columns // blocks

    def body(perm_ref, own_ref, other_ref, a_ref, b_ref, v_ref, sq_ref):
        weight = jnp.concatenate([own_ref[...].astype(F32), other_ref[...].astype(F32)], axis=0)
        merged = weight + 2.0 * dot(a_ref[...], b_ref[...])
        sq_ref[...] = jnp.sum(merged * merged, axis=0, keepdims=True)
        v_ref[...] = merged.astype(BF16)

    return pl.pallas_call(
        body,
        out_shape=(
            jax.ShapeDtypeStruct((2 * height, columns), BF16),
            jax.ShapeDtypeStruct((1, columns), F32),
        ),
        grid_spec=pltpu.PrefetchScalarGridSpec(
            num_scalar_prefetch=1,
            grid=(blocks,),
            in_specs=[
                pl.BlockSpec((height, size), lambda i, p: (0, p[i])),
                pl.BlockSpec((height, size), lambda i, p: (0, p[i])),
                fixed(adapter_a.shape),
                pl.BlockSpec((RANK, size), lambda i, p: (0, i)),
            ],
            out_specs=[
                pl.BlockSpec((2 * height, size), lambda i, p: (0, i)),
                pl.BlockSpec((1, size), lambda i, p: (0, i)),
            ],
        ),
        compiler_params=params(1),
        cost_estimate=cost(4 * own.size * 64, 4 * bytes_of([own])),
        name="merge_rows",
    )(perm, own, other, adapter_a, adapter_b)


def inverse_rms(x):
    wide = x.astype(F32)
    return lax.rsqrt(jnp.sum(wide * wide, axis=1, keepdims=True) / D + EPSILON)


def project_qkv(parts, weights, low, scale, cosine, sine):
    rows, width = parts[0].shape
    local = weights.shape[2]
    bm = 256

    def body(*refs):
        part_refs = refs[: len(parts)]
        v_ref, a_ref, s_ref, cos_ref, sin_ref, out_ref, u_ref, r_ref = refs[len(parts) :]
        x = jnp.concatenate([ref[...] for ref in part_refs], axis=1)
        r = inverse_rms(x)
        r_ref[...] = jnp.broadcast_to(r, r_ref.shape)
        u_ref[...] = (dot(x, a_ref[...]) * r).astype(BF16)
        cos, sin = cos_ref[...], sin_ref[...]
        for k in range(3):
            y = dot(x, v_ref[k]) * r * s_ref[k]
            for at in range(0, local, HEAD):
                head = y[:, at : at + HEAD]
                if k < 2:
                    head = head * cos + pltpu.roll(head, HEAD // 2, 1) * sin
                out_ref[:, k * local + at : k * local + at + HEAD] = head.astype(BF16)

    outs = (
        jax.ShapeDtypeStruct((rows, 3 * local), BF16),
        jax.ShapeDtypeStruct((rows, 128), BF16),
        jax.ShapeDtypeStruct((rows, 128), F32),
    )
    return pl.pallas_call(
        body,
        out_shape=outs,
        grid=(rows // bm,),
        in_specs=[pl.BlockSpec((bm, width), lambda i: (i, 0))] * len(parts)
        + [
            fixed(weights.shape),
            fixed(low.shape),
            fixed(scale.shape),
            pl.BlockSpec((bm, HEAD), lambda i: (i, 0)),
            pl.BlockSpec((bm, HEAD), lambda i: (i, 0)),
        ],
        out_specs=[
            pl.BlockSpec((bm, 3 * local), lambda i: (i, 0)),
            pl.BlockSpec((bm, 128), lambda i: (i, 0)),
            pl.BlockSpec((bm, 128), lambda i: (i, 0)),
        ],
        compiler_params=params(1),
        cost_estimate=cost(6 * rows * D * local, bytes_of([*parts, weights, *outs])),
        name="project_qkv",
    )(*parts, weights, low, scale, cosine, sine)


def project_hidden(parts, weights, low, scale, down_low):
    rows, width = parts[0].shape
    local = weights.shape[2]
    bm = 256

    def body(*refs):
        part_refs = refs[: len(parts)]
        v_ref, a_ref, s_ref, d_ref, gate_ref, up_ref, hid_ref, u_ref, ud_ref, r_ref = refs[
            len(parts) :
        ]
        x = jnp.concatenate([ref[...] for ref in part_refs], axis=1)
        r = inverse_rms(x)
        r_ref[...] = jnp.broadcast_to(r, r_ref.shape)
        u_ref[...] = (dot(x, a_ref[...]) * r).astype(BF16)
        for at, size in tiles(local):
            cut = slice(at, at + size)
            gate = dot(x, v_ref[0, :, cut]) * r * s_ref[0, :, cut]
            up = dot(x, v_ref[1, :, cut]) * r * s_ref[1, :, cut]
            gate_ref[:, cut] = gate.astype(BF16)
            up_ref[:, cut] = up.astype(BF16)
            hid_ref[:, cut] = (gate * jax.nn.sigmoid(gate) * up).astype(BF16)
        ud_ref[...] = dot(hid_ref[...], d_ref[...]).astype(BF16)

    wide = jax.ShapeDtypeStruct((rows, local), BF16)
    outs = (
        wide,
        wide,
        wide,
        jax.ShapeDtypeStruct((rows, 128), BF16),
        jax.ShapeDtypeStruct((rows, 128), BF16),
        jax.ShapeDtypeStruct((rows, 128), F32),
    )
    return pl.pallas_call(
        body,
        out_shape=outs,
        grid=(rows // bm,),
        in_specs=[pl.BlockSpec((bm, width), lambda i: (i, 0))] * len(parts)
        + [fixed(weights.shape), fixed(low.shape), fixed(scale.shape), fixed(down_low.shape)],
        out_specs=[pl.BlockSpec((bm, local), lambda i: (i, 0))] * 3
        + [pl.BlockSpec((bm, 128), lambda i: (i, 0))] * 3,
        compiler_params=params(1),
        cost_estimate=cost(4 * rows * D * local, bytes_of([*parts, weights, *outs]), rows * local),
        name="project_hidden",
    )(*parts, weights, low, scale, down_low)


def hidden_backward(parts, down, down_scale, down_low, gate, up, scale):
    rows, width = parts[0].shape
    local = down.shape[0]
    bm = 256

    def body(*refs):
        part_refs = refs[: len(parts)]
        v_ref, ds_ref, b_ref, gate_ref, up_ref, s_ref, gg_ref, gu_ref, t_ref, in_ref, low_ref = refs[
            len(parts) :
        ]

        @pl.when(pl.program_id(0) == 0)
        def _():
            t_ref[...] = jnp.zeros_like(t_ref)

        raw = jnp.concatenate([ref[...] for ref in part_refs], axis=1).astype(F32)
        g = (raw * ds_ref[...]).astype(BF16)
        low_ref[...] = dot(g, b_ref[...], NT).astype(BF16)
        inner = jnp.zeros((bm, 1), F32)
        for at, size in tiles(local):
            cut = slice(at, at + size)
            back = dot(g, v_ref[cut, :], NT)
            y_gate = gate_ref[:, cut].astype(F32)
            y_up = up_ref[:, cut].astype(F32)
            sig = jax.nn.sigmoid(y_gate)
            act = y_gate * sig
            g_gate = back * y_up * (sig + act * (1.0 - sig))
            g_up = back * act
            dot_gate = g_gate * y_gate
            dot_up = g_up * y_up
            t_ref[0, :, cut] += jnp.sum(dot_gate, axis=0, keepdims=True)
            t_ref[1, :, cut] += jnp.sum(dot_up, axis=0, keepdims=True)
            inner += jnp.sum(dot_gate + dot_up, axis=1, keepdims=True)
            gg_ref[:, cut] = (g_gate * s_ref[0, :, cut]).astype(BF16)
            gu_ref[:, cut] = (g_up * s_ref[1, :, cut]).astype(BF16)
        in_ref[...] = jnp.broadcast_to(inner, in_ref.shape)

    wide = jax.ShapeDtypeStruct((rows, local), BF16)
    outs = (
        wide,
        wide,
        jax.ShapeDtypeStruct((2, 1, local), F32),
        jax.ShapeDtypeStruct((rows, 128), F32),
        jax.ShapeDtypeStruct((rows, 128), BF16),
    )
    return pl.pallas_call(
        body,
        out_shape=outs,
        grid=(rows // bm,),
        in_specs=[pl.BlockSpec((bm, width), lambda i: (i, 0))] * len(parts)
        + [fixed(down.shape), fixed(down_scale.shape), fixed(down_low.shape)]
        + [pl.BlockSpec((bm, local), lambda i: (i, 0))] * 2
        + [fixed(scale.shape)],
        out_specs=[pl.BlockSpec((bm, local), lambda i: (i, 0))] * 2
        + [
            pl.BlockSpec((2, 1, local), lambda i: (0, 0, 0)),
            pl.BlockSpec((bm, 128), lambda i: (i, 0)),
            pl.BlockSpec((bm, 128), lambda i: (i, 0)),
        ],
        compiler_params=params(1),
        cost_estimate=cost(
            2 * rows * D * local, bytes_of([*parts, down, gate, up, *outs]), rows * local
        ),
        name="hidden_backward",
    )(*parts, down, down_scale, down_low, gate, up, scale)


def matmul(lefts, rights, dims, at, step, count, width, add=None, add_at=0, kind=BF16):
    rows = lefts[0].shape[0]
    bm = min(512, rows)
    rank = len(lefts)

    def body(*refs):
        total = None
        for left, right in zip(refs[:rank], refs[rank : 2 * rank]):
            value = dot(left[...], right[...], dims)
            total = value if total is None else total + value
        if add is not None:
            total = total + refs[2 * rank][...].astype(F32)
        refs[-1][...] = total.astype(kind)

    specs = [pl.BlockSpec((bm, a.shape[1]), lambda p, m: (m, 0)) for a in lefts]
    arrays = []
    depth = 0
    for array, index in rights:
        if dims is NT:
            size = array.shape[-1]
            if index is None:
                specs.append(pl.BlockSpec((width, size), lambda p, m: (at + step * p, 0)))
            else:
                specs.append(
                    pl.BlockSpec(
                        (None, width, size), lambda p, m, k=index: (k, at + step * p, 0)
                    )
                )
        else:
            size = array.shape[-2]
            specs.append(pl.BlockSpec((size, width), lambda p, m: (0, at + step * p)))
        arrays.append(array)
        depth += size
    if add is not None:
        specs.append(pl.BlockSpec((None, bm, width), lambda p, m: (add_at + p, m, 0)))
        arrays.append(add)
    out = jax.ShapeDtypeStruct((count, rows, width), kind)
    return pl.pallas_call(
        body,
        out_shape=out,
        grid=(count, rows // bm),
        in_specs=specs,
        out_specs=pl.BlockSpec((None, bm, width), lambda p, m: (p, m, 0)),
        compiler_params=params(2),
        cost_estimate=cost(
            2 * count * rows * width * depth,
            count * (bytes_of(lefts) + 2 * width * depth) + bytes_of([out]),
        ),
        name="matmul_add",
    )(*lefts, *arrays)


def visible(start, query, key, last):
    return (key >= start) & ((key <= jnp.minimum(query, last)) | (key == query))


def attention_forward(table, qkv_q, keys, values, starts, offset):
    rows = qkv_q.shape[0]
    length, local = keys.shape
    heads = local // HEAD
    factor = HEAD**-0.5

    def body(table_ref, q_ref, k_ref, v_ref, start_ref, out_ref, lse_ref):
        i = pl.program_id(1)
        base = offset + i * BQ
        q = q_ref[...]
        start = start_ref[...]
        query = base + lax.broadcasted_iota(jnp.int32, (1, BQ), 1)
        last = table_ref[0] - 1

        def step(j, carry):
            top, total, acc = carry
            at = pl.multiple_of(j * BK, BK)
            scores = dot(k_ref[pl.ds(at, BK), :], q, NT) * factor
            key = at + lax.broadcasted_iota(jnp.int32, (BK, BQ), 0)
            scores = jnp.where(visible(start, query, key, last), scores, MASKED)
            higher = jnp.maximum(top, jnp.max(scores, axis=0, keepdims=True))
            fade = jnp.exp(top - higher)
            weights = jnp.exp(scores - higher)
            total = total * fade + jnp.sum(weights, axis=0, keepdims=True)
            acc = acc * fade + dot(v_ref[pl.ds(at, BK), :], weights.astype(BF16), TN)
            return higher, total, acc

        empty = (
            jnp.full((1, BQ), MASKED, F32),
            jnp.zeros((1, BQ), F32),
            jnp.zeros((HEAD, BQ), F32),
        )
        block = offset // BQ + i
        top, total, acc = lax.fori_loop(table_ref[1 + block], block + 1, step, empty)
        out_ref[...] = jnp.transpose(acc / total).astype(BF16)
        lse_ref[...] = top + jnp.log(total)

    outs = (
        jax.ShapeDtypeStruct((rows, local), BF16),
        jax.ShapeDtypeStruct((heads, 1, rows), F32),
    )
    first = offset // BQ
    return pl.pallas_call(
        body,
        out_shape=outs,
        grid_spec=pltpu.PrefetchScalarGridSpec(
            num_scalar_prefetch=1,
            grid=(heads, rows // BQ),
            in_specs=[
                pl.BlockSpec((BQ, HEAD), lambda h, i, t: (i, h)),
                pl.BlockSpec((length, HEAD), lambda h, i, t: (0, h)),
                pl.BlockSpec((length, HEAD), lambda h, i, t: (0, h)),
                pl.BlockSpec((1, BQ), lambda h, i, t: (0, first + i)),
            ],
            out_specs=[
                pl.BlockSpec((BQ, HEAD), lambda h, i, t: (i, h)),
                pl.BlockSpec((None, 1, BQ), lambda h, i, t: (h, 0, i)),
            ],
        ),
        compiler_params=params(2),
        cost_estimate=cost(
            2 * rows * length * local, bytes_of([keys, values, *outs]), rows * length * heads // 2
        ),
        name="attention_forward",
    )(table, qkv_q, keys, values, starts)


def attention_backward(table, qkv, grad, attended, lse, starts, cosine, sine, scale):
    length = qkv.shape[0]
    local = grad.shape[1]
    heads = local // HEAD
    factor = HEAD**-0.5
    blocks = length // BQ

    def body(table_ref, q_ref, k_ref, v_ref, g_ref, att_ref, lse_ref, start_ref, cos_ref, sin_ref, s_ref, gq_ref, gk_ref, gv_ref, t_ref, in_ref, dk_ref, dv_ref):
        last = table_ref[0] - 1
        dk_ref[...] = jnp.zeros_like(dk_ref)
        dv_ref[...] = jnp.zeros_like(dv_ref)
        t_ref[...] = jnp.zeros_like(t_ref)

        @pl.when(pl.program_id(0) == 0)
        def _():
            in_ref[...] = jnp.zeros_like(in_ref)

        def back(values, here):
            return values * cos_ref[here, :] - pltpu.roll(values, HEAD // 2, 1) * sin_ref[here, :]

        def per_query(i, nothing):
            here = pl.ds(pl.multiple_of(i * BQ, BQ), BQ)
            q, g = q_ref[here, :], g_ref[here, :]
            start = start_ref[:, here]
            total = lse_ref[:, here]
            pairs = g.astype(F32) * att_ref[here, :].astype(F32)
            delta = jnp.sum(jnp.transpose(pairs), axis=0, keepdims=True)
            query = i * BQ + lax.broadcasted_iota(jnp.int32, (1, BQ), 1)

            def step(j, dq):
                at = pl.multiple_of(j * BK, BK)
                there = pl.ds(at, BK)
                k, v = k_ref[there, :], v_ref[there, :]
                scores = dot(k, q, NT) * factor
                key = at + lax.broadcasted_iota(jnp.int32, (BK, BQ), 0)
                seen = visible(start, query, key, last)
                weights = jnp.exp(jnp.where(seen, scores - total, MASKED))
                slopes = (weights * (dot(v, g, NT) - delta)).astype(BF16)
                dv_ref[there, :] += dot(weights.astype(BF16), g)
                dk_ref[there, :] += dot(slopes, q)
                return dq + dot(slopes, k, TN)

            dq = lax.fori_loop(table_ref[1 + i], i + 1, step, jnp.zeros((BQ, HEAD), F32))
            gy = back(dq * factor, here)
            both = gy * back(q.astype(F32), here)
            t_ref[0] += jnp.sum(both, axis=0, keepdims=True)
            in_ref[here, :] += both
            gq_ref[here, :] = (gy * s_ref[0]).astype(BF16)
            return nothing

        lax.fori_loop(0, blocks, per_query, 0)

        def per_key(i, nothing):
            here = pl.ds(pl.multiple_of(i * BQ, BQ), BQ)
            gy = back(dk_ref[here, :] * factor, here)
            both = gy * back(k_ref[here, :].astype(F32), here)
            t_ref[1] += jnp.sum(both, axis=0, keepdims=True)
            gk_ref[here, :] = (gy * s_ref[1]).astype(BF16)
            gv = dv_ref[here, :]
            more = gv * v_ref[here, :].astype(F32)
            t_ref[2] += jnp.sum(more, axis=0, keepdims=True)
            gv_ref[here, :] = (gv * s_ref[2]).astype(BF16)
            in_ref[here, :] += both + more
            return nothing

        lax.fori_loop(0, blocks, per_key, 0)

    column = jax.ShapeDtypeStruct((length, local), BF16)
    outs = (
        column,
        column,
        column,
        jax.ShapeDtypeStruct((3, 1, local), F32),
        jax.ShapeDtypeStruct((length, HEAD), F32),
    )
    per_head = pl.BlockSpec((length, HEAD), lambda h, t: (0, h))
    return pl.pallas_call(
        body,
        out_shape=outs,
        grid_spec=pltpu.PrefetchScalarGridSpec(
            num_scalar_prefetch=1,
            grid=(heads,),
            in_specs=[
                per_head,
                pl.BlockSpec((length, HEAD), lambda h, t: (0, heads + h)),
                pl.BlockSpec((length, HEAD), lambda h, t: (0, 2 * heads + h)),
                per_head,
                per_head,
                pl.BlockSpec((None, 1, length), lambda h, t: (h, 0, 0)),
                fixed(starts.shape),
                fixed(cosine.shape),
                fixed(sine.shape),
                pl.BlockSpec((3, 1, HEAD), lambda h, t: (0, 0, h)),
            ],
            out_specs=[
                per_head,
                per_head,
                per_head,
                pl.BlockSpec((3, 1, HEAD), lambda h, t: (0, 0, h)),
                pl.BlockSpec((length, HEAD), lambda h, t: (0, 0)),
            ],
            scratch_shapes=[pltpu.VMEM((length, HEAD), F32), pltpu.VMEM((length, HEAD), F32)],
        ),
        compiler_params=params(1),
        cost_estimate=cost(
            5 * length * length * local, bytes_of([qkv, grad, *outs]), length * length * heads // 2
        ),
        name="attention_backward",
    )(table, qkv, qkv, qkv, grad, attended, lse, starts, cosine, sine, scale)


def layer(
    n_dp,
    n_mp,
    tokens,
    norm_gains,
    query_key_value_weight,
    output_weight,
    gate_up_weight,
    down_weight,
    a_in,
    a_down,
    b_dmodel,
    b_hidden,
    m_dmodel,
    m_hidden,
    segment_ids,
    valid_mask,
    cotangent,
):
    length = segment_ids.shape[1]
    block = D // n_mp
    width = 2 * block
    hidden = FF // n_mp
    n_hi = n_mp // 4
    positions = 2 * n_hi
    chunk = length // CHUNKS
    me = lax.axis_index("mp")
    row = (me // ROW) % 2
    high_masks = [4 << k for k in range(n_hi.bit_length() - 1)]
    masks = [
        ((pos >> 1) << 2) | (side << 1) | (pos & 1) for pos in range(positions) for side in range(2)
    ]
    place_of = [masks.index(k) for k in range(n_mp)]
    perm = me ^ jnp.array(masks, jnp.int32)

    def swapped(blocks):
        for k in range(n_mp.bit_length() - 1):
            bit = (me >> k) % 2 == 1
            blocks = [jnp.where(bit, blocks[i ^ (1 << k)], b) for i, b in enumerate(blocks)]
        return blocks

    def to_relative(values):
        blocks = swapped([values[:, i * block : (i + 1) * block] for i in range(n_mp)])
        return jnp.concatenate([blocks[k] for k in masks], axis=1)

    def flip(values, mask):
        return lax.ppermute(values, "mp", [(i, i ^ mask) for i in range(n_mp)])

    def gather(values):
        far = [values]
        for mask in high_masks:
            far = far + [flip(v, mask) for v in far]
        return [v for f in far for v in (f, flip(f, 1))]

    def total(values):
        for mask in [1, *high_masks]:
            values = values + flip(values, mask)
        return values

    def total_relative(values):
        lead = values.shape[:-1]
        for mask in [1, *high_masks]:
            bit = 1 if mask == 1 else mask >> 1
            cut = (*lead, positions // (2 * bit), 2, bit * width)
            theirs = flip(values, mask).reshape(cut)
            theirs = jnp.concatenate([theirs[..., 1:2, :], theirs[..., 0:1, :]], axis=-2)
            values = (values.reshape(cut) + theirs).reshape(values.shape)
        return values

    def reduce_far(near, far):
        blocks = [near, *far]
        for mask in reversed(high_masks):
            half = len(blocks) // 2
            sent = [flip(b.astype(BF16), mask) for b in blocks[half:]]
            blocks = [a.astype(F32) + b.astype(F32) for a, b in zip(blocks[:half], sent)]
        return blocks[0]

    def product_scatter(lefts, rights, dims):
        odd = matmul(lefts, rights, dims, 1, 2, n_hi, width)
        theirs = flip(odd, 1)
        far = []
        if n_hi > 1:
            far = list(matmul(lefts, rights, dims, 2, 2, n_hi - 1, width, theirs, 1))
        near = matmul(lefts, rights, dims, 0, 2, 1, width, theirs, 0, F32)[0]
        return reduce_far(near, far)

    def my_row(values):
        return lax.dynamic_slice_in_dim(values, row * length, length, 0)

    def other_row(values):
        return lax.dynamic_slice_in_dim(values, (1 - row) * length, length, 0)

    def to_row(values):
        return jnp.concatenate([my_row(values), flip(other_row(values), ROW)], axis=1)

    def from_row(values):
        mine, theirs = values[:, :block], flip(values[:, block:], ROW)
        return jnp.where(
            row == 0,
            jnp.concatenate([mine, theirs], axis=0),
            jnp.concatenate([theirs, mine], axis=0),
        )

    def cut(values):
        return [values[c * chunk : (c + 1) * chunk] for c in range(CHUNKS)]

    stream = to_row(tokens)
    x_parts = [gather(v) for v in cut(stream)]
    thin, broad = a_in.shape[1], a_down.shape[0]
    packed = jnp.concatenate(
        [
            jnp.pad(
                jnp.concatenate(
                    [
                        jnp.transpose(a_in, (0, 2, 1)).reshape(6 * RANK, thin),
                        b_dmodel.reshape(5 * RANK, thin),
                        m_dmodel,
                    ],
                    axis=0,
                ),
                ((0, 0), (0, broad - thin)),
            ),
            jnp.transpose(a_down),
            b_hidden.reshape(2 * RANK, broad),
            m_hidden,
        ],
        axis=0,
    ).astype(BF16)
    model_rows = 11 * RANK + 5
    gathered = lax.all_gather(packed, ("dp", "mp"), axis=0)
    model = jnp.transpose(gathered[:, :model_rows, :thin], (1, 0, 2)).reshape(model_rows, D)
    model = to_relative(model)
    wide = jnp.transpose(gathered[:, model_rows:, :], (1, 0, 2)).reshape(3 * RANK + 2, n_mp, hidden)
    wide = jnp.concatenate(
        [lax.dynamic_index_in_dim(wide, i, 1, False) for i in (me, me ^ ROW)], axis=1
    )

    qkv_other = flip(query_key_value_weight, ROW)
    out_other = flip(output_weight, ROW)
    grad_output = to_row(cotangent)
    gate_up_other = flip(gate_up_weight, ROW)
    down_other = flip(down_weight, ROW)
    cot_parts = [gather(v) for v in cut(grad_output)]

    segments = lax.dynamic_slice_in_dim(segment_ids, row, 1, 0)
    valid = lax.dynamic_slice_in_dim(valid_mask, row, 1, 0)
    starts = jnp.zeros_like(segments)
    for s in range(SEGMENTS):
        count = jnp.sum((segments == s).astype(jnp.int32))
        starts = starts + jnp.where(segments > s, count, 0)
    table = jnp.concatenate([jnp.sum(valid, axis=1), starts[0, ::BQ] // BK])
    index = jnp.arange(length, dtype=jnp.int32)[None, :]
    frequency = ROPE_BASE ** (-(jnp.arange(HEAD // 2, dtype=F32) * (2.0 / HEAD)))
    angles = (index - starts)[0].astype(F32)[:, None] * frequency
    cos, sin = jnp.cos(angles), jnp.sin(angles)
    cosine = jnp.concatenate([cos, cos], axis=1)
    sine = jnp.concatenate([-sin, sin], axis=1)

    low_a = jnp.transpose(model[: 6 * RANK])
    model_b = [model[(6 + k) * RANK : (7 + k) * RANK] for k in range(5)]
    model_m = model[11 * RANK :].astype(F32)
    down_a = jnp.transpose(wide[:RANK])
    hidden_b = wide[RANK : 3 * RANK].reshape(2, RANK, 2 * hidden)
    hidden_m = wide[3 * RANK :].astype(F32)
    gains = to_relative(norm_gains)
    gain_columns = [gains[k].reshape(D, 1) for k in range(2)]
    lane = ((0, 0), (0, 128 - 6 * RANK))
    low_in = [jnp.pad((low_a.astype(F32) * g).astype(BF16), lane) for g in gain_columns]
    qkv_b = jnp.stack([b[:, :width] for b in model_b[:3]])
    qkv_v, qkv_sq = merge_columns(
        perm, query_key_value_weight, qkv_other, low_a, qkv_b, gain_columns[0], 0
    )
    qkv_m = model_m[:3, :width].reshape(3, 1, width)
    qkv_scale = qkv_m * lax.rsqrt(qkv_sq)
    out_a = low_a[:width, 3 * RANK : 4 * RANK]
    out_v, out_sq = merge_rows(perm, output_weight, out_other, out_a, model_b[3])
    gu_v, gu_sq = merge_columns(
        perm, gate_up_weight, gate_up_other, low_a, hidden_b, gain_columns[1], 4
    )
    gu_m = hidden_m.reshape(2, 1, 2 * hidden)
    gu_scale = gu_m * lax.rsqrt(gu_sq)
    down_v, down_sq = merge_rows(perm, down_weight, down_other, down_a, model_b[4])
    row_sq = total_relative(jnp.concatenate([out_sq, down_sq], axis=0))
    row_m = model_m[3:5]
    row_scale = row_m * lax.rsqrt(row_sq)
    out_scale, down_scale = row_scale[0:1], row_scale[1:2]

    qkv, qkv_u, r1, attended, lse = [], [], [], [], []
    keys, values = [], []
    cos_cut, sin_cut = cut(cosine), cut(sine)
    for c in range(CHUNKS):
        o, u, r = project_qkv(x_parts[c], qkv_v, low_in[0], qkv_scale, cos_cut[c], sin_cut[c])
        qkv.append(o)
        qkv_u.append(u)
        r1.append(r)
        keys.append(o[:, width : 2 * width])
        values.append(o[:, 2 * width :])
        att, l = attention_forward(
            table, o, jnp.concatenate(keys), jnp.concatenate(values), starts, c * chunk
        )
        attended.append(att)
        lse.append(l)
    middle, out_y, h_parts = [], [], []
    stream_cut, cot_cut = cut(stream), cut(grad_output)
    for c in range(CHUNKS):
        y = product_scatter([attended[c]], [(out_v, None)], NN) * out_scale[:, :width]
        out_y.append(y)
        h = stream_cut[c].astype(F32) + y
        middle.append(h)
        h_parts.append(gather(h.astype(BF16)))
    gate, up, hid, gu_u, down_u, r2 = [], [], [], [], [], []
    down_a_wide = jnp.pad(down_a, ((0, 0), (0, 128 - RANK)))
    for c in range(CHUNKS):
        g, u, h, ug, ud, r = project_hidden(h_parts[c], gu_v, low_in[1], gu_scale, down_a_wide)
        for bag, value in zip((gate, up, hid, gu_u, down_u, r2), (g, u, h, ug, ud, r)):
            bag.append(value)

    down_b_wide = jnp.pad(model_b[4], ((0, 128 - RANK), (0, 0)))
    g_gate, g_up, gu_t, inner2, down_gu = [], [], [], [], []
    for c in range(CHUNKS):
        outs = hidden_backward(
            cot_parts[c], down_v, down_scale, down_b_wide, gate[c], up[c], gu_scale
        )
        for bag, value in zip((g_gate, g_up, gu_t, inner2, down_gu), outs):
            bag.append(value)
    grad_middle, grad_out_parts = [], []
    for c in range(CHUNKS):
        sums = total(inner2[c][:, 0])
        g_x = product_scatter([g_gate[c], g_up[c]], [(gu_v, 0), (gu_v, 1)], NT)
        r = r2[c][:, :1]
        g = cot_cut[c].astype(F32) + r * g_x - middle[c] * (r * r * (sums / D)[:, None])
        grad_middle.append(g)
        grad_out_parts.append(gather((g * out_scale[:, :width]).astype(BF16)))
    grad_att = []
    for c in range(CHUNKS):
        rights = [out_v[:, p * width : (p + 1) * width] for p in range(positions)]
        grad_att.append(
            matmul(grad_out_parts[c], [(v, None) for v in rights], NT, 0, 1, 1, width)[0]
        )
    att_all = jnp.concatenate(attended)
    g_q, g_k, g_v, qkv_t, inner1 = attention_backward(
        table,
        jnp.concatenate(qkv),
        jnp.concatenate(grad_att),
        att_all,
        jnp.concatenate(lse, axis=2),
        starts,
        cosine,
        sine,
        qkv_scale,
    )
    sums1 = total(jnp.sum(inner1, axis=1))
    input_grad = []
    for c in range(CHUNKS):
        lefts = [cut(g)[c] for g in (g_q, g_k, g_v)]
        g_x = product_scatter(lefts, [(qkv_v, 0), (qkv_v, 1), (qkv_v, 2)], NT)
        r = r1[c][:, :1]
        s = cut(sums1)[c][:, None]
        g = grad_middle[c] + r * g_x - stream_cut[c].astype(F32) * (r * r * (s / D))
        input_grad.append(g.astype(BF16))

    down_y = [product_scatter([hid[c]], [(down_v, None)], NN) * down_scale[:, :width] for c in range(CHUNKS)]
    activations = jnp.concatenate(
        [(middle[c] + down_y[c]).astype(BF16) for c in range(CHUNKS)]
    )
    down_t = sum(jnp.sum(cot_cut[c].astype(F32) * down_y[c], axis=0) for c in range(CHUNKS))
    out_t = sum(jnp.sum(grad_middle[c] * out_y[c], axis=0) for c in range(CHUNKS))

    def over_tokens(left, right):
        return sum(dot(a, b, TN) for a, b in zip(left, right))

    def spread(lefts, parts):
        return jnp.concatenate(
            [over_tokens(lefts, [p[k] for p in parts]) for k in range(positions)], axis=1
        )

    def small(values):
        return values.astype(BF16)

    def to_natural(values):
        blocks = [values[:, i * block : (i + 1) * block] for i in place_of]
        return jnp.stack(swapped(blocks))

    def to_places(values):
        rows, both = values.shape
        half = both // 2
        holder = jnp.zeros((n_mp, rows, half), F32)
        holder = lax.dynamic_update_slice_in_dim(holder, values[None, :, :half], me, 0)
        return lax.dynamic_update_slice_in_dim(holder, values[None, :, half:], me ^ ROW, 0)

    def to_owner(values):
        rows, size = values.shape[1:]
        piece = size // n_dp
        v = jnp.transpose(values.reshape(n_mp, rows, n_dp, piece), (0, 2, 1, 3))
        v = v.reshape(n_dp, n_mp, rows, piece)
        mask, count = 1, n_mp
        while count > 1:
            v = v.reshape(n_dp, count // 2, 2, rows, piece)
            bit = (me // mask) % 2
            kept = lax.dynamic_index_in_dim(v, bit, 2, False)
            sent = lax.dynamic_index_in_dim(v, 1 - bit, 2, False)
            v = kept + flip(sent, mask)
            mask, count = mask * 2, count // 2
        v = v.reshape(n_dp, rows, piece)
        mine = lax.axis_index("dp")
        mask, count = 1, n_dp
        while count > 1:
            v = v.reshape(count // 2, 2, rows, piece)
            bit = (mine // mask) % 2
            kept = lax.dynamic_index_in_dim(v, bit, 1, False)
            sent = lax.dynamic_index_in_dim(v, 1 - bit, 1, False)
            v = kept + lax.ppermute(sent, "dp", [(i, i ^ mask) for i in range(n_dp)])
            mask, count = mask * 2, count // 2
        return v.reshape(rows, piece)

    gu_t = sum(gu_t)
    gu_coef = gu_t / gu_sq
    down_coef = jnp.concatenate(gather(down_t[None]), axis=1) / row_sq[1:2]
    gu_gu = []
    for c in range(CHUNKS):
        low = jnp.concatenate(
            [
                dot(g_gate[c], hidden_b[0], NT),
                dot(g_up[c], hidden_b[1], NT),
            ],
            axis=1,
        )
        gu_gu.append(small(low * r2[c][:, :1]))
    gu_ga = 2.0 * gains[1:2] * spread(gu_gu, h_parts)
    gu_na = jnp.concatenate(
        [dot(small(hidden_b[k] * gu_coef[k]), gu_v[k], NT) for k in range(2)], axis=0
    )
    gu_ga = gu_ga - 2.0 / gains[1:2] * gu_na
    low_back = [small(low_a.astype(F32) / g) for g in gain_columns]
    gu_gb = []
    for k, bag in enumerate((g_gate, g_up)):
        at = (4 + k) * RANK
        first = over_tokens([u[:, at : at + RANK] for u in gu_u], bag)
        second = dot(low_back[1][:, at : at + RANK], gu_v[k], TN) * gu_coef[k]
        gu_gb.append(2.0 * (first - second))
    down_ga = over_tokens(down_gu, hid)[:RANK] - dot(
        small(model_b[4] * down_coef), down_v, NT
    )
    down_gb = spread(down_u, cot_parts)[:RANK] * down_scale - dot(down_a, down_v, TN) * down_coef
    mlp_model = jnp.concatenate(
        [to_natural(jnp.concatenate([gu_ga, 2.0 * down_gb])), to_places((down_t / row_m[1, :width])[None])],
        axis=1,
    )
    mlp_wide = to_places(
        jnp.concatenate([2.0 * down_ga, *gu_gb, (gu_t / gu_m).reshape(2, 2 * hidden)])
    )
    mlp_model = to_owner(mlp_model)
    mlp_wide = to_owner(mlp_wide)

    qkv_coef = qkv_t / qkv_sq
    out_coef = jnp.concatenate(gather(out_t[None]), axis=1) / row_sq[0:1]
    grads = (g_q, g_k, g_v)
    low = jnp.concatenate([dot(grads[k], qkv_b[k], NT) for k in range(3)], axis=1)
    r1_all = jnp.concatenate(r1)[:, :1]
    qkv_gu = cut(small(low * r1_all))
    qkv_ga = 2.0 * gains[0:1] * spread(qkv_gu, x_parts)
    qkv_na = jnp.concatenate(
        [dot(small(qkv_b[k] * qkv_coef[k]), qkv_v[k], NT) for k in range(3)], axis=0
    )
    qkv_ga = qkv_ga - 2.0 / gains[0:1] * qkv_na
    u_all = jnp.concatenate(qkv_u)
    qkv_gb = []
    for k in range(3):
        at = k * RANK
        first = dot(u_all[:, at : at + RANK], grads[k], TN)
        second = dot(low_back[0][:, at : at + RANK], qkv_v[k], TN) * qkv_coef[k]
        qkv_gb.append(2.0 * (first - second))
    out_gu, out_u = [], []
    for c in range(CHUNKS):
        out_gu.append(
            small(
                sum(
                    dot(grad_out_parts[c][p], model_b[3][:, p * width : (p + 1) * width], NT)
                    for p in range(positions)
                )
            )
        )
        out_u.append(small(dot(attended[c], out_a)))
    out_ga = over_tokens(out_gu, attended) - dot(small(model_b[3] * out_coef), out_v, NT)
    out_gb = spread(out_u, grad_out_parts) - dot(out_a, out_v, TN) * out_coef
    att_model = jnp.concatenate(
        [
            to_natural(jnp.concatenate([qkv_ga, 2.0 * out_gb])),
            to_places(
                jnp.concatenate(
                    [
                        2.0 * out_ga,
                        *qkv_gb,
                        (qkv_t / qkv_m).reshape(3, width),
                        (out_t / row_m[0, :width])[None],
                    ]
                )
            ),
        ],
        axis=1,
    )
    att_model = to_owner(att_model)

    def stacked(values, count):
        return values.reshape(count, RANK, values.shape[1])

    rank4 = 4 * RANK
    grad_a = jnp.concatenate(
        [
            stacked(att_model[: 3 * RANK], 3),
            stacked(att_model[rank4 : rank4 + RANK], 1),
            stacked(mlp_model[: 2 * RANK], 2),
        ]
    )
    grad_b = jnp.concatenate(
        [
            stacked(att_model[rank4 + RANK : rank4 + 4 * RANK], 3),
            stacked(att_model[3 * RANK : rank4], 1),
            stacked(mlp_model[2 * RANK : 3 * RANK], 1),
        ]
    )
    grad_m = jnp.concatenate([att_model[rank4 + 4 * RANK :], mlp_model[3 * RANK :]])
    return (
        from_row(activations),
        from_row(jnp.concatenate(input_grad)),
        jnp.transpose(grad_a, (0, 2, 1)),
        jnp.transpose(mlp_wide[:RANK]),
        grad_b,
        stacked(mlp_wide[RANK : 3 * RANK], 2),
        grad_m,
        mlp_wide[3 * RANK :],
    )


def solution(mesh):
    in_specs = (
        P("dp", "mp"),
        P(),
        P(None, None, "mp"),
        P("mp", None),
        P(None, None, "mp"),
        P("mp", None),
        P(None, ("dp", "mp"), None),
        P(("dp", "mp"), None),
        P(None, None, ("dp", "mp")),
        P(None, None, ("dp", "mp")),
        P(None, ("dp", "mp")),
        P(None, ("dp", "mp")),
        P("dp", None),
        P("dp", None),
        P("dp", "mp"),
    )
    out_specs = (
        P("dp", "mp"),
        P("dp", "mp"),
        P(None, ("dp", "mp"), None),
        P(("dp", "mp"), None),
        P(None, None, ("dp", "mp")),
        P(None, None, ("dp", "mp")),
        P(None, ("dp", "mp")),
        P(None, ("dp", "mp")),
    )
    local = functools.partial(layer, mesh.shape["dp"], mesh.shape["mp"])
    return jax.shard_map(local, mesh=mesh, in_specs=in_specs, out_specs=out_specs, check_vma=False)
```

time: 2750 us -> 1160 us (0.42)
  waiting for transfers between devices: 1230 us -> 344 us
  matrix products: 586 us -> 90.5 us
  blocking collectives: 411 us -> 0 us
  Pallas kernels: 0 us -> 401 us
  other arithmetic: 232 us -> 96.3 us
  local copies, waits for them, and re-layouts: 246 us -> 127 us
  starting transfers between devices: 1.5 us -> 68.2 us
    unnamed x23 -> x1, waiting for transfers between devices: 722 us -> 0.02 us
    dot_general x70 -> x72, matrix products: 564 us -> 90.5 us  [dot(): return lax.dot_general(a, b, dims, preferred_element_type=F32)]
    pallas_call x0 -> x39, Pallas kernels: none -> 401 us  [the longest x26 163 us: matmul(): pl.pallas_call(body, out_shape=out, grid=(count, rows // bm), in_specs=sp...]
    reduce_scatter x4 -> x0, waiting for transfers between devices: 344 us -> none  [the longest x2 233 us: scatter_inputs(): lax.psum_scatter(values.astype(jnp.bfloat16), 'mp', scatter_dimension=1,...]
    ppermute x0 -> x77, waiting for transfers between devices: none -> 343 us  [the longest x71 339 us: flip(): return lax.ppermute(values, 'mp', [(i, i ^ mask) for i in range(n_mp)])]
    all_gather x8 -> x0, blocking collectives: 318 us -> none  [the longest x1 62.1 us: local(): lax.all_gather(b_hidden.astype(jnp.bfloat16), ('dp', 'mp'), axis=2, tiled...]
    all_gather x4 -> x1, waiting for transfers between devices: 146 us -> 0.01 us  [layer(): gathered = lax.all_gather(packed, ('dp', 'mp'), axis=0)]
    psum x4 -> x0, blocking collectives: 93 us -> none  [token_sums(): return lax.psum(values, 'mp')]
  transfers between devices with their start and end apart: 17 -> 78, of which waited for: 14 -> 30; matrix products, arithmetic and copies ran while one was open for 25% -> 22% of each run, Pallas kernels for 0% -> 31%
where the time goes in v1:
time: 1160 us; the launch traced here: 1140 us
  Pallas kernels  401 us (35%)
  waiting for transfers between devices  344 us (30%)
  local copies, waits for them, and re-layouts  127 us (11%)
  other arithmetic  96.3 us (8%)
  matrix products  90.5 us (8%)
  starting transfers between devices  68.2 us (6%)
  between operations  17.1 us (1%)
    ppermute x71, waiting for transfers between devices, flip(): return lax.ppermute(values, 'mp', [(i, i ^ mask) for i in range(n_mp)])  339 us
    pallas_call x26, Pallas kernels, matmul(): pl.pallas_call(body, out_shape=out, grid=(count, rows // bm), in_specs=sp...  163 us
    dot_general x72, matrix products, dot(): return lax.dot_general(a, b, dims, preferred_element_type=F32)  90.5 us
    ppermute x71, starting transfers between devices, flip(): return lax.ppermute(values, 'mp', [(i, i ^ mask) for i in range(n_mp)])  56.2 us
    pallas_call x1, Pallas kernels, attention_backward(): pl.pallas_call(body, out_shape=outs, grid_spec=pltpu.PrefetchScalarGridSp...  53.5 us
    pallas_call x2, Pallas kernels, project_hidden(): pl.pallas_call(body, out_shape=outs, grid=(rows // bm,), in_specs=[pl.Blo...  44.1 us
    pallas_call x2, Pallas kernels, attention_forward(): pl.pallas_call(body, out_shape=outs, grid_spec=pltpu.PrefetchScalarGridSp...  40.4 us
    unnamed x378, local copies, waits for them, and re-layouts  39.6 us
  transfers between devices with their start and end apart: 78, of which 30 were waited for; matrix products, arithmetic and copies ran while one was open for 22% of the time, Pallas kernels for 31%

profile of v1, /device:TPU:0, one launch (start us, length us, event | category | flops | bytes accessed | tf_op | source)
XLA Modules:
  0.0 1143.2 jit_solution(9464616578012417986)
XLA Ops:
  20.5 5.2 subtract_convert_fusion
  26.7 43.7 %collective-permute-done = bf16[2048,256]{1,0:T(8,128)(2,1)S(1)} collective-permute-done((bf16[2048,256]{1,0:T(8,128)(2,1)S(1)}, bf16[2048,256]{1,0:T(8,128)(2,1)S(1)}, u32[]{:S(2)}, u32[]{:S(2)}) %collective-permute-start) | collective-permute-done | bytes 1048608 | tf_op jit(solution)/shard_map/ppermute | solution.py:587
  84.8 14.3 %collective-permute-done.2.refs_2_ = bf16[1024,512]{1,0:T(8,128)(2,1)} collective-permute-done((bf16[1024,512]{1,0:T(8,128)(2,1)S(1)}, bf16[1024,512]{1,0:T(8,128)(2,1)}, u32[]{:S(2)}, u32[]{:S(2)}) %collective-permute-start.2) | collective-permute-done | bytes 1048608 | tf_op jit(solution)/shard_map/ppermute | solution.py:587
  121.2 16.4 %collective-permute-done.4.other_ref = bf16[3,2048,256]{2,1,0:T(8,128)(2,1)} collective-permute-done((bf16[3,2048,256]{2,1,0:T(8,128)(2,1)}, bf16[3,2048,256]{2,1,0:T(8,128)(2,1)}, u32[]{:S(2)}, u32[]{:S(2)}) %collective-permute-start.4) | collective-permute-done | bytes 3145760 | tf_op jit(solution)/shard_map/ppermute | solution.py:587
  139.3 10.0 merge_columns.2
  151.5 12.8 %project_qkv.2 = (bf16[1024,1536]{1,0:T(8,128)(2,1)}, bf16[1024,128]{1,0:T(8,128)(2,1)}, f32[1024,128]{1,0:T(8,128)}) custom-call(bf16[1024,512]{1,0:T(8,128)(2,1)} %copy-done.31, bf16[1024,512]{1,0:T(8,128)(2,1)} %collective-permute-done.1.refs_1_, bf16[1024,512]{1,0:T(8,128)(2,1)} %collective-permute-done.2.refs_2_, ...), custom_call_target="tpu_custom_call" | custom-call | flops 6442450944 | bytes 14417920 | tf_op jit(solution)/shard_map/project_qkv/pallas_call | solution.py:171
  169.0 17.9 %attention_forward.2 = (bf16[1024,512]{1,0:T(8,128)(2,1)}, f32[4,1,1024]{2,1,0:T(1,128)}) custom-call(s32[9]{0:T(128)} %pad_add_fusion.table_ref, bf16[1024,1536]{1,0:T(8,128)(2,1)} %get-tuple-element.55.q_ref, bf16[1024,512]{1,0:T(8,128)(2,1)} %get-tuple-element.205.k_ref, bf16[1024,512]{1,0:T(8,128)(2,1)} %get-tuple-element.204.v_ref, s32[1,2048]{1,0:T(1,128)} %copy-done.151), custom_call_target="tpu_custom_call" | custom-call | flops 1073741824 | bytes 3162112 | tf_op jit(solution)/shard_map/attention_forward/pallas_call | solution.py:405
  187.6 7.3 merge_rows.2
  199.9 12.8 %project_qkv.3 = (bf16[1024,1536]{1,0:T(8,128)(2,1)}, bf16[1024,128]{1,0:T(8,128)(2,1)}, f32[1024,128]{1,0:T(8,128)}) custom-call(bf16[1024,512]{1,0:T(8,128)(2,1)} %copy-done.34, bf16[1024,512]{1,0:T(8,128)(2,1)} %collective-permute-done.17.refs_1_, bf16[1024,512]{1,0:T(8,128)(2,1)} %collective-permute-done.18.refs_2_, ...), custom_call_target="tpu_custom_call" | custom-call | flops 6442450944 | bytes 14417920 | tf_op jit(solution)/shard_map/project_qkv/pallas_call | solution.py:171
  217.8 22.6 %attention_forward.3 = (bf16[1024,512]{1,0:T(8,128)(2,1)}, f32[4,1,1024]{2,1,0:T(1,128)}) custom-call(s32[9]{0:T(128)} %pad_add_fusion.table_ref, bf16[1024,1536]{1,0:T(8,128)(2,1)} %get-tuple-element.64.q_ref, bf16[2048,512]{1,0:T(8,128)(2,1)} %pad_maximum_fusion.1.k_ref, bf16[2048,512]{1,0:T(8,128)(2,1)} %pad_maximum_fusion.2.v_ref, s32[1,2048]{1,0:T(1,128)} %copy-done.151), custom_call_target="tpu_custom_call" | custom-call | flops 2147483648 | bytes 5259264 | tf_op jit(solution)/shard_map/attention_forward/pallas_call | solution.py:405
  248.8 9.7 merge_rows.3
  282.3 13.6 %collective-permute-done.7 = bf16[1024,512]{1,0:T(8,128)(2,1)S(1)} collective-permute-done((bf16[1024,512]{1,0:T(8,128)(2,1)}, bf16[1024,512]{1,0:T(8,128)(2,1)S(1)}, u32[]{:S(2)}, u32[]{:S(2)}) %collective-permute-start.7) | collective-permute-done | bytes 1048608 | tf_op jit(solution)/shard_map/ppermute | solution.py:587
  295.8 20.9 %collective-permute-done.21 = bf16[1024,512]{1,0:T(8,128)(2,1)S(1)} collective-permute-done((bf16[1024,512]{1,0:T(8,128)(2,1)}, bf16[1024,512]{1,0:T(8,128)(2,1)S(1)}, u32[]{:S(2)}, u32[]{:S(2)}) %collective-permute-start.21) | collective-permute-done | bytes 1048608 | tf_op jit(solution)/shard_map/ppermute | solution.py:587
  329.0 19.8 %collective-permute-done.23.refs_2_ = bf16[1024,512]{1,0:T(8,128)(2,1)} collective-permute-done((bf16[1024,512]{1,0:T(8,128)(2,1)}, bf16[1024,512]{1,0:T(8,128)(2,1)}, u32[]{:S(2)}, u32[]{:S(2)}) %collective-permute-start.23) | collective-permute-done | bytes 1048608 | tf_op jit(solution)/shard_map/ppermute | solution.py:587
  350.1 8.7 copy.250.own_ref
  366.7 8.5 copy.251.other_ref
  375.2 14.4 %merge_columns.3 = (bf16[2,2048,1408]{2,1,0:T(8,128)(2,1)}, f32[2,1,1408]{2,1,0:T(1,128)}) custom-call(s32[8]{0:T(128)} %broadcast_xor_fusion.perm_ref, bf16[2,2048,704]{2,1,0:T(8,128)(2,1)} %copy.250.own_ref, bf16[2,2048,704]{2,1,0:T(8,128)(2,1)} %copy.251.other_ref, bf16[2048,96]{1,0:T(8,128)(2,1)} %copy.243.a_ref, bf16[2,16,1408]{2,1,0:T(8,128)(2,1)} %bitcast.481, ...), custom_call_target="tpu_custom_call" | custom-call | flops 738197504 | bytes 23068672 | tf_op jit(solution)/shard_map/merge_columns/pallas_call | solution.py:76
  391.5 22.0 %project_hidden.3 = (bf16[1024,1408]{1,0:T(8,128)(2,1)}, bf16[1024,1408]{1,0:T(8,128)(2,1)}, bf16[1024,1408]{1,0:T(8,128)(2,1)}, bf16[1024,128]{1,0:T(8,128)(2,1...) custom-call(bf16[1024,512]{1,0:T(8,128)(2,1)} %get-tuple-element.308.refs_0_, ...), custom_call_target="tpu_custom_call" | custom-call | flops 11811160064 | bytes 25427968 | tf_op jit(solution)/shard_map/project_hidden/pallas_call | solution.py:226
  413.5 7.7 matmul_add.35
  423.7 22.1 %project_hidden.2 = (bf16[1024,1408]{1,0:T(8,128)(2,1)}, bf16[1024,1408]{1,0:T(8,128)(2,1)}, bf16[1024,1408]{1,0:T(8,128)(2,1)}, bf16[1024,128]{1,0:T(8,128)(2,1...) custom-call(bf16[1024,512]{1,0:T(8,128)(2,1)} %get-tuple-element.162.refs_0_, bf16[1024,512]{1,0:T(8,128)(2,1)} %copy-done.86, ...), custom_call_target="tpu_custom_call" | custom-call | flops 11811160064 | bytes 25427968 | tf_op jit(solution)/shard_map/project_hidden/pallas_call | solution.py:226
  445.8 8.2 matmul_add.29
  498.7 22.2 %collective-permute-done.16 = bf16[1024,512]{1,0:T(8,128)(2,1)} collective-permute-done((bf16[1024,512]{1,0:T(8,128)(2,1)}, bf16[1024,512]{1,0:T(8,128)(2,1)}, u32[]{:S(2)}, u32[]{:S(2)}) %collective-permute-start.16) | collective-permute-done | bytes 1048608 | tf_op jit(solution)/shard_map/ppermute | solution.py:587
  530.8 41.2 %collective-permute-done.65 = f32[1,512]{1,0:T(1,128)S(1)} collective-permute-done((f32[1,512]{1,0:T(1,128)S(1)}, f32[1,512]{1,0:T(1,128)S(1)}, u32[]{:S(2)}, u32[]{:S(2)}) %collective-permute-start.65) | collective-permute-done | bytes 2080 | tf_op jit(solution)/shard_map/ppermute | solution.py:587
  582.8 18.8 %collective-permute-done.27 = bf16[2048,256]{1,0:T(8,128)(2,1)S(1)} collective-permute-done((bf16[2048,256]{1,0:T(8,128)(2,1)S(1)}, bf16[2048,256]{1,0:T(8,128)(2,1)S(1)}, u32[]{:S(2)}, u32[]{:S(2)}) %collective-permute-start.27) | collective-permute-done | bytes 1048608 | tf_op jit(solution)/shard_map/ppermute | solution.py:587
  604.4 16.4 %hidden_backward.2 = (bf16[1024,1408]{1,0:T(8,128)(2,1)}, bf16[1024,1408]{1,0:T(8,128)(2,1)}, f32[2,1,1408]{2,1,0:T(1,128)}, f32[1024,128]{1,0:T(8,128)}, bf16[1024,128]{1,0:T(8,128)(2,1)}) custom-call(bf16[1024,512]{1,0:T(8,128)(2,1)} %copy-done.37, bf16[1024,512]{1,0:T(8,128)(2,1)} %copy-done.85, bf16[1024,512]{1,0:T(8,128)(2,1)} %copy-done.84, ...), custom_call_target="tpu_custom_call" | custom-call | flops 5905580032 | bytes 22293504 | tf_op jit(solution)/shard_map/hidden_backward/pallas_call | solution.py:285
  620.9 16.7 %hidden_backward.3 = (bf16[1024,1408]{1,0:T(8,128)(2,1)}, bf16[1024,1408]{1,0:T(8,128)(2,1)}, f32[2,1,1408]{2,1,0:T(1,128)}, f32[1024,128]{1,0:T(8,128)}, bf16[1024,128]{1,0:T(8,128)(2,1)}) custom-call(bf16[1024,512]{1,0:T(8,128)(2,1)} %copy-done.39, bf16[1024,512]{1,0:T(8,128)(2,1)} %copy-done.90, bf16[1024,512]{1,0:T(8,128)(2,1)} %collective-permute-done.40.refs_2_, ...), custom_call_target="tpu_custom_call" | custom-call | flops 5905580032 | bytes 22293504 | tf_op jit(solution)/shard_map/hidden_backward/pallas_call | solution.py:285
  655.0 12.1 %matmul_add.42 = bf16[2,1024,512]{2,1,0:T(8,128)(2,1)} custom-call(bf16[1024,1408]{1,0:T(8,128)(2,1)} %get-tuple-element.77.refs_0_, bf16[1024,1408]{1,0:T(8,128)(2,1)} %get-tuple-element.78.refs_1_, bf16[2,2048,1408]{2,1,0:T(8,128)(2,1)} %get-tuple-element.60.refs_4_.refs_2_.refs_3_, bf16[2,2048,1408]{2,1,0:T(8,128)(2,1)} %get-tuple-element.60.refs_4_.refs_2_.refs_3_), custom_call_target="tpu_custom_call" | custom-call | flops 5905580032 | bytes 19398656 | tf_op jit(solution)/shard_map/matmul_add/pallas_call | solution.py:344
  670.4 12.3 %matmul_add.38 = bf16[2,1024,512]{2,1,0:T(8,128)(2,1)} custom-call(bf16[1024,1408]{1,0:T(8,128)(2,1)} %get-tuple-element.70.refs_0_, bf16[1024,1408]{1,0:T(8,128)(2,1)} %get-tuple-element.71.refs_1_, bf16[2,2048,1408]{2,1,0:T(8,128)(2,1)} %get-tuple-element.60.refs_4_.refs_2_.refs_3_, bf16[2,2048,1408]{2,1,0:T(8,128)(2,1)} %get-tuple-element.60.refs_4_.refs_2_.refs_3_), custom_call_target="tpu_custom_call" | custom-call | flops 5905580032 | bytes 19398656 | tf_op jit(solution)/shard_map/matmul_add/pallas_call | solution.py:344
  737.9 8.4 collective-permute-done.73
  747.1 5.2 collective-permute-done.74
  757.9 7.8 matmul_add.40
  766.1 7.7 matmul_add.44
  782.5 7.9 matmul_add.39
  790.5 8.2 matmul_add.43
  798.7 10.6 collective-permute-done.43
  809.4 5.2 multiply_reduce_fusion
  835.6 32.6 %collective-permute-done.69 = f32[4,1,49,64]{3,1,2,0:T(1,128)S(1)} collective-permute-done((f32[4,1,49,64]{3,1,2,0:T(1,128)S(1)}, f32[4,1,49,64]{3,1,2,0:T(1,128)S(1)}, u32[]{:S(2)}, u32[]{:S(2)}) %collective-permute-start.69) | collective-permute-done | bytes 50208 | tf_op jit(solution)/shard_map/ppermute | solution.py:587
  885.7 5.7 matmul_add.41
  892.3 5.9 matmul_add.45
  901.0 53.5 %attention_backward.1 = (bf16[2048,512]{1,0:T(8,128)(2,1)}, bf16[2048,512]{1,0:T(8,128)(2,1)}, bf16[2048,512]{1,0:T(8,128)(2,1)}, f32[3,1,512]{2,1,0:T(1,128)}, f32[2048,128]{1,0:T(8,128)}) custom-call(s32[9]{0:T(128)} %pad_add_fusion.table_ref, bf16[2048,1536]{1,0:T(8,128)(2,1)} %pad_maximum_fusion.q_ref.k_ref.v_ref, ...), custom_call_target="tpu_custom_call" | custom-call | flops 10737418240 | bytes 15734784 | tf_op jit(solution)/shard_map/attention_backward/pallas_call | solution.py:506
  1017.5 8.1 matmul_add.49
  1027.2 8.2 matmul_add.46
  1047.1 10.3 collective-permute-done.60
  1073.2 5.2 matmul_add.50
  1078.4 5.3 matmul_add.47
  1083.8 6.7 collective-permute-done.54
  1092.7 17.2 %collective-permute-done.50 = bf16[1024,512]{1,0:T(8,128)(2,1)} collective-permute-done((bf16[1024,512]{1,0:T(8,128)(2,1)}, bf16[1024,512]{1,0:T(8,128)(2,1)}, u32[]{:S(2)}, u32[]{:S(2)}) %collective-permute-start.50) | collective-permute-done | bytes 1048608 | tf_op jit(solution)/shard_map/ppermute | solution.py:587
  1115.9 18.2 %collective-permute-done.55 = bf16[2048,256]{1,0:T(8,128)(2,1)S(1)} collective-permute-done((bf16[2048,256]{1,0:T(8,128)(2,1)S(1)}, bf16[2048,256]{1,0:T(8,128)(2,1)S(1)}, u32[]{:S(2)}, u32[]{:S(2)}) %collective-permute-start.55) | collective-permute-done | bytes 1048608 | tf_op jit(solution)/shard_map/ppermute | solution.py:587
  (840 shorter events, 429.7 us)
Async XLA Ops:
  7.2 91.9 %all-gather.2.cloned.1.call-start = ((), (), s32[]{:S(2)}) async-start(), calls=%async_computation | async-start | bytes 2973696 | tf_op jit(solution)/shard_map/all_gather | solution.py:670
  12.9 174.7 %collective-permute-start.5 = (bf16[256,2048]{1,0:T(8,128)(2,1)}, bf16[256,2048]{1,0:T(8,128)(2,1)}, u32[]{:S(2)}, u32[]{:S(2)}) collective-permute-start(bf16[256,2048]{1,0:T(8,128)(2,1)} %own_ref.5), channel_id=1, source_target_pairs={{0,2},{1,3},{2,0},{3,1},{4,6},{5,7},{6,4},{7,5},{8,10},{9,11},{10,... | collective-permute-start | bytes 3145736 | tf_op jit(solution)/shard_map/ppermute | solution.py:587
  17.6 52.8 %collective-permute-start = (bf16[2048,256]{1,0:T(8,128)(2,1)S(1)}, bf16[2048,256]{1,0:T(8,128)(2,1)S(1)}, u32[]{:S(2)}, u32[]{:S(2)}) collective-permute-start(bf16[2048,256]{1,0:T(8,128)(2,1)S(1)} %get-tuple-element.229), channel_id=1, source_target_pairs={{0,2},{1,3},{2,0},{3,1},{4,6},{5,7},{6,4},{7,5},{8,10},{9,11},{10,... | collective-permute-start | bytes 3145736 | tf_op jit(solution)/shard_map/ppermute | solution.py:587
  17.8 119.8 %collective-permute-start.4 = (bf16[3,2048,256]{2,1,0:T(8,128)(2,1)}, bf16[3,2048,256]{2,1,0:T(8,128)(2,1)}, u32[]{:S(2)}, u32[]{:S(2)}) collective-permute-start(bf16[3,2048,256]{2,1,0:T(8,128)(2,1)} %own_ref.4), channel_id=1, source_target_pairs={{0,2},{1,3},{2,0},{3,1},{4,6},{5,7},{6,4},{7,5},{8,10},{9,11},{10,... | collective-permute-start | bytes 9437192 | tf_op jit(solution)/shard_map/ppermute | solution.py:587
  72.8 26.3 %collective-permute-start.2 = (bf16[1024,512]{1,0:T(8,128)(2,1)S(1)}, bf16[1024,512]{1,0:T(8,128)(2,1)}, u32[]{:S(2)}, u32[]{:S(2)}) collective-permute-start(bf16[1024,512]{1,0:T(8,128)(2,1)S(1)} %get-tuple-element.226.refs_0_), channel_id=1, source_target_pairs={{0,4},{1,5},{2,6},{3,7},{4,0},{5,1},{6,2},{7,3},{8,12},{9,13},{10,... | collective-permute-start | bytes 3145736 | tf_op jit(solution)/shard_map/ppermute | solution.py:587
  84.7 66.0 %collective-permute-start.1 = (bf16[1024,512]{1,0:T(8,128)(2,1)S(1)}, bf16[1024,512]{1,0:T(8,128)(2,1)}, u32[]{:S(2)}, u32[]{:S(2)}) collective-permute-start(bf16[1024,512]{1,0:T(8,128)(2,1)S(1)} %get-tuple-element.226.refs_0_), channel_id=1, source_target_pairs={{0,1},{1,0},{2,3},{3,2},{4,5},{5,4},{6,7},{7,6},{8,9},{9,8},{10,11... | collective-permute-start | bytes 3145736 | tf_op jit(solution)/shard_map/ppermute | solution.py:587
  84.7 66.3 %collective-permute-start.18 = (bf16[1024,512]{1,0:T(8,128)(2,1)S(1)}, bf16[1024,512]{1,0:T(8,128)(2,1)}, u32[]{:S(2)}, u32[]{:S(2)}) collective-permute-start(bf16[1024,512]{1,0:T(8,128)(2,1)S(1)} %get-tuple-element.227.refs_0_), channel_id=1, source_target_pairs={{0,4},{1,5},{2,6},{3,7},{4,0},{5,1},{6,2},{7,3},{8,12},{9,13},{10,... | collective-permute-start | bytes 3145736 | tf_op jit(solution)/shard_map/ppermute | solution.py:587
  99.1 51.9 %collective-permute-start.3 = (bf16[1024,512]{1,0:T(8,128)(2,1)}, bf16[1024,512]{1,0:T(8,128)(2,1)}, u32[]{:S(2)}, u32[]{:S(2)}) collective-permute-start(bf16[1024,512]{1,0:T(8,128)(2,1)} %collective-permute-done.2.refs_2_), channel_id=1, source_target_pairs={{0,1},{1,0},{2,3},{3,2},{4,5},{5,4},{6,7},{7,6},{8,9},{9,8},{10,11... | collective-permute-start | bytes 3145736 | tf_op jit(solution)/shard_map/ppermute | solution.py:587
  137.6 111.2 %collective-permute-start.8 = (bf16[704,2048]{1,0:T(8,128)(2,1)}, bf16[704,2048]{1,0:T(8,128)(2,1)}, u32[]{:S(2)}, u32[]{:S(2)}) collective-permute-start(bf16[704,2048]{1,0:T(8,128)(2,1)} %own_ref.6), channel_id=1, source_target_pairs={{0,2},{1,3},{2,0},{3,1},{4,6},{5,7},{6,4},{7,5},{8,10},{9,11},{10,... | collective-permute-start | bytes 8650760 | tf_op jit(solution)/shard_map/ppermute | solution.py:587
  150.7 216.0 %collective-permute-start.14 = (bf16[2,2048,704]{1,2,0:T(8,128)(2,1)}, bf16[2,2048,704]{1,2,0:T(8,128)(2,1)}, u32[]{:S(2)}, u32[]{:S(2)}) collective-permute-start(bf16[2,2048,704]{1,2,0:T(8,128)(2,1)} %param.20), channel_id=1, source_target_pairs={{0,2},{1,3},{2,0},{3,1},{4,6},{5,7},{6,4},{7,5},{8,10},{9,11},{10,... | collective-permute-start | bytes 17301512 | tf_op jit(solution)/shard_map/ppermute | solution.py:587
  151.0 48.9 %collective-permute-start.17 = (bf16[1024,512]{1,0:T(8,128)(2,1)S(1)}, bf16[1024,512]{1,0:T(8,128)(2,1)}, u32[]{:S(2)}, u32[]{:S(2)}) collective-permute-start(bf16[1024,512]{1,0:T(8,128)(2,1)S(1)} %get-tuple-element.227.refs_0_), channel_id=1, source_target_pairs={{0,1},{1,0},{2,3},{3,2},{4,5},{5,4},{6,7},{7,6},{8,9},{9,8},{10,11... | collective-permute-start | bytes 3145736 | tf_op jit(solution)/shard_map/ppermute | solution.py:587
  151.0 48.9 %collective-permute-start.19 = (bf16[1024,512]{1,0:T(8,128)(2,1)}, bf16[1024,512]{1,0:T(8,128)(2,1)}, u32[]{:S(2)}, u32[]{:S(2)}) collective-permute-start(bf16[1024,512]{1,0:T(8,128)(2,1)} %collective-permute-done.18.refs_2_), channel_id=1, source_target_pairs={{0,1},{1,0},{2,3},{3,2},{4,5},{5,4},{6,7},{7,6},{8,9},{9,8},{10,11... | collective-permute-start | bytes 3145736 | tf_op jit(solution)/shard_map/ppermute | solution.py:587
  199.8 65.3 %collective-permute-start.6 = (bf16[2,1024,512]{2,1,0:T(8,128)(2,1)}, bf16[2,1024,512]{2,1,0:T(8,128)(2,1)S(1)}, u32[]{:S(2)}, u32[]{:S(2)}) collective-permute-start(bf16[2,1024,512]{2,1,0:T(8,128)(2,1)} %matmul_add.26), channel_id=1, source_target_pairs={{0,1},{1,0},{2,3},{3,2},{4,5},{5,4},{6,7},{7,6},{8,9},{9,8},{10,11... | collective-permute-start | bytes 6291464 | tf_op jit(solution)/shard_map/ppermute | solution.py:587
  269.5 26.3 %collective-permute-start.7 = (bf16[1024,512]{1,0:T(8,128)(2,1)}, bf16[1024,512]{1,0:T(8,128)(2,1)S(1)}, u32[]{:S(2)}, u32[]{:S(2)}) collective-permute-start(bf16[1024,512]{1,0:T(8,128)(2,1)} %bitcast.474), channel_id=1, source_target_pairs={{0,4},{1,5},{2,6},{3,7},{4,0},{5,1},{6,2},{7,3},{8,12},{9,13},{10,... | collective-permute-start | bytes 3145736 | tf_op jit(solution)/shard_map/ppermute | solution.py:587
  274.3 42.4 %collective-permute-start.21 = (bf16[1024,512]{1,0:T(8,128)(2,1)}, bf16[1024,512]{1,0:T(8,128)(2,1)S(1)}, u32[]{:S(2)}, u32[]{:S(2)}) collective-permute-start(bf16[1024,512]{1,0:T(8,128)(2,1)} %bitcast.475), channel_id=1, source_target_pairs={{0,4},{1,5},{2,6},{3,7},{4,0},{5,1},{6,2},{7,3},{8,12},{9,13},{10,... | collective-permute-start | bytes 3145736 | tf_op jit(solution)/shard_map/ppermute | solution.py:587
  322.3 26.5 %collective-permute-start.23 = (bf16[1024,512]{1,0:T(8,128)(2,1)}, bf16[1024,512]{1,0:T(8,128)(2,1)}, u32[]{:S(2)}, u32[]{:S(2)}) collective-permute-start(bf16[1024,512]{1,0:T(8,128)(2,1)} %get-tuple-element.308.refs_0_), channel_id=1, source_target_pairs={{0,4},{1,5},{2,6},{3,7},{4,0},{5,1},{6,2},{7,3},{8,12},{9,13},{10,... | collective-permute-start | bytes 3145736 | tf_op jit(solution)/shard_map/ppermute | solution.py:587
  325.2 169.9 %collective-permute-start.28 = (bf16[2048,256]{1,0:T(8,128)(2,1)}, bf16[2048,256]{1,0:T(8,128)(2,1)}, u32[]{:S(2)}, u32[]{:S(2)}) collective-permute-start(bf16[2048,256]{1,0:T(8,128)(2,1)} %get-tuple-element.221), channel_id=1, source_target_pairs={{0,2},{1,3},{2,0},{3,1},{4,6},{5,7},{6,4},{7,5},{8,10},{9,11},{10,... | collective-permute-start | bytes 3145736 | tf_op jit(solution)/shard_map/ppermute | solution.py:587
  328.5 63.0 %collective-permute-start.22 = (bf16[1024,512]{1,0:T(8,128)(2,1)}, bf16[1024,512]{1,0:T(8,128)(2,1)}, u32[]{:S(2)}, u32[]{:S(2)}) collective-permute-start(bf16[1024,512]{1,0:T(8,128)(2,1)} %get-tuple-element.308.refs_0_), channel_id=1, source_target_pairs={{0,1},{1,0},{2,3},{3,2},{4,5},{5,4},{6,7},{7,6},{8,9},{9,8},{10,11... | collective-permute-start | bytes 3145736 | tf_op jit(solution)/shard_map/ppermute | solution.py:587
  328.5 63.0 %collective-permute-start.12 = (bf16[1024,512]{1,0:T(8,128)(2,1)}, bf16[1024,512]{1,0:T(8,128)(2,1)}, u32[]{:S(2)}, u32[]{:S(2)}) collective-permute-start(bf16[1024,512]{1,0:T(8,128)(2,1)} %get-tuple-element.162.refs_0_), channel_id=1, source_target_pairs={{0,4},{1,5},{2,6},{3,7},{4,0},{5,1},{6,2},{7,3},{8,12},{9,13},{10,... | collective-permute-start | bytes 3145736 | tf_op jit(solution)/shard_map/ppermute | solution.py:587
  348.8 42.7 %collective-permute-start.24 = (bf16[1024,512]{1,0:T(8,128)(2,1)}, bf16[1024,512]{1,0:T(8,128)(2,1)}, u32[]{:S(2)}, u32[]{:S(2)}) collective-permute-start(bf16[1024,512]{1,0:T(8,128)(2,1)} %collective-permute-done.23.refs_2_), channel_id=1, source_target_pairs={{0,1},{1,0},{2,3},{3,2},{4,5},{5,4},{6,7},{7,6},{8,9},{9,8},{10,11... | collective-permute-start | bytes 3145736 | tf_op jit(solution)/shard_map/ppermute | solution.py:587
  390.9 30.8 %collective-permute-start.11 = (bf16[1024,512]{1,0:T(8,128)(2,1)}, bf16[1024,512]{1,0:T(8,128)(2,1)S(1)}, u32[]{:S(2)}, u32[]{:S(2)}) collective-permute-start(bf16[1024,512]{1,0:T(8,128)(2,1)} %get-tuple-element.162.refs_0_), channel_id=1, source_target_pairs={{0,1},{1,0},{2,3},{3,2},{4,5},{5,4},{6,7},{7,6},{8,9},{9,8},{10,11... | collective-permute-start | bytes 3145736 | tf_op jit(solution)/shard_map/ppermute | solution.py:587
  391.5 30.3 %collective-permute-start.13 = (bf16[1024,512]{1,0:T(8,128)(2,1)}, bf16[1024,512]{1,0:T(8,128)(2,1)S(1)}, u32[]{:S(2)}, u32[]{:S(2)}) collective-permute-start(bf16[1024,512]{1,0:T(8,128)(2,1)} %collective-permute-done.12.refs_2_), channel_id=1, source_target_pairs={{0,1},{1,0},{2,3},{3,2},{4,5},{5,4},{6,7},{7,6},{8,9},{9,8},{10,11... | collective-permute-start | bytes 3145736 | tf_op jit(solution)/shard_map/ppermute | solution.py:587
  421.2 45.2 %collective-permute-start.25 = (bf16[2,1024,512]{2,1,0:T(8,128)(2,1)}, bf16[2,1024,512]{2,1,0:T(8,128)(2,1)S(1)}, u32[]{:S(2)}, u32[]{:S(2)}) collective-permute-start(bf16[2,1024,512]{2,1,0:T(8,128)(2,1)} %matmul_add.35), channel_id=1, source_target_pairs={{0,1},{1,0},{2,3},{3,2},{4,5},{5,4},{6,7},{7,6},{8,9},{9,8},{10,11... | collective-permute-start | bytes 6291464 | tf_op jit(solution)/shard_map/ppermute | solution.py:587
  479.2 41.7 %collective-permute-start.16 = (bf16[1024,512]{1,0:T(8,128)(2,1)}, bf16[1024,512]{1,0:T(8,128)(2,1)}, u32[]{:S(2)}, u32[]{:S(2)}) collective-permute-start(bf16[1024,512]{1,0:T(8,128)(2,1)} %bitcast.471), channel_id=1, source_target_pairs={{0,4},{1,5},{2,6},{3,7},{4,0},{5,1},{6,2},{7,3},{8,12},{9,13},{10,... | collective-permute-start | bytes 3145736 | tf_op jit(solution)/shard_map/ppermute | solution.py:587
  524.6 53.6 %collective-permute-start.30 = (bf16[1024,512]{1,0:T(8,128)(2,1)S(1)}, bf16[1024,512]{1,0:T(8,128)(2,1)S(1)}, u32[]{:S(2)}, u32[]{:S(2)}) collective-permute-start(bf16[1024,512]{1,0:T(8,128)(2,1)S(1)} %get-tuple-element.160.refs_0_), channel_id=1, source_target_pairs={{0,4},{1,5},{2,6},{3,7},{4,0},{5,1},{6,2},{7,3},{8,12},{9,13},{10,... | collective-permute-start | bytes 3145736 | tf_op jit(solution)/shard_map/ppermute | solution.py:587
  526.4 51.9 %collective-permute-start.40 = (bf16[1024,512]{1,0:T(8,128)(2,1)S(1)}, bf16[1024,512]{1,0:T(8,128)(2,1)}, u32[]{:S(2)}, u32[]{:S(2)}) collective-permute-start(bf16[1024,512]{1,0:T(8,128)(2,1)S(1)} %get-tuple-element.161.refs_0_), channel_id=1, source_target_pairs={{0,4},{1,5},{2,6},{3,7},{4,0},{5,1},{6,2},{7,3},{8,12},{9,13},{10,... | collective-permute-start | bytes 3145736 | tf_op jit(solution)/shard_map/ppermute | solution.py:587
  527.3 44.7 %collective-permute-start.65 = (f32[1,512]{1,0:T(1,128)S(1)}, f32[1,512]{1,0:T(1,128)S(1)}, u32[]{:S(2)}, u32[]{:S(2)}) collective-permute-start(f32[1,512]{1,0:T(1,128)S(1)} %bitcast.518), channel_id=1, source_target_pairs={{0,4},{1,5},{2,6},{3,7},{4,0},{5,1},{6,2},{7,3},{8,12},{9,13},{10,... | collective-permute-start | bytes 6152 | tf_op jit(solution)/shard_map/ppermute | solution.py:587
  529.1 43.0 %collective-permute-start.64 = (f32[1,512]{1,0:T(1,128)S(1)}, f32[1,512]{1,0:T(1,128)S(1)}, u32[]{:S(2)}, u32[]{:S(2)}) collective-permute-start(f32[1,512]{1,0:T(1,128)S(1)} %bitcast.519), channel_id=1, source_target_pairs={{0,1},{1,0},{2,3},{3,2},{4,5},{5,4},{6,7},{7,6},{8,9},{9,8},{10,11... | collective-permute-start | bytes 6152 | tf_op jit(solution)/shard_map/ppermute | solution.py:587
  529.1 51.3 %collective-permute-start.39 = (bf16[1024,512]{1,0:T(8,128)(2,1)S(1)}, bf16[1024,512]{1,0:T(8,128)(2,1)S(1)}, u32[]{:S(2)}, u32[]{:S(2)}) collective-permute-start(bf16[1024,512]{1,0:T(8,128)(2,1)S(1)} %get-tuple-element.161.refs_0_), channel_id=1, source_target_pairs={{0,1},{1,0},{2,3},{3,2},{4,5},{5,4},{6,7},{7,6},{8,9},{9,8},{10,11... | collective-permute-start | bytes 3145736 | tf_op jit(solution)/shard_map/ppermute | solution.py:587
  574.7 26.9 %collective-permute-start.27 = (bf16[2048,256]{1,0:T(8,128)(2,1)S(1)}, bf16[2048,256]{1,0:T(8,128)(2,1)S(1)}, u32[]{:S(2)}, u32[]{:S(2)}) collective-permute-start(bf16[2048,256]{1,0:T(8,128)(2,1)S(1)} %get-tuple-element.223), channel_id=1, source_target_pairs={{0,2},{1,3},{2,0},{3,1},{4,6},{5,7},{6,4},{7,5},{8,10},{9,11},{10,... | collective-permute-start | bytes 3145736 | tf_op jit(solution)/shard_map/ppermute | solution.py:587
  578.3 42.6 %collective-permute-start.41 = (bf16[1024,512]{1,0:T(8,128)(2,1)}, bf16[1024,512]{1,0:T(8,128)(2,1)}, u32[]{:S(2)}, u32[]{:S(2)}) collective-permute-start(bf16[1024,512]{1,0:T(8,128)(2,1)} %collective-permute-done.40.refs_2_), channel_id=1, source_target_pairs={{0,1},{1,0},{2,3},{3,2},{4,5},{5,4},{6,7},{7,6},{8,9},{9,8},{10,11... | collective-permute-start | bytes 3145736 | tf_op jit(solution)/shard_map/ppermute | solution.py:587
  685.5 30.2 %collective-permute-start.34 = (f32[1024]{0:T(1024)S(1)}, f32[1024]{0:T(1024)}, u32[]{:S(2)}, u32[]{:S(2)}) collective-permute-start(f32[1024]{0:T(1024)S(1)} %slice_reduce_fusion.1), channel_id=1, source_target_pairs={{0,1},{1,0},{2,3},{3,2},{4,5},{5,4},{6,7},{7,6},{8,9},{9,8},{10,11... | collective-permute-start | bytes 12296 | tf_op jit(solution)/shard_map/ppermute | solution.py:587
  711.7 46.2 %collective-permute-start.32 = (bf16[2,1024,512]{2,1,0:T(8,128)(2,1)}, bf16[2,1024,512]{2,1,0:T(8,128)(2,1)}, u32[]{:S(2)}, u32[]{:S(2)}) collective-permute-start(bf16[2,1024,512]{2,1,0:T(8,128)(2,1)} %matmul_add.38), channel_id=1, source_target_pairs={{0,1},{1,0},{2,3},{3,2},{4,5},{5,4},{6,7},{7,6},{8,9},{9,8},{10,11... | collective-permute-start | bytes 6291464 | tf_op jit(solution)/shard_map/ppermute | solution.py:587
  711.9 54.2 %collective-permute-start.42 = (bf16[2,1024,512]{2,1,0:T(8,128)(2,1)}, bf16[2,1024,512]{2,1,0:T(8,128)(2,1)}, u32[]{:S(2)}, u32[]{:S(2)}) collective-permute-start(bf16[2,1024,512]{2,1,0:T(8,128)(2,1)} %matmul_add.42), channel_id=1, source_target_pairs={{0,1},{1,0},{2,3},{3,2},{4,5},{5,4},{6,7},{7,6},{8,9},{9,8},{10,11... | collective-permute-start | bytes 6291464 | tf_op jit(solution)/shard_map/ppermute | solution.py:587
  765.6 33.1 %collective-permute-start.33 = (bf16[1024,512]{1,0:T(8,128)(2,1)}, bf16[1024,512]{1,0:T(8,128)(2,1)}, u32[]{:S(2)}, u32[]{:S(2)}) collective-permute-start(bf16[1024,512]{1,0:T(8,128)(2,1)} %bitcast.467), channel_id=1, source_target_pairs={{0,4},{1,5},{2,6},{3,7},{4,0},{5,1},{6,2},{7,3},{8,12},{9,13},{10,... | collective-permute-start | bytes 3145736 | tf_op jit(solution)/shard_map/ppermute | solution.py:587
  773.9 35.5 %collective-permute-start.43 = (bf16[1024,512]{1,0:T(8,128)(2,1)}, bf16[1024,512]{1,0:T(8,128)(2,1)}, u32[]{:S(2)}, u32[]{:S(2)}) collective-permute-start(bf16[1024,512]{1,0:T(8,128)(2,1)} %bitcast.468), channel_id=1, source_target_pairs={{0,4},{1,5},{2,6},{3,7},{4,0},{5,1},{6,2},{7,3},{8,12},{9,13},{10,... | collective-permute-start | bytes 3145736 | tf_op jit(solution)/shard_map/ppermute | solution.py:587
  817.9 58.1 %collective-permute-start.37 = (bf16[1024,512]{1,0:T(8,128)(2,1)S(1)}, bf16[1024,512]{1,0:T(8,128)(2,1)S(1)}, u32[]{:S(2)}, u32[]{:S(2)}) collective-permute-start(bf16[1024,512]{1,0:T(8,128)(2,1)S(1)} %get-tuple-element.306.refs_0_), channel_id=1, source_target_pairs={{0,4},{1,5},{2,6},{3,7},{4,0},{5,1},{6,2},{7,3},{8,12},{9,13},{10,... | collective-permute-start | bytes 3145736 | tf_op jit(solution)/shard_map/ppermute | solution.py:587
  819.5 60.0 %collective-permute-start.36 = (bf16[1024,512]{1,0:T(8,128)(2,1)S(1)}, bf16[1024,512]{1,0:T(8,128)(2,1)}, u32[]{:S(2)}, u32[]{:S(2)}) collective-permute-start(bf16[1024,512]{1,0:T(8,128)(2,1)S(1)} %get-tuple-element.306.refs_0_), channel_id=1, source_target_pairs={{0,1},{1,0},{2,3},{3,2},{4,5},{5,4},{6,7},{7,6},{8,9},{9,8},{10,11... | collective-permute-start | bytes 3145736 | tf_op jit(solution)/shard_map/ppermute | solution.py:587
  827.9 48.5 %collective-permute-start.47 = (bf16[1024,512]{1,0:T(8,128)(2,1)S(1)}, bf16[1024,512]{1,0:T(8,128)(2,1)S(1)}, u32[]{:S(2)}, u32[]{:S(2)}) collective-permute-start(bf16[1024,512]{1,0:T(8,128)(2,1)S(1)} %get-tuple-element.307.refs_0_), channel_id=1, source_target_pairs={{0,4},{1,5},{2,6},{3,7},{4,0},{5,1},{6,2},{7,3},{8,12},{9,13},{10,... | collective-permute-start | bytes 3145736 | tf_op jit(solution)/shard_map/ppermute | solution.py:587
  833.3 44.2 %collective-permute-start.46 = (bf16[1024,512]{1,0:T(8,128)(2,1)S(1)}, bf16[1024,512]{1,0:T(8,128)(2,1)S(1)}, u32[]{:S(2)}, u32[]{:S(2)}) collective-permute-start(bf16[1024,512]{1,0:T(8,128)(2,1)S(1)} %get-tuple-element.307.refs_0_), channel_id=1, source_target_pairs={{0,1},{1,0},{2,3},{3,2},{4,5},{5,4},{6,7},{7,6},{8,9},{9,8},{10,11... | collective-permute-start | bytes 3145736 | tf_op jit(solution)/shard_map/ppermute | solution.py:587
  834.4 33.8 %collective-permute-start.69 = (f32[4,1,49,64]{3,1,2,0:T(1,128)S(1)}, f32[4,1,49,64]{3,1,2,0:T(1,128)S(1)}, u32[]{:S(2)}, u32[]{:S(2)}) collective-permute-start(f32[4,1,49,64]{3,1,2,0:T(1,128)S(1)} %constant_dynamic-slice_fusion.9), channel_id=1, source_target_pairs={{0,4},{1,5},{2,6},{3,7},{4,0},{5,1},{6,2},{7,3},{8,12},{9,13},{10,... | collective-permute-start | bytes 150536 | tf_op jit(solution)/shard_map/ppermute | solution.py:587
  873.3 162.6 %collective-permute-start.71 = (f32[1,49,64]{2,0,1:T(1,128)}, f32[1,49,64]{2,0,1:T(1,128)}, u32[]{:S(2)}, u32[]{:S(2)}) collective-permute-start(f32[1,49,64]{2,0,1:T(1,128)} %constant_dynamic-slice_fusion.6), channel_id=1, source_target_pairs={{0,16},{8,24},{16,0},{24,8},{1,17},{9,25},{17,1},{25,9},{2,18},{10... | collective-permute-start | bytes 37640 | tf_op jit(solution)/shard_map/ppermute | solution.py:852
  972.6 64.1 %collective-permute-start.51 = (f32[2048]{0:T(1024)}, f32[2048]{0:T(1024)}, u32[]{:S(2)}, u32[]{:S(2)}) collective-permute-start(f32[2048]{0:T(1024)} %reduce_sum.138), channel_id=1, source_target_pairs={{0,1},{1,0},{2,3},{3,2},{4,5},{5,4},{6,7},{7,6},{8,9},{9,8},{10,11... | collective-permute-start | bytes 24584 | tf_op jit(solution)/shard_map/ppermute | solution.py:587
  1025.6 33.5 %collective-permute-start.53 = (bf16[2,1024,512]{2,1,0:T(8,128)(2,1)}, bf16[2,1024,512]{2,1,0:T(8,128)(2,1)}, u32[]{:S(2)}, u32[]{:S(2)}) collective-permute-start(bf16[2,1024,512]{2,1,0:T(8,128)(2,1)} %matmul_add.49), channel_id=1, source_target_pairs={{0,1},{1,0},{2,3},{3,2},{4,5},{5,4},{6,7},{7,6},{8,9},{9,8},{10,11... | collective-permute-start | bytes 6291464 | tf_op jit(solution)/shard_map/ppermute | solution.py:587
  1035.4 31.2 %collective-permute-start.49 = (bf16[2,1024,512]{2,1,0:T(8,128)(2,1)}, bf16[2,1024,512]{2,1,0:T(8,128)(2,1)}, u32[]{:S(2)}, u32[]{:S(2)}) collective-permute-start(bf16[2,1024,512]{2,1,0:T(8,128)(2,1)} %matmul_add.46), channel_id=1, source_target_pairs={{0,1},{1,0},{2,3},{3,2},{4,5},{5,4},{6,7},{7,6},{8,9},{9,8},{10,11... | collective-permute-start | bytes 6291464 | tf_op jit(solution)/shard_map/ppermute | solution.py:587
  1064.1 26.3 %collective-permute-start.54 = (bf16[1024,512]{1,0:T(8,128)(2,1)}, bf16[1024,512]{1,0:T(8,128)(2,1)S(1)}, u32[]{:S(2)}, u32[]{:S(2)}) collective-permute-start(bf16[1024,512]{1,0:T(8,128)(2,1)} %bitcast.466), channel_id=1, source_target_pairs={{0,4},{1,5},{2,6},{3,7},{4,0},{5,1},{6,2},{7,3},{8,12},{9,13},{10,... | collective-permute-start | bytes 3145736 | tf_op jit(solution)/shard_map/ppermute | solution.py:587
  1071.5 38.4 %collective-permute-start.50 = (bf16[1024,512]{1,0:T(8,128)(2,1)}, bf16[1024,512]{1,0:T(8,128)(2,1)}, u32[]{:S(2)}, u32[]{:S(2)}) collective-permute-start(bf16[1024,512]{1,0:T(8,128)(2,1)} %bitcast.469), channel_id=1, source_target_pairs={{0,4},{1,5},{2,6},{3,7},{4,0},{5,1},{6,2},{7,3},{8,12},{9,13},{10,... | collective-permute-start | bytes 3145736 | tf_op jit(solution)/shard_map/ppermute | solution.py:587
  1073.1 40.3 %collective-permute-start.63 = (f32[1,132,64]{1,2,0:T(8,128)S(1)}, f32[1,132,64]{1,2,0:T(8,128)S(1)}, u32[]{:S(2)}, u32[]{:S(2)}) collective-permute-start(f32[1,132,64]{1,2,0:T(8,128)S(1)} %constant_dynamic-slice_fusion.14), channel_id=1, source_target_pairs={{0,16},{8,24},{16,0},{24,8},{1,17},{9,25},{17,1},{25,9},{2,18},{10... | collective-permute-start | bytes 101384 | tf_op jit(solution)/shard_map/ppermute | solution.py:852
  (209 other events, 2362.7 us)
Sparse Core Ops, SparseCore 0:
  13.0 66.6 all-gather.1

commit v2 on v1

v2 whole, which is shorter than its diff:
```python
import functools

import jax
import jax.numpy as jnp
from jax import lax
from jax.experimental import pallas as pl
from jax.experimental.pallas import tpu as pltpu
from jax.sharding import PartitionSpec as P

D = 2048
HEAD = 128
FF = 5632
RANK = 16
SEGMENTS = 8
EPSILON = 1e-05
ROPE_BASE = 10000.0
MASKED = -1e30
ROW = 2
CHUNKS = 2
BQ = 256
BK = 256
HEADS_FORWARD = 2
HEADS_BACKWARD = 2
COST = 0.15
F32 = jnp.float32
BF16 = jnp.bfloat16

NN = (((1,), (0,)), ((), ()))
NT = (((1,), (1,)), ((), ()))
TN = (((0,), (0,)), ((), ()))


def dot(a, b, dims=NN):
    return lax.dot_general(a, b, dims, preferred_element_type=F32)


def params(rank):
    return pltpu.CompilerParams(
        dimension_semantics=("arbitrary",) * rank, vmem_limit_bytes=56 * 2**20
    )


def cost(flops, moved, exps=0):
    return pl.CostEstimate(
        flops=int(flops * COST), bytes_accessed=int(moved * COST), transcendentals=int(exps * COST)
    )


def bytes_of(arrays):
    return sum(a.size * a.dtype.itemsize for a in arrays)


def fixed(shape):
    rank = len(shape)
    return pl.BlockSpec(shape, lambda *_: (0,) * rank, pipeline_mode=pl.Buffered(1))


def tiles(width, step=768):
    return [(at, min(step, width - at)) for at in range(0, width, step)]


def merge_columns(perm, own, pieces, adapter_a, adapter_b, gain, first):
    count, rows, width = own.shape
    blocks = perm.shape[0] - 1
    size = rows // blocks
    local = adapter_b.shape[2]
    parts = 2 * len(pieces[0])
    deep = blocks // parts

    def body(perm_ref, own_ref, *rest):
        piece_refs = rest[:parts]
        a_ref, b_ref, gain_ref, v_ref, sq_ref = rest[parts:]
        at = perm_ref[pl.program_id(0)] // deep
        swap = perm_ref[blocks] * (parts // 2)
        place = jnp.where(at >= swap, at - swap, at + parts // 2)

        @pl.when(pl.program_id(0) == 0)
        def _():
            sq_ref[...] = jnp.zeros_like(sq_ref)

        for k in range(count):
            low = (first + k) * RANK
            product = dot(a_ref[:, low : low + RANK], b_ref[k])
            other = piece_refs[0][k].astype(F32)
            for i in range(1, parts):
                other = jnp.where(place == i, piece_refs[i][k].astype(F32), other)
            weight = jnp.concatenate([own_ref[k].astype(F32), other], axis=1)
            merged = weight + 2.0 * product
            sq_ref[k] += jnp.sum(merged * merged, axis=0, keepdims=True)
            v_ref[k] = (merged * gain_ref[...]).astype(BF16)

    return pl.pallas_call(
        body,
        out_shape=(
            jax.ShapeDtypeStruct((count, rows, local), BF16),
            jax.ShapeDtypeStruct((count, 1, local), F32),
        ),
        grid_spec=pltpu.PrefetchScalarGridSpec(
            num_scalar_prefetch=1,
            grid=(blocks,),
            in_specs=[
                pl.BlockSpec((count, size, width), lambda i, p: (0, p[i], 0)),
                *[pl.BlockSpec((count, size, width), lambda i, p: (0, p[i] % deep, 0))] * parts,
                pl.BlockSpec((size, adapter_a.shape[1]), lambda i, p: (i, 0)),
                fixed(adapter_b.shape),
                pl.BlockSpec((size, 1), lambda i, p: (i, 0)),
            ],
            out_specs=[
                pl.BlockSpec((count, size, local), lambda i, p: (0, i, 0)),
                pl.BlockSpec((count, 1, local), lambda i, p: (0, 0, 0)),
            ],
        ),
        compiler_params=params(1),
        cost_estimate=cost(4 * own.size * 64, 4 * bytes_of([own])),
        name="merge_columns",
    )(perm, own, *pieces[0], *pieces[1], adapter_a, adapter_b, gain)


def merge_rows(perm, own, pieces, adapter_a, adapter_b, gain=None):
    count, height, columns = own.shape
    blocks = perm.shape[0] - 1
    size = columns // blocks
    whole = len(pieces) == 1
    parts = len(pieces[0])
    pieces = [p.reshape(-1, columns) for group in pieces for p in group]
    tall = pieces[0].shape[0]

    def body(perm_ref, own_ref, *rest):
        piece_refs = rest[: len(pieces)]
        a_ref, b_ref, *extra = rest[len(pieces) :]
        v_ref, sq_ref = extra[-2:]
        held = [ref[...].astype(F32) for ref in piece_refs]
        if not whole:
            first = perm_ref[blocks] == 0
            low, high = held[:parts], held[parts:]
            found = [
                [jnp.where(first, a, b) for a, b in zip(low, high)],
                [jnp.where(first, b, a) for a, b in zip(low, high)],
            ]
        if gain is not None:

            @pl.when(pl.program_id(0) == 0)
            def _():
                sq_ref[...] = jnp.zeros_like(sq_ref)

        for k in range(count):
            product = dot(a_ref[k], b_ref[k])
            if whole:
                others = held
            else:
                others = [*found[0], *found[1]] if count == 1 else found[k]
            places = [(0, own_ref[k].astype(F32))]
            for i, other in enumerate(others):
                places.append((height + i * tall, other))
            down = None
            for at, weight in places:
                part = slice(at, at + weight.shape[0])
                merged = weight + 2.0 * product[part]
                square = merged * merged
                if gain is None:
                    more = jnp.sum(square, axis=0, keepdims=True)
                    down = more if down is None else down + more
                else:
                    sq_ref[k, part] += jnp.sum(square, axis=1, keepdims=True)
                    merged = merged * extra[0][...]
                v_ref[k, part] = merged.astype(BF16)
            if gain is None:
                sq_ref[k] = down

    if gain is None:
        squares = jax.ShapeDtypeStruct((count, 1, columns), F32)
        squares_spec = pl.BlockSpec((count, 1, size), lambda i, p: (0, 0, i))
        extra_specs, extra = [], []
    else:
        squares = jax.ShapeDtypeStruct((count, 2 * height, 1), F32)
        squares_spec = pl.BlockSpec((count, 2 * height, 1), lambda i, p: (0, 0, 0))
        extra_specs, extra = [pl.BlockSpec((1, size), lambda i, p: (0, i))], [gain]
    return pl.pallas_call(
        body,
        out_shape=(jax.ShapeDtypeStruct((count, 2 * height, columns), BF16), squares),
        grid_spec=pltpu.PrefetchScalarGridSpec(
            num_scalar_prefetch=1,
            grid=(blocks,),
            in_specs=[
                pl.BlockSpec((count, height, size), lambda i, p: (0, 0, p[i])),
                *[pl.BlockSpec((tall, size), lambda i, p: (0, p[i]))] * len(pieces),
                fixed(adapter_a.shape),
                pl.BlockSpec((count, RANK, size), lambda i, p: (0, 0, i)),
                *extra_specs,
            ],
            out_specs=[
                pl.BlockSpec((count, 2 * height, size), lambda i, p: (0, 0, i)),
                squares_spec,
            ],
        ),
        compiler_params=params(1),
        cost_estimate=cost(4 * own.size * 64, 4 * bytes_of([own])),
        name="merge_rows",
    )(perm, own, *pieces, adapter_a, adapter_b, *extra)


def inverse_rms(x):
    wide = x.astype(F32)
    return lax.rsqrt(jnp.sum(wide * wide, axis=1, keepdims=True) / D + EPSILON)


def project_qkv(parts, weights, low, scale, cosine, sine):
    rows, width = parts[0].shape
    local = weights.shape[2]
    bm = min(512, rows)

    def body(*refs):
        part_refs = refs[: len(parts)]
        v_ref, a_ref, s_ref, cos_ref, sin_ref, out_ref, u_ref, r_ref = refs[len(parts) :]
        x = jnp.concatenate([ref[...] for ref in part_refs], axis=1)
        r = inverse_rms(x)
        r_ref[...] = jnp.broadcast_to(r, r_ref.shape)
        u_ref[...] = (dot(x, a_ref[...]) * r).astype(BF16)
        cos, sin = cos_ref[...], sin_ref[...]
        for k in range(3):
            y = dot(x, v_ref[k]) * r * s_ref[k]
            for at in range(0, local, HEAD):
                head = y[:, at : at + HEAD]
                if k < 2:
                    head = head * cos + pltpu.roll(head, HEAD // 2, 1) * sin
                out_ref[:, k * local + at : k * local + at + HEAD] = head.astype(BF16)

    outs = (
        jax.ShapeDtypeStruct((rows, 3 * local), BF16),
        jax.ShapeDtypeStruct((rows, 128), BF16),
        jax.ShapeDtypeStruct((rows, 128), F32),
    )
    return pl.pallas_call(
        body,
        out_shape=outs,
        grid=(rows // bm,),
        in_specs=[pl.BlockSpec((bm, width), lambda i: (i, 0))] * len(parts)
        + [
            fixed(weights.shape),
            fixed(low.shape),
            fixed(scale.shape),
            pl.BlockSpec((bm, HEAD), lambda i: (i, 0)),
            pl.BlockSpec((bm, HEAD), lambda i: (i, 0)),
        ],
        out_specs=[
            pl.BlockSpec((bm, 3 * local), lambda i: (i, 0)),
            pl.BlockSpec((bm, 128), lambda i: (i, 0)),
            pl.BlockSpec((bm, 128), lambda i: (i, 0)),
        ],
        compiler_params=params(1),
        cost_estimate=cost(6 * rows * D * local, bytes_of([*parts, weights, *outs])),
        name="project_qkv",
    )(*parts, weights, low, scale, cosine, sine)


def project_hidden(parts, weights, low, scale, down_low):
    rows, width = parts[0].shape
    local = weights.shape[1]
    bm = min(512, rows)

    def body(*refs):
        part_refs = refs[: len(parts)]
        v_ref, a_ref, s_ref, d_ref, gate_ref, up_ref, hid_ref, u_ref, ud_ref, r_ref = refs[
            len(parts) :
        ]
        x = jnp.concatenate([ref[...] for ref in part_refs], axis=1)
        r = inverse_rms(x)
        r_ref[...] = jnp.broadcast_to(r, r_ref.shape)
        u_ref[...] = (dot(x, a_ref[...]) * r).astype(BF16)
        for at, size in tiles(local):
            cut = slice(at, at + size)
            gate = dot(x, v_ref[0, cut, :], NT) * r * s_ref[0, :, cut]
            up = dot(x, v_ref[1, cut, :], NT) * r * s_ref[1, :, cut]
            gate_ref[:, cut] = gate.astype(BF16)
            up_ref[:, cut] = up.astype(BF16)
            hid_ref[:, cut] = (gate * jax.nn.sigmoid(gate) * up).astype(BF16)
        ud_ref[...] = dot(hid_ref[...], d_ref[...]).astype(BF16)

    wide = jax.ShapeDtypeStruct((rows, local), BF16)
    outs = (
        wide,
        wide,
        wide,
        jax.ShapeDtypeStruct((rows, 128), BF16),
        jax.ShapeDtypeStruct((rows, 128), BF16),
        jax.ShapeDtypeStruct((rows, 128), F32),
    )
    return pl.pallas_call(
        body,
        out_shape=outs,
        grid=(rows // bm,),
        in_specs=[pl.BlockSpec((bm, width), lambda i: (i, 0))] * len(parts)
        + [fixed(weights.shape), fixed(low.shape), fixed(scale.shape), fixed(down_low.shape)],
        out_specs=[pl.BlockSpec((bm, local), lambda i: (i, 0))] * 3
        + [pl.BlockSpec((bm, 128), lambda i: (i, 0))] * 3,
        compiler_params=params(1),
        cost_estimate=cost(4 * rows * D * local, bytes_of([*parts, weights, *outs]), rows * local),
        name="project_hidden",
    )(*parts, weights, low, scale, down_low)


def hidden_backward(parts, down, down_scale, down_low, gate, up, scale):
    rows, width = parts[0].shape
    local = down.shape[0]
    bm = min(512, rows)

    def body(*refs):
        part_refs = refs[: len(parts)]
        v_ref, ds_ref, b_ref, gate_ref, up_ref, s_ref, out_ref, t_ref, in_ref, low_ref = refs[
            len(parts) :
        ]

        @pl.when(pl.program_id(0) == 0)
        def _():
            t_ref[...] = jnp.zeros_like(t_ref)

        raw = jnp.concatenate([ref[...] for ref in part_refs], axis=1).astype(F32)
        g = (raw * ds_ref[...]).astype(BF16)
        low_ref[...] = dot(g, b_ref[...], NT).astype(BF16)
        inner = jnp.zeros((bm, 1), F32)
        for at, size in tiles(local):
            cut = slice(at, at + size)
            back = dot(g, v_ref[cut, :], NT)
            y_gate = gate_ref[:, cut].astype(F32)
            y_up = up_ref[:, cut].astype(F32)
            sig = jax.nn.sigmoid(y_gate)
            act = y_gate * sig
            g_gate = back * y_up * (sig + act * (1.0 - sig))
            g_up = back * act
            dot_gate = g_gate * y_gate
            dot_up = g_up * y_up
            t_ref[0, :, cut] += jnp.sum(dot_gate, axis=0, keepdims=True)
            t_ref[1, :, cut] += jnp.sum(dot_up, axis=0, keepdims=True)
            inner += jnp.sum(dot_gate + dot_up, axis=1, keepdims=True)
            out_ref[0, :, cut] = (g_gate * s_ref[0, :, cut]).astype(BF16)
            out_ref[1, :, cut] = (g_up * s_ref[1, :, cut]).astype(BF16)
        in_ref[...] = jnp.broadcast_to(inner, in_ref.shape)

    outs = (
        jax.ShapeDtypeStruct((2, rows, local), BF16),
        jax.ShapeDtypeStruct((2, 1, local), F32),
        jax.ShapeDtypeStruct((rows, 128), F32),
        jax.ShapeDtypeStruct((rows, 128), BF16),
    )
    return pl.pallas_call(
        body,
        out_shape=outs,
        grid=(rows // bm,),
        in_specs=[pl.BlockSpec((bm, width), lambda i: (i, 0))] * len(parts)
        + [fixed(down.shape), fixed(down_scale.shape), fixed(down_low.shape)]
        + [pl.BlockSpec((bm, local), lambda i: (i, 0))] * 2
        + [fixed(scale.shape)],
        out_specs=[
            pl.BlockSpec((2, bm, local), lambda i: (0, i, 0)),
            pl.BlockSpec((2, 1, local), lambda i: (0, 0, 0)),
            pl.BlockSpec((bm, 128), lambda i: (i, 0)),
            pl.BlockSpec((bm, 128), lambda i: (i, 0)),
        ],
        compiler_params=params(1),
        cost_estimate=cost(
            2 * rows * D * local, bytes_of([*parts, down, gate, up, *outs]), rows * local
        ),
        name="hidden_backward",
    )(*parts, down, down_scale, down_low, gate, up, scale)


def matmul(left, right, dims, half, width, add=None):
    count, rows, depth = left.shape
    size = D // 2
    bm = rows if count > 1 else min(512, rows)
    split = [width, size - width] if add is not None else [size]
    split = [v for v in split if v]

    def body(left_ref, right_ref, *rest):
        outs = rest[-1 - len(split) : -1] if count > 1 else rest[-len(split) :]
        k = pl.program_id(1)
        total = dot(left_ref[...], right_ref[...], dims)
        if count > 1:
            acc_ref = rest[-1]

            @pl.when(k == 0)
            def _():
                acc_ref[...] = total

            @pl.when((k > 0) & (k < count - 1))
            def _():
                acc_ref[...] += total

        def finish():
            value = total + acc_ref[...] if count > 1 else total
            if add is not None:
                value = value + rest[0][...].astype(F32)
            at = 0
            for out, columns in zip(outs, split):
                out[...] = value[:, at : at + columns].astype(out.dtype)
                at += columns

        if count > 1:
            pl.when(k == count - 1)(finish)
        else:
            finish()

    specs = [pl.BlockSpec((None, bm, depth), lambda m, k: (k, m, 0))]
    if dims is NT:
        specs.append(pl.BlockSpec((None, size, depth), lambda m, k: (k, half, 0)))
    else:
        specs.append(pl.BlockSpec((None, depth, size), lambda m, k: (k, 0, half)))
    arrays = [left, right]
    if add is not None:
        specs.append(pl.BlockSpec((bm, size), lambda m, k: (m, 0)))
        arrays.append(add)
    kinds = [F32, BF16] if add is not None else [BF16]
    outs = [jax.ShapeDtypeStruct((rows, v), kind) for v, kind in zip(split, kinds)]
    return pl.pallas_call(
        body,
        out_shape=outs,
        grid=(rows // bm, count),
        in_specs=specs,
        out_specs=[pl.BlockSpec((bm, v), lambda m, k: (m, 0)) for v in split],
        scratch_shapes=[pltpu.VMEM((bm, size), F32)] if count > 1 else [],
        compiler_params=params(2),
        cost_estimate=cost(
            2 * count * rows * size * depth,
            bytes_of([left, *outs]) + 2 * count * size * depth,
        ),
        name="matmul_half",
    )(*arrays)


def matmul_parts(parts, right):
    rows, width = parts[0].shape
    out = jax.ShapeDtypeStruct((rows, right.shape[0]), BF16)
    bm = min(512, rows)

    def body(*refs):
        left = jnp.concatenate([ref[...] for ref in refs[: len(parts)]], axis=1)
        refs[-1][...] = dot(left, refs[-2][...], NT).astype(BF16)

    return pl.pallas_call(
        body,
        out_shape=out,
        grid=(rows // bm,),
        in_specs=[pl.BlockSpec((bm, width), lambda m: (m, 0))] * len(parts) + [fixed(right.shape)],
        out_specs=pl.BlockSpec((bm, right.shape[0]), lambda m: (m, 0)),
        compiler_params=params(1),
        cost_estimate=cost(2 * rows * D * right.shape[0], bytes_of([*parts, right, out])),
        name="matmul_parts",
    )(*parts, right)


def visible(start, query, key, last):
    return (key >= start) & ((key <= jnp.minimum(query, last)) | (key == query))


def attention_forward(table, qkv_q, keys, values, starts, offset):
    rows = qkv_q.shape[0]
    length, local = keys.shape
    heads = local // HEAD
    together = min(HEADS_FORWARD, heads)
    wide = together * HEAD
    factor = HEAD**-0.5

    def body(table_ref, q_ref, k_ref, v_ref, start_ref, out_ref, lse_ref):
        i = pl.program_id(1)
        base = offset + i * BQ
        start = start_ref[...]
        query = base + lax.broadcasted_iota(jnp.int32, (1, BQ), 1)
        last = table_ref[0] - 1
        columns = [slice(h * HEAD, (h + 1) * HEAD) for h in range(together)]
        queries = [q_ref[:, c] for c in columns]

        def step(j, carry):
            at = pl.multiple_of(j * BK, BK)
            key = at + lax.broadcasted_iota(jnp.int32, (BK, BQ), 0)
            seen = visible(start, query, key, last)
            results = []
            for c, q, (top, total, acc) in zip(columns, queries, carry):
                scores = dot(k_ref[pl.ds(at, BK), c], q, NT) * factor
                scores = jnp.where(seen, scores, MASKED)
                higher = jnp.maximum(top, jnp.max(scores, axis=0, keepdims=True))
                fade = jnp.exp(top - higher)
                weights = jnp.exp(scores - higher)
                total = total * fade + jnp.sum(weights, axis=0, keepdims=True)
                acc = acc * fade + dot(v_ref[pl.ds(at, BK), c], weights.astype(BF16), TN)
                results.append((higher, total, acc))
            return tuple(results)

        empty = (
            jnp.full((1, BQ), MASKED, F32),
            jnp.zeros((1, BQ), F32),
            jnp.zeros((HEAD, BQ), F32),
        )
        block = offset // BQ + i
        carry = lax.fori_loop(table_ref[1 + block], block + 1, step, (empty,) * together)
        for h, (top, total, acc) in enumerate(carry):
            out_ref[:, columns[h]] = jnp.transpose(acc / total).astype(BF16)
            lse_ref[h] = top + jnp.log(total)

    outs = (
        jax.ShapeDtypeStruct((rows, local), BF16),
        jax.ShapeDtypeStruct((heads, 1, rows), F32),
    )
    first = offset // BQ
    return pl.pallas_call(
        body,
        out_shape=outs,
        grid_spec=pltpu.PrefetchScalarGridSpec(
            num_scalar_prefetch=1,
            grid=(heads // together, rows // BQ),
            in_specs=[
                pl.BlockSpec((BQ, wide), lambda h, i, t: (i, h)),
                pl.BlockSpec((length, wide), lambda h, i, t: (0, h)),
                pl.BlockSpec((length, wide), lambda h, i, t: (0, h)),
                pl.BlockSpec((1, BQ), lambda h, i, t: (0, first + i)),
            ],
            out_specs=[
                pl.BlockSpec((BQ, wide), lambda h, i, t: (i, h)),
                pl.BlockSpec((together, 1, BQ), lambda h, i, t: (h, 0, i)),
            ],
        ),
        compiler_params=params(2),
        cost_estimate=cost(
            2 * rows * length * local, bytes_of([keys, values, *outs]), rows * length * heads // 2
        ),
        name="attention_forward",
    )(table, qkv_q, keys, values, starts)


def attention_backward(table, qkv, grad, attended, lse, starts, cosine, sine, scale):
    length = qkv.shape[0]
    local = grad.shape[1]
    heads = local // HEAD
    together = min(HEADS_BACKWARD, heads)
    wide = together * HEAD
    steps = heads // together
    factor = HEAD**-0.5
    blocks = length // BQ
    columns = [slice(h * HEAD, (h + 1) * HEAD) for h in range(together)]

    def body(table_ref, q_ref, k_ref, v_ref, g_ref, att_ref, lse_ref, start_ref, cos_ref, sin_ref, s_ref, out_ref, t_ref, in_ref, dk_ref, dv_ref):
        last = table_ref[0] - 1
        dk_ref[...] = jnp.zeros_like(dk_ref)
        dv_ref[...] = jnp.zeros_like(dv_ref)
        t_ref[...] = jnp.zeros_like(t_ref)

        @pl.when(pl.program_id(0) == 0)
        def _():
            in_ref[...] = jnp.zeros_like(in_ref)

        def per_query(i, nothing):
            here = pl.ds(pl.multiple_of(i * BQ, BQ), BQ)
            start = start_ref[:, here]
            query = i * BQ + lax.broadcasted_iota(jnp.int32, (1, BQ), 1)
            cos, sin = cos_ref[here, :], sin_ref[here, :]

            def back(values):
                return values * cos - pltpu.roll(values, HEAD // 2, 1) * sin

            fixed_parts = []
            for h, c in enumerate(columns):
                g = g_ref[here, c]
                pairs = g.astype(F32) * att_ref[here, c].astype(F32)
                delta = jnp.sum(jnp.transpose(pairs), axis=0, keepdims=True)
                fixed_parts.append((q_ref[here, c], g, lse_ref[h, :, here], delta))

            def step(j, carry):
                at = pl.multiple_of(j * BK, BK)
                there = pl.ds(at, BK)
                key = at + lax.broadcasted_iota(jnp.int32, (BK, BQ), 0)
                seen = visible(start, query, key, last)
                results = []
                for c, (q, g, total, delta), dq in zip(columns, fixed_parts, carry):
                    k, v = k_ref[there, c], v_ref[there, c]
                    scores = dot(k, q, NT) * factor
                    weights = jnp.exp(jnp.where(seen, scores - total, MASKED))
                    slopes = (weights * (dot(v, g, NT) - delta)).astype(BF16)
                    dv_ref[there, c] += dot(weights.astype(BF16), g)
                    dk_ref[there, c] += dot(slopes, q)
                    results.append(dq + dot(slopes, k, TN))
                return tuple(results)

            empty = (jnp.zeros((BQ, HEAD), F32),) * together
            grads = lax.fori_loop(table_ref[1 + i], i + 1, step, empty)
            for h, c in enumerate(columns):
                gy = back(grads[h] * factor)
                both = gy * back(fixed_parts[h][0].astype(F32))
                t_ref[0, :, c] += jnp.sum(both, axis=0, keepdims=True)
                in_ref[here, :] += both
                out_ref[0, here, c] = (gy * s_ref[0, :, c]).astype(BF16)
            return nothing

        lax.fori_loop(0, blocks, per_query, 0)

        def per_key(i, nothing):
            here = pl.ds(pl.multiple_of(i * BQ, BQ), BQ)
            cos, sin = cos_ref[here, :], sin_ref[here, :]

            def back(values):
                return values * cos - pltpu.roll(values, HEAD // 2, 1) * sin

            for c in columns:
                gy = back(dk_ref[here, c] * factor)
                both = gy * back(k_ref[here, c].astype(F32))
                t_ref[1, :, c] += jnp.sum(both, axis=0, keepdims=True)
                out_ref[1, here, c] = (gy * s_ref[1, :, c]).astype(BF16)
                gv = dv_ref[here, c]
                more = gv * v_ref[here, c].astype(F32)
                t_ref[2, :, c] += jnp.sum(more, axis=0, keepdims=True)
                out_ref[2, here, c] = (gv * s_ref[2, :, c]).astype(BF16)
                in_ref[here, :] += both + more
            return nothing

        lax.fori_loop(0, blocks, per_key, 0)

    outs = (
        jax.ShapeDtypeStruct((3, length, local), BF16),
        jax.ShapeDtypeStruct((3, 1, local), F32),
        jax.ShapeDtypeStruct((length, HEAD), F32),
    )
    per_head = pl.BlockSpec((length, wide), lambda h, t: (0, h))
    return pl.pallas_call(
        body,
        out_shape=outs,
        grid_spec=pltpu.PrefetchScalarGridSpec(
            num_scalar_prefetch=1,
            grid=(steps,),
            in_specs=[
                per_head,
                pl.BlockSpec((length, wide), lambda h, t: (0, steps + h)),
                pl.BlockSpec((length, wide), lambda h, t: (0, 2 * steps + h)),
                per_head,
                per_head,
                pl.BlockSpec((together, 1, length), lambda h, t: (h, 0, 0)),
                fixed(starts.shape),
                fixed(cosine.shape),
                fixed(sine.shape),
                pl.BlockSpec((3, 1, wide), lambda h, t: (0, 0, h)),
            ],
            out_specs=[
                pl.BlockSpec((3, length, wide), lambda h, t: (0, 0, h)),
                pl.BlockSpec((3, 1, wide), lambda h, t: (0, 0, h)),
                pl.BlockSpec((length, HEAD), lambda h, t: (0, 0)),
            ],
            scratch_shapes=[pltpu.VMEM((length, wide), F32), pltpu.VMEM((length, wide), F32)],
        ),
        compiler_params=params(1),
        cost_estimate=cost(
            5 * length * length * local, bytes_of([qkv, grad, *outs]), length * length * heads // 2
        ),
        name="attention_backward",
    )(table, qkv, qkv, qkv, grad, attended, lse, starts, cosine, sine, scale)


def layer(
    n_dp,
    n_mp,
    tokens,
    norm_gains,
    query_key_value_weight,
    output_weight,
    gate_up_weight,
    down_weight,
    a_in,
    a_down,
    b_dmodel,
    b_hidden,
    m_dmodel,
    m_hidden,
    segment_ids,
    valid_mask,
    cotangent,
):
    length = segment_ids.shape[1]
    block = D // n_mp
    width = 2 * block
    hidden = FF // n_mp
    n_hi = n_mp // 4
    positions = 2 * n_hi
    chunk = length // CHUNKS
    me = lax.axis_index("mp")
    row = (me // ROW) % 2
    high_masks = [4 << k for k in range(n_hi.bit_length() - 1)]
    masks = [
        (high << 2) | (side << 1) | low
        for low in range(2)
        for high in range(n_hi)
        for side in range(2)
    ]
    parity = lax.axis_index("dp") % 2
    perm = jnp.concatenate([me ^ jnp.array(masks, jnp.int32), parity.astype(jnp.int32)[None]])

    def swapped(blocks):
        for k in range(n_mp.bit_length() - 1):
            bit = (me >> k) % 2 == 1
            blocks = [jnp.where(bit, blocks[i ^ (1 << k)], b) for i, b in enumerate(blocks)]
        return blocks

    def to_relative(values):
        blocks = swapped([values[:, i * block : (i + 1) * block] for i in range(n_mp)])
        return jnp.concatenate([blocks[k] for k in masks], axis=1)

    def flip(values, mask):
        return lax.ppermute(values, "mp", [(i, i ^ mask) for i in range(n_mp)])

    def gather(values):
        far = [values]
        for mask in high_masks:
            far = far + [flip(v, mask) for v in far]
        return far + [flip(f, 1) for f in far]

    def total(values):
        for mask in [1, *high_masks]:
            values = values + flip(values, mask)
        return values

    def total_relative(values):
        lead = values.shape[:-1]
        for mask in [1, *high_masks]:
            bit = n_hi if mask == 1 else mask >> 2
            cut = (*lead, positions // (2 * bit), 2, bit * width)
            theirs = flip(values, mask).reshape(cut)
            theirs = jnp.concatenate([theirs[..., 1:2, :], theirs[..., 0:1, :]], axis=-2)
            values = (values.reshape(cut) + theirs).reshape(values.shape)
        return values

    def reduce_far(near, far):
        blocks = [near, *far]
        for mask in reversed(high_masks):
            half = len(blocks) // 2
            sent = [flip(b.astype(BF16), mask) for b in blocks[half:]]
            blocks = [a.astype(F32) + b.astype(F32) for a, b in zip(blocks[:half], sent)]
        return blocks[0]

    def tie(*values):
        return lax.optimization_barrier(values)

    def scatter_begin(left, right, dims, *early):
        [odd] = matmul(left, right, dims, 1, width)
        theirs, *early = tie(flip(odd, 1), *early)
        outs = matmul(left, right, dims, 0, width, theirs)
        return (*outs, *early)

    def scatter_end(near, far=None):
        return reduce_far(near, [far[:, k * width : (k + 1) * width] for k in range(n_hi - 1)])

    spread_order = [("mp", 1)]
    spread_order += [("mp", k) for k in range(2, n_mp.bit_length() - 1)]
    spread_order += [("dp", k) for k in range(n_dp.bit_length() - 1)]
    spread_order += [("mp", 0)]

    def spread_step(values, axis, k):
        mine, count = (me, n_mp) if axis == "mp" else (lax.axis_index("dp"), n_dp)
        theirs = lax.ppermute(values, axis, [(i, i ^ (1 << k)) for i in range(count)])
        upper = (mine >> k) % 2 == 1
        return jnp.stack([jnp.where(upper, theirs, values), jnp.where(upper, values, theirs)])

    def spread_rest(values):
        shape = values.shape[1:]
        for axis, k in spread_order[1:]:
            values = spread_step(values, axis, k)
        added = spread_order[::-1]
        wanted = [("dp", k) for k in reversed(range(n_dp.bit_length() - 1))]
        wanted += [("mp", k) for k in reversed(range(n_mp.bit_length() - 1))]
        rank = len(added)
        values = jnp.transpose(values, (*[added.index(w) for w in wanted], rank, rank + 1))
        return values.reshape(n_dp * n_mp, *shape)

    def rows_of(values, which, c):
        return lax.dynamic_slice_in_dim(values, which * length + c * chunk, chunk, 0)

    def to_row(values):
        return [
            jnp.concatenate(
                [rows_of(values, row, c), flip(rows_of(values, 1 - row, c), ROW)], axis=1
            )
            for c in range(CHUNKS)
        ]

    def fetch(values, axis, parts=1, along=1):
        size = values.shape[axis] // 2
        half = lax.dynamic_slice_in_dim(values, parity * size, size, axis)
        same = [flip(v, ROW) for v in jnp.split(half, parts, axis=along)]
        rest = [lax.ppermute(v, "dp", [(i, i ^ 1) for i in range(n_dp)]) for v in same]
        return same, rest

    def from_row(chunks):
        theirs = jnp.concatenate([flip(v[:, block:], ROW) for v in chunks])
        mine = jnp.concatenate([v[:, :block] for v in chunks])
        return jnp.where(
            row == 0,
            jnp.concatenate([mine, theirs], axis=0),
            jnp.concatenate([theirs, mine], axis=0),
        )

    def cut(values):
        return [values[c * chunk : (c + 1) * chunk] for c in range(CHUNKS)]

    thin = a_in.shape[1]
    packs = [
        jnp.concatenate(
            [
                jnp.transpose(a_in, (0, 2, 1)).reshape(6 * RANK, thin),
                jnp.pad(
                    jnp.concatenate([b_dmodel.reshape(5 * RANK, thin), m_dmodel]),
                    ((0, RANK - 5), (0, 0)),
                ),
            ],
            axis=1,
        ).astype(BF16),
        jnp.concatenate(
            [jnp.transpose(a_down), b_hidden.reshape(2 * RANK, -1), m_hidden], axis=0
        ).astype(BF16),
    ]
    packs = [spread_step(p, *spread_order[0]) for p in packs]
    stream_cut = to_row(tokens)
    packs[0], packs[1], stream_cut[-1], qkv_own = tie(
        *packs, stream_cut[-1], query_key_value_weight
    )
    packs = [spread_rest(p) for p in packs]
    x_parts = [gather(v) for v in stream_cut]
    qkv_pieces = fetch(qkv_own, 1, 2)
    qkv_pieces[0][0], cot_own, out_own = tie(qkv_pieces[0][0], cotangent, output_weight)
    cot_cut = to_row(cot_own)
    out_pieces = [[flip(out_own, ROW)]]
    cot_parts = [gather(v) for v in cot_cut]
    low_rows, others = packs[0][:, :, :thin], packs[0][:, :, thin:]
    model = jnp.concatenate([low_rows, others[:, : 5 * RANK + 5]], axis=1)
    model_rows = 11 * RANK + 5
    model = to_relative(jnp.transpose(model, (1, 0, 2)).reshape(model_rows, D))
    wide = jnp.transpose(packs[1], (1, 0, 2)).reshape(3 * RANK + 2, n_mp, hidden)
    wide = jnp.concatenate(
        [lax.dynamic_index_in_dim(wide, i, 1, False) for i in (me, me ^ ROW)], axis=1
    )

    segments = lax.dynamic_slice_in_dim(segment_ids, row, 1, 0)
    valid = lax.dynamic_slice_in_dim(valid_mask, row, 1, 0)
    starts = jnp.zeros_like(segments)
    for s in range(SEGMENTS):
        count = jnp.sum((segments == s).astype(jnp.int32))
        starts = starts + jnp.where(segments > s, count, 0)
    table = jnp.concatenate([jnp.sum(valid, axis=1), starts[0, ::BQ] // BK])
    index = jnp.arange(length, dtype=jnp.int32)[None, :]
    frequency = ROPE_BASE ** (-(jnp.arange(HEAD // 2, dtype=F32) * (2.0 / HEAD)))
    angles = (index - starts)[0].astype(F32)[:, None] * frequency
    cos, sin = jnp.cos(angles), jnp.sin(angles)
    cosine = jnp.concatenate([cos, cos], axis=1)
    sine = jnp.concatenate([-sin, sin], axis=1)

    low_a = jnp.transpose(model[: 6 * RANK])
    model_b = [model[(6 + k) * RANK : (7 + k) * RANK] for k in range(5)]
    model_m = model[11 * RANK :].astype(F32)
    down_a = jnp.transpose(wide[:RANK])
    hidden_b = wide[RANK : 3 * RANK].reshape(2, RANK, 2 * hidden)
    hidden_m = wide[3 * RANK :].astype(F32)
    gains = to_relative(norm_gains)
    gain_columns = [gains[k].reshape(D, 1) for k in range(2)]
    lane = ((0, 0), (0, 128 - 6 * RANK))
    low_in = [jnp.pad((low_a.astype(F32) * g).astype(BF16), lane) for g in gain_columns]
    qkv_b = jnp.stack([b[:, :width] for b in model_b[:3]])
    qkv_v, qkv_sq = merge_columns(
        perm, query_key_value_weight, qkv_pieces, low_a, qkv_b, gain_columns[0], 0
    )
    gate_up_rows = jnp.transpose(gate_up_weight, (0, 2, 1))
    qkv_v, gate_up_own = tie(qkv_v, gate_up_rows)
    gate_up_pieces = fetch(gate_up_own, 0, 2)
    qkv_m = model_m[:3, :width].reshape(3, 1, width)
    qkv_scale = qkv_m * lax.rsqrt(qkv_sq)
    out_a = low_a[:width, 3 * RANK : 4 * RANK]
    out_v, out_sq = merge_rows(
        perm, output_weight[None], out_pieces, out_a[None], model_b[3][None]
    )
    qkv, qkv_u, r1, attended, lse = [], [], [], [], []
    keys, values = [], []
    cos_cut, sin_cut = cut(cosine), cut(sine)
    for c in range(CHUNKS):
        o, u, r = project_qkv(x_parts[c], qkv_v, low_in[0], qkv_scale, cos_cut[c], sin_cut[c])
        qkv.append(o)
        qkv_u.append(u)
        r1.append(r)
        keys.append(o[:, width : 2 * width])
        values.append(o[:, 2 * width :])
        query, cot_parts[c] = tie(o, cot_parts[c])
        att, l = attention_forward(
            table, query, jnp.concatenate(keys), jnp.concatenate(values), starts, c * chunk
        )
        attended.append(att)
        lse.append(l)
        if c == 0:
            qkv[0], down_own = tie(qkv[0], down_weight)
            down_pieces = fetch(down_own, 0)
    gu_v, gu_sq = merge_rows(
        perm,
        gate_up_rows,
        gate_up_pieces,
        jnp.transpose(hidden_b, (0, 2, 1)),
        model[4 * RANK : 6 * RANK].reshape(2, RANK, D),
        gains[1:2],
    )
    gu_sq = gu_sq.reshape(2, 1, 2 * hidden)
    gu_m = hidden_m.reshape(2, 1, 2 * hidden)
    gu_scale = gu_m * lax.rsqrt(gu_sq)
    down_v, down_sq = merge_rows(
        perm, down_weight[None], down_pieces, down_a[None], model_b[4][None]
    )
    out_sq = total_relative(out_sq[0])
    row_sq = jnp.concatenate([out_sq, total_relative(down_sq[0])], axis=0)
    row_m = model_m[3:5]
    out_scale = row_m[0:1] * lax.rsqrt(out_sq)
    down_scale = row_m[1:2] * lax.rsqrt(row_sq[1:2])
    out_rows, down_rows = out_v[0], down_v[0]

    middle, out_y, h_parts = [], [], []
    for c in range(CHUNKS):
        outs = scatter_begin(attended[c][None], out_v, NN, out_scale)
        out_scale = outs[-1]
        y = scatter_end(*outs[:-1]) * out_scale[:, :width]
        out_y.append(y)
        h = stream_cut[c].astype(F32) + y
        middle.append(h)
        h_parts.append(gather(h.astype(BF16)))
    hid, gu_u, down_u, r2 = [], [], [], []
    g_hidden, gu_t, down_gu = [], [], []
    grad_middle, grad_out_parts = [], []
    down_a_wide = jnp.pad(down_a, ((0, 0), (0, 128 - RANK)))
    down_b_wide = jnp.pad(model_b[4], ((0, 128 - RANK), (0, 0)))
    begun = []
    for c in range(CHUNKS):
        gate, up, h, ug, ud, r = project_hidden(
            h_parts[c], gu_v, low_in[1], gu_scale, down_a_wide
        )
        g, t, inner, low = hidden_backward(
            cot_parts[c], down_rows, down_scale, down_b_wide, gate, up, gu_scale
        )
        outs = scatter_begin(g, gu_v, NN, total(inner[:, 0]))
        if c + 1 < CHUNKS:
            h_parts[c + 1][0], near = tie(h_parts[c + 1][0], outs[0])
            outs = (near, *outs[1:])
        begun.append(outs)
        bags = (hid, gu_u, down_u, r2, g_hidden, gu_t, down_gu)
        for bag, value in zip(bags, (h, ug, ud, r, g, t, low)):
            bag.append(value)
    for c in range(CHUNKS):
        *outs, sums = begun[c]
        r = r2[c][:, :1]
        g = cot_cut[c].astype(F32) + r * scatter_end(*outs) - middle[c] * (r * r * (sums / D)[:, None])
        grad_middle.append(g)
        grad_out_parts.append(gather((g * out_scale[:, :width]).astype(BF16)))
    hid, g_hidden, _ = tie(hid, g_hidden, begun[-1][0])
    down_begun = [scatter_begin(hid[c][None], down_v, NN) for c in range(CHUNKS)]
    down_begun, grad_out_parts = tie(down_begun, grad_out_parts)
    grad_att = [matmul_parts(grad_out_parts[c], out_rows) for c in range(CHUNKS)]
    att_all = jnp.concatenate(attended)
    g_qkv, qkv_t, inner1 = attention_backward(
        table,
        jnp.concatenate(qkv),
        jnp.concatenate(grad_att),
        att_all,
        jnp.concatenate(lse, axis=2),
        starts,
        cosine,
        sine,
        qkv_scale,
    )
    down_y = [scatter_end(*outs) * down_scale[:, :width] for outs in down_begun]
    activations = [(middle[c] + down_y[c]).astype(BF16) for c in range(CHUNKS)]
    down_t = sum(jnp.sum(cot_cut[c].astype(F32) * down_y[c], axis=0) for c in range(CHUNKS))
    out_t = sum(jnp.sum(grad_middle[c] * out_y[c], axis=0) for c in range(CHUNKS))
    sums1 = total(jnp.sum(inner1, axis=1))
    begun = []
    for c in range(CHUNKS):
        outs = scatter_begin(g_qkv[:, c * chunk : (c + 1) * chunk], qkv_v, NT, sums1)
        sums1 = outs[-1]
        begun.append(outs[:-1])
    input_grad = []
    for c in range(CHUNKS):
        r = r1[c][:, :1]
        s = cut(sums1)[c][:, None]
        g = grad_middle[c] + r * scatter_end(*begun[c]) - stream_cut[c].astype(F32) * (r * r * (s / D))
        input_grad.append(g.astype(BF16))
    g_qkv, _ = tie(g_qkv, begun[-1][0])

    def over_tokens(left, right):
        return sum(dot(a, b, TN) for a, b in zip(left, right))

    def spread(lefts, parts):
        return jnp.concatenate(
            [over_tokens(lefts, [p[k] for p in parts]) for k in range(positions)], axis=1
        )

    def small(values):
        return values.astype(BF16)

    def halve(values, mask, axis):
        kept, sent = jnp.split(values, 2, axis=axis)
        return kept + flip(sent, mask)

    def to_block(values):
        values = halve(values, 1, 1)
        for mask in reversed(high_masks):
            values = halve(values, mask, 1)
        return values

    def to_owner(*arrays):
        mine = lax.axis_index("dp")
        here = [(d * n_mp + m, m * n_dp + d) for d in range(n_dp) for m in range(n_mp)]
        arrays = [halve(v, ROW, 1) for v in arrays]
        pieces = []
        for v in arrays:
            rows, size = v.shape
            pieces.append(jnp.transpose(v.reshape(rows, n_dp, size // n_dp), (1, 0, 2)))
        mask = n_dp // 2
        while mask:
            upper = (mine // mask) % 2 == 1
            for i, v in enumerate(pieces):
                low, high = v[:mask], v[mask:]
                sent = jnp.where(upper, low, high)
                sent = lax.ppermute(sent, "dp", [(i, i ^ mask) for i in range(n_dp)])
                pieces[i] = jnp.where(upper, high, low) + sent
            mask //= 2
        return [lax.ppermute(v[0], ("dp", "mp"), here) for v in pieces]

    gu_t = sum(gu_t)
    gu_coef = gu_t / gu_sq
    row_coef = jnp.concatenate(gather(jnp.stack([out_t, down_t])), axis=1) / row_sq
    out_coef, down_coef = row_coef[0:1], row_coef[1:2]
    gu_gu = []
    for c in range(CHUNKS):
        low = jnp.concatenate(
            [
                dot(g_hidden[c][0], hidden_b[0], NT),
                dot(g_hidden[c][1], hidden_b[1], NT),
            ],
            axis=1,
        )
        gu_gu.append(small(low * r2[c][:, :1]))
    gu_ga = 2.0 * gains[1:2] * spread(gu_gu, h_parts)
    gu_na = jnp.concatenate(
        [dot(small(hidden_b[k] * gu_coef[k]), gu_v[k]) for k in range(2)], axis=0
    )
    gu_ga = gu_ga - 2.0 / gains[1:2] * gu_na
    low_back = [small(model[: 6 * RANK].astype(F32) / gains[k : k + 1]) for k in range(2)]
    gu_gb = []
    for k in range(2):
        at = (4 + k) * RANK
        first = over_tokens([u[:, at : at + RANK] for u in gu_u], [g[k] for g in g_hidden])
        second = dot(low_back[1][at : at + RANK], gu_v[k], NT) * gu_coef[k]
        gu_gb.append(2.0 * (first - second))
    down_ga = over_tokens(down_gu, hid)[:RANK] - dot(
        small(model_b[4] * down_coef), down_rows, NT
    )
    down_gb = spread(down_u, cot_parts)[:RANK] * down_scale - dot(down_a, down_rows, TN) * down_coef
    qkv_coef = qkv_t / qkv_sq
    low = jnp.concatenate([dot(g_qkv[k], qkv_b[k], NT) for k in range(3)], axis=1)
    r1_all = jnp.concatenate(r1)[:, :1]
    qkv_gu = cut(small(low * r1_all))
    qkv_ga = 2.0 * gains[0:1] * spread(qkv_gu, x_parts)
    qkv_na = jnp.concatenate(
        [dot(small(qkv_b[k] * qkv_coef[k]), qkv_v[k], NT) for k in range(3)], axis=0
    )
    qkv_ga = qkv_ga - 2.0 / gains[0:1] * qkv_na
    u_all = jnp.concatenate(qkv_u)
    qkv_gb = []
    for k in range(3):
        at = k * RANK
        first = dot(u_all[:, at : at + RANK], g_qkv[k], TN)
        second = dot(low_back[0][at : at + RANK], qkv_v[k]) * qkv_coef[k]
        qkv_gb.append(2.0 * (first - second))
    out_gu, out_u = [], []
    for c in range(CHUNKS):
        out_gu.append(
            small(
                sum(
                    dot(grad_out_parts[c][p], model_b[3][:, p * width : (p + 1) * width], NT)
                    for p in range(positions)
                )
            )
        )
        out_u.append(small(dot(attended[c], out_a)))
    out_ga = over_tokens(out_gu, attended) - dot(small(model_b[3] * out_coef), out_rows, NT)
    out_gb = spread(out_u, grad_out_parts) - dot(out_a, out_rows, TN) * out_coef
    both = to_block(jnp.concatenate([qkv_ga, 2.0 * out_gb, gu_ga, 2.0 * down_gb]))
    model_grads, wide_grads = to_owner(
        jnp.concatenate(
            [
                both,
                2.0 * out_ga,
                *qkv_gb,
                (qkv_t / qkv_m).reshape(3, width),
                (out_t / row_m[0, :width])[None],
                (down_t / row_m[1, :width])[None],
            ]
        ),
        jnp.concatenate([2.0 * down_ga, *gu_gb, (gu_t / gu_m).reshape(2, 2 * hidden)]),
    )

    def stacked(values, count):
        return values.reshape(count, RANK, values.shape[1])

    def ranks(first, count):
        return stacked(model_grads[first * RANK : (first + count) * RANK], count)

    return (
        from_row(activations),
        from_row(input_grad),
        jnp.transpose(jnp.concatenate([ranks(0, 3), ranks(7, 1), ranks(4, 2)]), (0, 2, 1)),
        jnp.transpose(wide_grads[:RANK]),
        jnp.concatenate([ranks(8, 3), ranks(3, 1), ranks(6, 1)]),
        stacked(wide_grads[RANK : 3 * RANK], 2),
        model_grads[11 * RANK :],
        wide_grads[3 * RANK :],
    )


def solution(mesh):
    in_specs = (
        P("dp", "mp"),
        P(),
        P(None, None, "mp"),
        P("mp", None),
        P(None, None, "mp"),
        P("mp", None),
        P(None, ("dp", "mp"), None),
        P(("dp", "mp"), None),
        P(None, None, ("dp", "mp")),
        P(None, None, ("dp", "mp")),
        P(None, ("dp", "mp")),
        P(None, ("dp", "mp")),
        P("dp", None),
        P("dp", None),
        P("dp", "mp"),
    )
    out_specs = (
        P("dp", "mp"),
        P("dp", "mp"),
        P(None, ("dp", "mp"), None),
        P(("dp", "mp"), None),
        P(None, None, ("dp", "mp")),
        P(None, None, ("dp", "mp")),
        P(None, ("dp", "mp")),
        P(None, ("dp", "mp")),
    )
    local = functools.partial(layer, mesh.shape["dp"], mesh.shape["mp"])
    return jax.shard_map(local, mesh=mesh, in_specs=in_specs, out_specs=out_specs, check_vma=False)
```

time: 1160 us -> 1040 us (0.90)
  waiting for transfers between devices: 344 us -> 275 us
  local copies, waits for them, and re-layouts: 127 us -> 72.1 us
  Pallas kernels: 401 us -> 380 us
  matrix products: 90.5 us -> 111 us
  between operations: 17.1 us -> 4.11 us
    ppermute x71, waiting for transfers between devices: 339 us -> 172 us  [flip(): return lax.ppermute(values, 'mp', [(i, i ^ mask) for i in range(n_mp)])]
    ppermute x6 -> x21, waiting for transfers between devices: 4.96 us -> 103 us  [the longest x5 47.3 us: fetch(): lax.ppermute(v, 'dp', [(i, i ^ 1) for i in range(n_dp)])]
    unnamed x378 -> x434, local copies, waits for them, and re-layouts: 39.6 us -> 13.4 us
    dot_general x72, matrix products: 90.5 us -> 111 us  [dot(): return lax.dot_general(a, b, dims, preferred_element_type=F32)]
    dynamic_update_slice x6 -> x0, local copies, waits for them, and re-layouts: 15.8 us -> none  [the longest x3 7.91 us: to_places(): lax.dynamic_update_slice_in_dim(holder, values[None, :, half:], me ^ ROW, 0)]
    pallas_call x2 -> x1, Pallas kernels: 24.5 us -> 11.2 us  [merge_columns(): pl.pallas_call(body, out_shape=(jax.ShapeDtypeStruct((count, rows, local)...]
    pallas_call x28 -> x21, Pallas kernels: 180 us -> 171 us  [the longest x16 127 us: matmul(): pl.pallas_call(body, out_shape=outs, grid=(rows // bm, count), in_specs=s...]
  transfers between devices with their start and end apart: 78 -> 92, of which waited for: 30 -> 31; matrix products, arithmetic and copies ran while one was open for 22% -> 22% of each run, Pallas kernels for 31% -> 29%
where the time goes in v2:
time: 1040 us; the launch traced here: 1020 us
  Pallas kernels  380 us (37%)
  waiting for transfers between devices  275 us (26%)
  matrix products  111 us (11%)
  other arithmetic  102 us (10%)
  starting transfers between devices  76.7 us (7%)
  local copies, waits for them, and re-layouts  72.1 us (7%)
    ppermute x71, waiting for transfers between devices, flip(): return lax.ppermute(values, 'mp', [(i, i ^ mask) for i in range(n_mp)])  172 us
    pallas_call x16, Pallas kernels, matmul(): pl.pallas_call(body, out_shape=outs, grid=(rows // bm, count), in_specs=s...  127 us
    dot_general x72, matrix products, dot(): return lax.dot_general(a, b, dims, preferred_element_type=F32)  111 us
    ppermute x71, starting transfers between devices, flip(): return lax.ppermute(values, 'mp', [(i, i ^ mask) for i in range(n_mp)])  56.6 us
    pallas_call x1, Pallas kernels, attention_backward(): pl.pallas_call(body, out_shape=outs, grid_spec=pltpu.PrefetchScalarGridSp...  52.1 us
    ppermute x5, waiting for transfers between devices, fetch(): lax.ppermute(v, 'dp', [(i, i ^ 1) for i in range(n_dp)])  47.3 us
    pallas_call x2, Pallas kernels, project_hidden(): pl.pallas_call(body, out_shape=outs, grid=(rows // bm,), in_specs=[pl.Blo...  46.2 us
    ppermute x10, waiting for transfers between devices, spread_step(): theirs = lax.ppermute(values, axis, [(i, i ^ 1 << k) for i in range(count)])  44.3 us
  transfers between devices with their start and end apart: 92, of which 31 were waited for; matrix products, arithmetic and copies ran while one was open for 22% of the time, Pallas kernels for 29%

profile of v2, /device:TPU:0, one launch (start us, length us, event | category | flops | bytes accessed | tf_op | source)
XLA Modules:
  0.0 1022.3 jit_solution(11922869114796725422)
XLA Ops:
  14.0 5.3 subtract_convert_fusion
  42.2 18.4 %collective-permute-done.31 = bf16[2,50,176]{2,1,0:T(8,128)(2,1)S(1)} collective-permute-done((bf16[2,50,176]{2,1,0:T(8,128)(2,1)S(1)}, bf16[2,50,176]{2,1,0:T(8,128)(2,1)S(1)}, u32[]{:S(2)}, u32[]{:S(2)}) %collective-permute-start.31) | collective-permute-done | bytes 35232 | tf_op jit(solution)/shard_map/ppermute | solution.py:753
  74.7 8.2 collective-permute-done.33
  83.1 10.7 %collective-permute-done.13 = bf16[2,2,2,96,128]{4,3,2,1,0:T(8,128)(2,1)S(1)} collective-permute-done((bf16[2,2,2,96,128]{4,3,2,1,0:T(8,128)(2,1)S(1)}, bf16[2,2,2,96,128]{4,3,2,1,0:T(8,128)(2,1)S(1)}, u32[]{:S(2)}, u32[]{:S(2)}) %collective-permute-start.13) | collective-permute-done | bytes 196640 | tf_op jit(solution)/shard_map/ppermute | solution.py:753
  117.3 6.2 collective-permute-done.7.rest_0_
  123.5 13.7 %collective-permute-done.10.rest_3_ = bf16[3,512,256]{2,1,0:T(8,128)(2,1)} collective-permute-done((bf16[3,512,256]{2,1,0:T(8,128)(2,1)}, bf16[3,512,256]{2,1,0:T(8,128)(2,1)}, u32[]{:S(2)}, u32[]{:S(2)}) %collective-permute-start.10) | collective-permute-done | bytes 786464 | tf_op jit(solution)/shard_map/ppermute | solution.py:783
  145.6 7.7 collective-permute-done.9.rest_2_
  154.8 11.2 %merge_columns.1 = (bf16[3,2048,512]{2,1,0:T(8,128)(2,1)}, f32[3,1,512]{2,1,0:T(1,128)}) custom-call(s32[9]{0:T(128)} %pad_add_fusion.1.perm_ref, bf16[3,2048,256]{2,1,0:T(8,128)(2,1)} %own_ref.1, bf16[3,512,256]{2,1,0:T(8,128)(2,1)} %collective-permute-done.7.rest_0_, bf16[3,512,256]{2,1,0:T(8,128)(2,1)} %collective-permute-done.8.rest_1_, ...), custom_call_target="tpu_custom_call" | custom-call | flops 60397976 | bytes 1887436 | tf_op jit(solution)/shard_map/merge_columns/pallas_call | solution.py:92
  168.4 13.5 %project_qkv.2 = (bf16[1024,1536]{1,0:T(8,128)(2,1)}, bf16[1024,128]{1,0:T(8,128)(2,1)}, f32[1024,128]{1,0:T(8,128)}) custom-call(bf16[1024,512]{1,0:T(8,128)(2,1)} %pad_maximum_fusion.6.refs_0_, bf16[1024,512]{1,0:T(8,128)(2,1)} %collective-permute-done.1.refs_1_, bf16[1024,512]{1,0:T(8,128)(2,1)} %copy-done.62, ...), custom_call_target="tpu_custom_call" | custom-call | flops 966367616 | bytes 2162688 | tf_op jit(solution)/shard_map/project_qkv/pallas_call | solution.py:233
  187.3 7.4 merge_rows.3
  203.4 30.2 %collective-permute-done.22 = f32[1,2048]{1,0:T(1,128)S(1)} collective-permute-done((f32[1,2048]{1,0:T(1,128)S(1)}, f32[1,2048]{1,0:T(1,128)S(1)}, u32[]{:S(2)}, u32[]{:S(2)}) %collective-permute-start.22) | collective-permute-done | bytes 8224 | tf_op jit(solution)/shard_map/ppermute | solution.py:703
  237.3 13.4 %project_qkv.3 = (bf16[1024,1536]{1,0:T(8,128)(2,1)}, bf16[1024,128]{1,0:T(8,128)(2,1)}, f32[1024,128]{1,0:T(8,128)}) custom-call(bf16[1024,512]{1,0:T(8,128)(2,1)} %copy-done.5, bf16[1024,512]{1,0:T(8,128)(2,1)} %collective-permute-done.35.refs_1_, bf16[1024,512]{1,0:T(8,128)(2,1)} %collective-permute-done.36.refs_2_, ...), custom_call_target="tpu_custom_call" | custom-call | flops 966367616 | bytes 2162688 | tf_op jit(solution)/shard_map/project_qkv/pallas_call | solution.py:233
  252.9 14.5 %attention_forward.2 = (bf16[1024,512]{1,0:T(8,128)(2,1)}, f32[4,1,1024]{2,1,0:T(1,128)}) custom-call(s32[9]{0:T(128)} %pad_add_fusion.table_ref, bf16[1024,1536]{1,0:T(8,128)(2,1)} %get-tuple-element.190.q_ref, bf16[1024,512]{1,0:T(8,128)(2,1)} %get-tuple-element.323.k_ref, bf16[1024,512]{1,0:T(8,128)(2,1)} %get-tuple-element.322.v_ref, s32[1,2048]{1,0:T(1,128)} %copy-done.152), custom_call_target="tpu_custom_call" | custom-call | flops 161061280 | bytes 474316 | tf_op jit(solution)/shard_map/attention_forward/pallas_call | solution.py:504
  276.0 25.2 %attention_forward.3 = (bf16[1024,512]{1,0:T(8,128)(2,1)}, f32[4,1,1024]{2,1,0:T(1,128)}) custom-call(s32[9]{0:T(128)} %pad_add_fusion.table_ref, bf16[1024,1536]{1,0:T(8,128)(2,1)} %get-tuple-element.141.q_ref, bf16[2048,512]{1,0:T(8,128)(2,1)} %pad_maximum_fusion.1.k_ref, bf16[2048,512]{1,0:T(8,128)(2,1)} %pad_maximum_fusion.2.v_ref, s32[1,2048]{1,0:T(1,128)} %copy-done.152), custom_call_target="tpu_custom_call" | custom-call | flops 322122560 | bytes 788889 | tf_op jit(solution)/shard_map/attention_forward/pallas_call | solution.py:504
  301.2 9.7 merge_rows.5
  332.7 19.4 %collective-permute-done.23 = bf16[1024,512]{1,0:T(8,128)(2,1)S(1)} collective-permute-done((bf16[1024,512]{1,0:T(8,128)(2,1)}, bf16[1024,512]{1,0:T(8,128)(2,1)S(1)}, u32[]{:S(2)}, u32[]{:S(2)}) %collective-permute-start.23) | collective-permute-done | bytes 1048608 | tf_op jit(solution)/shard_map/ppermute | solution.py:703
  368.3 25.9 %collective-permute-done.29 = bf16[1,352,2048]{2,1,0:T(8,128)(2,1)} collective-permute-done((bf16[1,352,2048]{2,1,0:T(8,128)(2,1)}, bf16[1,352,2048]{2,1,0:T(8,128)(2,1)}, u32[]{:S(2)}, u32[]{:S(2)}) %collective-permute-start.29) | collective-permute-done | bytes 1441824 | tf_op jit(solution)/shard_map/ppermute | solution.py:783
  394.2 15.1 %merge_rows.4 = (bf16[2,1408,2048]{2,1,0:T(8,128)(2,1)}, f32[2,1408,1]{2,1,0:T(8,128)}) custom-call(s32[9]{0:T(128)} %pad_add_fusion.1.perm_ref, bf16[2,704,2048]{2,1,0:T(8,128)(2,1)} %bitcast.401, bf16[352,2048]{1,0:T(8,128)(2,1)} %bitcast.39.rest_0_, bf16[352,2048]{1,0:T(8,128)(2,1)} %bitcast.40.rest_1_, bf16[352,2048]{1,0:T(8,128)(2,1)} %bitcast.41.rest_2_, ...), custom_call_target="tpu_custom_call" | custom-call | flops 110729624 | bytes 3460300 | tf_op jit(solution)/shard_map/merge_rows/pallas_call | solution.py:178
  419.6 23.0 %project_hidden.2 = (bf16[1024,1408]{1,0:T(8,128)(2,1)}, bf16[1024,1408]{1,0:T(8,128)(2,1)}, bf16[1024,1408]{1,0:T(8,128)(2,1)}, bf16[1024,128]{1,0:T(8,128)(2,1...) custom-call(bf16[1024,512]{1,0:T(8,128)(2,1)} %copy-done.36, bf16[1024,512]{1,0:T(8,128)(2,1)} %collective-permute-done.24.refs_1_, ...), custom_call_target="tpu_custom_call" | custom-call | flops 1771673984 | bytes 3814195 | tf_op jit(solution)/shard_map/project_hidden/pallas_call | solution.py:288
  442.7 16.5 %hidden_backward.2 = (bf16[2,1024,1408]{2,1,0:T(8,128)(2,1)}, f32[2,1,1408]{2,1,0:T(1,128)}, f32[1024,128]{1,0:T(8,128)}, bf16[1024,128]{1,0:T(8,128)(2,1)}) custom-call(bf16[1024,512]{1,0:T(8,128)(2,1)} %pad_maximum_fusion.9.refs_0_, bf16[1024,512]{1,0:T(8,128)(2,1)} %collective-permute-done.16.refs_1_, bf16[1024,512]{1,0:T(8,128)(2,1)} %collective-permute-done.17.refs_2_, ...), custom_call_target="tpu_custom_call" | custom-call | flops 885836992 | bytes 3344025 | tf_op jit(solution)/shard_map/hidden_backward/pallas_call | solution.py:345
  459.2 12.1 %matmul_half.20 = bf16[1024,1024]{1,0:T(8,128)(2,1)} custom-call(bf16[2,1024,1408]{2,1,0:T(8,128)(2,1)} %get-tuple-element.214.left_ref, bf16[2,1408,2048]{2,1,0:T(8,128)(2,1)} %get-tuple-element.136.refs_4_.right_ref), custom_call_target="tpu_custom_call" | custom-call | flops 885836992 | bytes 2044723 | tf_op jit(solution)/shard_map/matmul_half/pallas_call | solution.py:414
  489.4 12.4 %matmul_half.21 = (f32[1024,512]{1,0:T(8,128)}, bf16[1024,512]{1,0:T(8,128)(2,1)}) custom-call(bf16[2,1024,1408]{2,1,0:T(8,128)(2,1)} %get-tuple-element.214.left_ref, bf16[2,1408,2048]{2,1,0:T(8,128)(2,1)} %get-tuple-element.136.refs_4_.right_ref, bf16[1024,1024]{1,0:T(8,128)(2,1)} %collective-permute-done.48.rest_0_), custom_call_target="tpu_custom_call" | custom-call | flops 885836992 | bytes 2202009 | tf_op jit(solution)/shard_map/matmul_half/pallas_call | solution.py:414
  505.4 23.2 %project_hidden.3 = (bf16[1024,1408]{1,0:T(8,128)(2,1)}, bf16[1024,1408]{1,0:T(8,128)(2,1)}, bf16[1024,1408]{1,0:T(8,128)(2,1)}, bf16[1024,128]{1,0:T(8,128)(2,1...) custom-call(bf16[1024,512]{1,0:T(8,128)(2,1)} %copy-done.37, bf16[1024,512]{1,0:T(8,128)(2,1)} %collective-permute-done.51.refs_1_, ...), custom_call_target="tpu_custom_call" | custom-call | flops 1771673984 | bytes 3814195 | tf_op jit(solution)/shard_map/project_hidden/pallas_call | solution.py:288
  539.0 16.8 %hidden_backward.3 = (bf16[2,1024,1408]{2,1,0:T(8,128)(2,1)}, f32[2,1,1408]{2,1,0:T(1,128)}, f32[1024,128]{1,0:T(8,128)}, bf16[1024,128]{1,0:T(8,128)(2,1)}) custom-call(bf16[1024,512]{1,0:T(8,128)(2,1)} %pad_maximum_fusion.10.refs_0_, bf16[1024,512]{1,0:T(8,128)(2,1)} %collective-permute-done.39.refs_1_, bf16[1024,512]{1,0:T(8,128)(2,1)} %copy-done.64, ...), custom_call_target="tpu_custom_call" | custom-call | flops 885836992 | bytes 3344025 | tf_op jit(solution)/shard_map/hidden_backward/pallas_call | solution.py:345
  563.1 11.5 %matmul_half.22 = bf16[1024,1024]{1,0:T(8,128)(2,1)} custom-call(bf16[2,1024,1408]{2,1,0:T(8,128)(2,1)} %get-tuple-element.215.left_ref, bf16[2,1408,2048]{2,1,0:T(8,128)(2,1)} %get-tuple-element.136.refs_4_.right_ref), custom_call_target="tpu_custom_call" | custom-call | flops 885836992 | bytes 2044723 | tf_op jit(solution)/shard_map/matmul_half/pallas_call | solution.py:414
  602.2 13.6 %matmul_half.23 = (f32[1024,512]{1,0:T(8,128)}, bf16[1024,512]{1,0:T(8,128)(2,1)}) custom-call(bf16[2,1024,1408]{2,1,0:T(8,128)(2,1)} %get-tuple-element.215.left_ref, bf16[2,1408,2048]{2,1,0:T(8,128)(2,1)} %get-tuple-element.136.refs_4_.right_ref, bf16[1024,1024]{1,0:T(8,128)(2,1)} %collective-permute-done.54.rest_0_), custom_call_target="tpu_custom_call" | custom-call | flops 885836992 | bytes 2202009 | tf_op jit(solution)/shard_map/matmul_half/pallas_call | solution.py:414
  628.6 7.0 matmul_half.26
  635.6 7.0 matmul_half.24
  665.1 17.3 %collective-permute-done.64.refs_1_ = bf16[1024,512]{1,0:T(8,128)(2,1)S(1)} collective-permute-done((bf16[1024,512]{1,0:T(8,128)(2,1)S(1)}, bf16[1024,512]{1,0:T(8,128)(2,1)S(1)}, u32[]{:S(2)}, u32[]{:S(2)}) %collective-permute-start.64) | collective-permute-done | bytes 1048608 | tf_op jit(solution)/shard_map/ppermute | solution.py:703
  682.4 21.5 %collective-permute-done.60.refs_1_ = bf16[1024,512]{1,0:T(8,128)(2,1)S(1)} collective-permute-done((bf16[1024,512]{1,0:T(8,128)(2,1)S(1)}, bf16[1024,512]{1,0:T(8,128)(2,1)S(1)}, u32[]{:S(2)}, u32[]{:S(2)}) %collective-permute-start.60) | collective-permute-done | bytes 1048608 | tf_op jit(solution)/shard_map/ppermute | solution.py:703
  708.1 7.0 matmul_half.25
  715.2 7.1 matmul_half.27
  727.8 5.8 matmul_parts.3
  733.6 5.9 matmul_parts.2
  742.3 52.1 %attention_backward.1 = (bf16[3,2048,512]{2,1,0:T(8,128)(2,1)}, f32[3,1,512]{2,1,0:T(1,128)}, f32[2048,128]{1,0:T(8,128)}) custom-call(s32[9]{0:T(128)} %pad_add_fusion.table_ref, bf16[2048,1536]{1,0:T(8,128)(2,1)} %pad_maximum_fusion.q_ref.k_ref.v_ref, bf16[2048,1536]{1,0:T(8,128)(2,1)} %pad_maximum_fusion.q_ref.k_ref.v_ref, ...), custom_call_target="tpu_custom_call" | custom-call | flops 1610612736 | bytes 2360217 | tf_op jit(solution)/shard_map/attention_backward/pallas_call | solution.py:621
  810.0 6.3 fusion.237
  816.3 7.6 matmul_half.28
  824.0 8.0 matmul_half.30
  842.1 14.2 %collective-permute-done.73 = f32[2048]{0:T(1024)S(1)} collective-permute-done((f32[2048]{0:T(1024)S(1)}, f32[2048]{0:T(1024)S(1)}, u32[]{:S(2)}, u32[]{:S(2)}) %collective-permute-start.73) | collective-permute-done | bytes 8224 | tf_op jit(solution)/shard_map/ppermute | solution.py:703
  856.9 5.3 fusion.72
  875.2 20.4 %collective-permute-done.88 = f32[50,704]{1,0:T(8,128)S(1)} collective-permute-done((f32[50,704]{1,0:T(8,128)S(1)}, f32[50,704]{1,0:T(8,128)S(1)}, u32[]{:S(2)}, u32[]{:S(2)}) %collective-permute-start.88) | collective-permute-done | bytes 140832 | tf_op jit(solution)/shard_map/ppermute | solution.py:703
  917.6 9.0 matmul_half.31
  939.7 6.2 collective-permute-start.82
  948.2 7.3 collective-permute-done.83
  960.2 8.8 matmul_half.29
  973.9 5.5 collective-permute-done.85
  990.0 16.4 %collective-permute-done.74 = bf16[1024,512]{1,0:T(8,128)(2,1)} collective-permute-done((bf16[1024,512]{1,0:T(8,128)(2,1)}, bf16[1024,512]{1,0:T(8,128)(2,1)}, u32[]{:S(2)}, u32[]{:S(2)}) %collective-permute-start.74) | collective-permute-done | bytes 1048608 | tf_op jit(solution)/shard_map/ppermute | solution.py:703
  1011.5 8.8 collective-permute-done.77
  (916 shorter events, 379.0 us)
Async XLA Ops:
  3.0 27.8 %collective-permute-start.4 = (bf16[96,128]{1,0:T(8,128)(2,1)S(1)}, bf16[96,128]{1,0:T(8,128)(2,1)S(1)}, u32[]{:S(2)}, u32[]{:S(2)}) collective-permute-start(bf16[96,128]{1,0:T(8,128)(2,1)S(1)} %pad_maximum_fusion.31), channel_id=1, source_target_pairs={{0,2},{1,3},{2,0},{3,1},{4,6},{5,7},{6,4},{7,5},{8,10},{9,11},{10,... | collective-permute-start | bytes 73736 | tf_op jit(solution)/shard_map/ppermute | solution.py:753
  32.1 134.0 %collective-permute-start.2 = (bf16[1024,512]{1,0:T(8,128)(2,1)}, bf16[1024,512]{1,0:T(8,128)(2,1)S(1)}, u32[]{:S(2)}, u32[]{:S(2)}) collective-permute-start(bf16[1024,512]{1,0:T(8,128)(2,1)} %pad_maximum_fusion.6.refs_0_), channel_id=1, source_target_pairs={{0,1},{1,0},{2,3},{3,2},{4,5},{5,4},{6,7},{7,6},{8,9},{9,8},{10,11... | collective-permute-start | bytes 3145736 | tf_op jit(solution)/shard_map/ppermute | solution.py:703
  32.1 91.4 %collective-permute-start.1 = (bf16[1024,512]{1,0:T(8,128)(2,1)}, bf16[1024,512]{1,0:T(8,128)(2,1)}, u32[]{:S(2)}, u32[]{:S(2)}) collective-permute-start(bf16[1024,512]{1,0:T(8,128)(2,1)} %pad_maximum_fusion.6.refs_0_), channel_id=1, source_target_pairs={{0,4},{1,5},{2,6},{3,7},{4,0},{5,1},{6,2},{7,3},{8,12},{9,13},{10,... | collective-permute-start | bytes 3145736 | tf_op jit(solution)/shard_map/ppermute | solution.py:703
  37.2 25.4 %collective-permute-start.11 = (bf16[2,96,128]{2,1,0:T(8,128)(2,1)S(1)}, bf16[2,96,128]{2,1,0:T(8,128)(2,1)S(1)}, u32[]{:S(2)}, u32[]{:S(2)}) collective-permute-start(bf16[2,96,128]{2,1,0:T(8,128)(2,1)S(1)} %pad_maximum_fusion.25), channel_id=1, source_target_pairs={{0,4},{1,5},{2,6},{3,7},{4,0},{5,1},{6,2},{7,3},{8,12},{9,13},{10,... | collective-permute-start | bytes 147464 | tf_op jit(solution)/shard_map/ppermute | solution.py:753
  39.3 128.6 %collective-permute-start.35 = (bf16[1024,512]{1,0:T(8,128)(2,1)S(1)}, bf16[1024,512]{1,0:T(8,128)(2,1)}, u32[]{:S(2)}, u32[]{:S(2)}) collective-permute-start(bf16[1024,512]{1,0:T(8,128)(2,1)S(1)} %pad_maximum_fusion.7.refs_0_), channel_id=1, source_target_pairs={{0,4},{1,5},{2,6},{3,7},{4,0},{5,1},{6,2},{7,3},{8,12},{9,13},{10,... | collective-permute-start | bytes 3145736 | tf_op jit(solution)/shard_map/ppermute | solution.py:703
  60.6 55.9 %collective-permute-start.8 = (bf16[3,512,256]{2,1,0:T(8,128)(2,1)}, bf16[3,512,256]{2,1,0:T(8,128)(2,1)}, u32[]{:S(2)}, u32[]{:S(2)}) collective-permute-start(bf16[3,512,256]{2,1,0:T(8,128)(2,1)} %get-tuple-element.326), channel_id=1, source_target_pairs={{0,2},{1,3},{2,0},{3,1},{4,6},{5,7},{6,4},{7,5},{8,10},{9,11},{10,... | collective-permute-start | bytes 2359304 | tf_op jit(solution)/shard_map/ppermute | solution.py:703
  123.5 29.8 %collective-permute-start.9 = (bf16[3,512,256]{2,1,0:T(8,128)(2,1)}, bf16[3,512,256]{2,1,0:T(8,128)(2,1)}, u32[]{:S(2)}, u32[]{:S(2)}) collective-permute-start(bf16[3,512,256]{2,1,0:T(8,128)(2,1)} %collective-permute-done.7.rest_0_), channel_id=1, source_target_pairs={{0,8},{8,0},{16,24},{24,16},{1,9},{9,1},{17,25},{25,17},{2,10},{10... | collective-permute-start | bytes 2359304 | tf_op jit(solution)/shard_map/ppermute | solution.py:783
  123.5 44.4 %collective-permute-start.3 = (bf16[1024,512]{1,0:T(8,128)(2,1)}, bf16[1024,512]{1,0:T(8,128)(2,1)}, u32[]{:S(2)}, u32[]{:S(2)}) collective-permute-start(bf16[1024,512]{1,0:T(8,128)(2,1)} %collective-permute-done.1.refs_1_), channel_id=1, source_target_pairs={{0,1},{1,0},{2,3},{3,2},{4,5},{5,4},{6,7},{7,6},{8,9},{9,8},{10,11... | collective-permute-start | bytes 3145736 | tf_op jit(solution)/shard_map/ppermute | solution.py:703
  137.3 48.6 %collective-permute-start.19 = (bf16[256,2048]{1,0:T(8,128)(2,1)}, bf16[256,2048]{1,0:T(8,128)(2,1)}, u32[]{:S(2)}, u32[]{:S(2)}) collective-permute-start(bf16[256,2048]{1,0:T(8,128)(2,1)} %param.19), channel_id=1, source_target_pairs={{0,2},{1,3},{2,0},{3,1},{4,6},{5,7},{6,4},{7,5},{8,10},{9,11},{10,... | collective-permute-start | bytes 3145736 | tf_op jit(solution)/shard_map/ppermute | solution.py:703
  153.2 29.9 %collective-permute-start.38 = (bf16[1024,256]{1,0:T(8,128)(2,1)}, bf16[1024,256]{1,0:T(8,128)(2,1)S(1)}, u32[]{:S(2)}, u32[]{:S(2)}) collective-permute-start(bf16[1024,256]{1,0:T(8,128)(2,1)} %get-tuple-element.329), channel_id=1, source_target_pairs={{0,2},{1,3},{2,0},{3,1},{4,6},{5,7},{6,4},{7,5},{8,10},{9,11},{10,... | collective-permute-start | bytes 1572872 | tf_op jit(solution)/shard_map/ppermute | solution.py:703
  166.1 28.7 %collective-permute-start.15 = (bf16[1024,256]{1,0:T(8,128)(2,1)S(1)}, bf16[1024,256]{1,0:T(8,128)(2,1)S(1)}, u32[]{:S(2)}, u32[]{:S(2)}) collective-permute-start(bf16[1024,256]{1,0:T(8,128)(2,1)S(1)} %get-tuple-element.331), channel_id=1, source_target_pairs={{0,2},{1,3},{2,0},{3,1},{4,6},{5,7},{6,4},{7,5},{8,10},{9,11},{10,... | collective-permute-start | bytes 1572872 | tf_op jit(solution)/shard_map/ppermute | solution.py:703
  167.9 30.1 %collective-permute-start.36 = (bf16[1024,512]{1,0:T(8,128)(2,1)S(1)}, bf16[1024,512]{1,0:T(8,128)(2,1)}, u32[]{:S(2)}, u32[]{:S(2)}) collective-permute-start(bf16[1024,512]{1,0:T(8,128)(2,1)S(1)} %pad_maximum_fusion.7.refs_0_), channel_id=1, source_target_pairs={{0,1},{1,0},{2,3},{3,2},{4,5},{5,4},{6,7},{7,6},{8,9},{9,8},{10,11... | collective-permute-start | bytes 3145736 | tf_op jit(solution)/shard_map/ppermute | solution.py:703
  167.9 67.3 %collective-permute-start.37 = (bf16[1024,512]{1,0:T(8,128)(2,1)}, bf16[1024,512]{1,0:T(8,128)(2,1)}, u32[]{:S(2)}, u32[]{:S(2)}) collective-permute-start(bf16[1024,512]{1,0:T(8,128)(2,1)} %collective-permute-done.35.refs_1_), channel_id=1, source_target_pairs={{0,1},{1,0},{2,3},{3,2},{4,5},{5,4},{6,7},{7,6},{8,9},{9,8},{10,11... | collective-permute-start | bytes 3145736 | tf_op jit(solution)/shard_map/ppermute | solution.py:703
  183.1 51.7 %collective-permute-start.44 = (bf16[352,2048]{1,0:T(8,128)(2,1)}, bf16[352,2048]{1,0:T(8,128)(2,1)}, u32[]{:S(2)}, u32[]{:S(2)}) collective-permute-start(bf16[352,2048]{1,0:T(8,128)(2,1)} %constant_dynamic-slice_fusion.2), channel_id=1, source_target_pairs={{0,2},{1,3},{2,0},{3,1},{4,6},{5,7},{6,4},{7,5},{8,10},{9,11},{10,... | collective-permute-start | bytes 4325384 | tf_op jit(solution)/shard_map/ppermute | solution.py:703
  185.8 49.5 %collective-permute-start.39 = (bf16[1024,512]{1,0:T(8,128)(2,1)}, bf16[1024,512]{1,0:T(8,128)(2,1)}, u32[]{:S(2)}, u32[]{:S(2)}) collective-permute-start(bf16[1024,512]{1,0:T(8,128)(2,1)} %pad_maximum_fusion.10.refs_0_), channel_id=1, source_target_pairs={{0,4},{1,5},{2,6},{3,7},{4,0},{5,1},{6,2},{7,3},{8,12},{9,13},{10,... | collective-permute-start | bytes 3145736 | tf_op jit(solution)/shard_map/ppermute | solution.py:703
  196.2 37.4 %collective-permute-start.16 = (bf16[1024,512]{1,0:T(8,128)(2,1)}, bf16[1024,512]{1,0:T(8,128)(2,1)}, u32[]{:S(2)}, u32[]{:S(2)}) collective-permute-start(bf16[1024,512]{1,0:T(8,128)(2,1)} %pad_maximum_fusion.9.refs_0_), channel_id=1, source_target_pairs={{0,4},{1,5},{2,6},{3,7},{4,0},{5,1},{6,2},{7,3},{8,12},{9,13},{10,... | collective-permute-start | bytes 3145736 | tf_op jit(solution)/shard_map/ppermute | solution.py:703
  198.0 35.5 %collective-permute-start.22 = (f32[1,2048]{1,0:T(1,128)S(1)}, f32[1,2048]{1,0:T(1,128)S(1)}, u32[]{:S(2)}, u32[]{:S(2)}) collective-permute-start(f32[1,2048]{1,0:T(1,128)S(1)} %bitcast_add_fusion.1), channel_id=1, source_target_pairs={{0,4},{1,5},{2,6},{3,7},{4,0},{5,1},{6,2},{7,3},{8,12},{9,13},{10,... | collective-permute-start | bytes 24584 | tf_op jit(solution)/shard_map/ppermute | solution.py:703
  234.8 66.4 %collective-permute-start.45 = (bf16[352,2048]{1,0:T(8,128)(2,1)}, bf16[352,2048]{1,0:T(8,128)(2,1)}, u32[]{:S(2)}, u32[]{:S(2)}) collective-permute-start(bf16[352,2048]{1,0:T(8,128)(2,1)} %collective-permute-done.44.rest_0_), channel_id=1, source_target_pairs={{0,8},{8,0},{16,24},{24,16},{1,9},{9,1},{17,25},{25,17},{2,10},{10... | collective-permute-start | bytes 4325384 | tf_op jit(solution)/shard_map/ppermute | solution.py:783
  235.2 39.2 %collective-permute-start.40 = (bf16[1024,512]{1,0:T(8,128)(2,1)}, bf16[1024,512]{1,0:T(8,128)(2,1)S(1)}, u32[]{:S(2)}, u32[]{:S(2)}) collective-permute-start(bf16[1024,512]{1,0:T(8,128)(2,1)} %pad_maximum_fusion.10.refs_0_), channel_id=1, source_target_pairs={{0,1},{1,0},{2,3},{3,2},{4,5},{5,4},{6,7},{7,6},{8,9},{9,8},{10,11... | collective-permute-start | bytes 3145736 | tf_op jit(solution)/shard_map/ppermute | solution.py:703
  235.3 40.7 %collective-permute-start.41 = (bf16[1024,512]{1,0:T(8,128)(2,1)}, bf16[1024,512]{1,0:T(8,128)(2,1)S(1)}, u32[]{:S(2)}, u32[]{:S(2)}) collective-permute-start(bf16[1024,512]{1,0:T(8,128)(2,1)} %collective-permute-done.39.refs_1_), channel_id=1, source_target_pairs={{0,1},{1,0},{2,3},{3,2},{4,5},{5,4},{6,7},{7,6},{8,9},{9,8},{10,11... | collective-permute-start | bytes 3145736 | tf_op jit(solution)/shard_map/ppermute | solution.py:703
  252.4 78.3 %collective-permute-start.28 = (bf16[1,352,2048]{2,1,0:T(8,128)(2,1)}, bf16[1,352,2048]{2,1,0:T(8,128)(2,1)}, u32[]{:S(2)}, u32[]{:S(2)}) collective-permute-start(bf16[1,352,2048]{2,1,0:T(8,128)(2,1)} %get-tuple-element.318), channel_id=1, source_target_pairs={{0,2},{1,3},{2,0},{3,1},{4,6},{5,7},{6,4},{7,5},{8,10},{9,11},{10,... | collective-permute-start | bytes 4325384 | tf_op jit(solution)/shard_map/ppermute | solution.py:703
  271.3 50.8 %collective-permute-start.20 = (bf16[1024,1024]{1,0:T(8,128)(2,1)}, bf16[1024,1024]{1,0:T(8,128)(2,1)S(1)}, u32[]{:S(2)}, u32[]{:S(2)}) collective-permute-start(bf16[1024,1024]{1,0:T(8,128)(2,1)} %matmul_half.16), channel_id=1, source_target_pairs={{0,1},{1,0},{2,3},{3,2},{4,5},{5,4},{6,7},{7,6},{8,9},{9,8},{10,11... | collective-permute-start | bytes 6291464 | tf_op jit(solution)/shard_map/ppermute | solution.py:703
  274.4 56.3 %collective-permute-start.27 = (bf16[1,352,2048]{2,1,0:T(8,128)(2,1)}, bf16[1,352,2048]{2,1,0:T(8,128)(2,1)}, u32[]{:S(2)}, u32[]{:S(2)}) collective-permute-start(bf16[1,352,2048]{2,1,0:T(8,128)(2,1)} %get-tuple-element.319), channel_id=1, source_target_pairs={{0,2},{1,3},{2,0},{3,1},{4,6},{5,7},{6,4},{7,5},{8,10},{9,11},{10,... | collective-permute-start | bytes 4325384 | tf_op jit(solution)/shard_map/ppermute | solution.py:703
  314.9 44.2 %collective-permute-start.42 = (bf16[1024,1024]{1,0:T(8,128)(2,1)}, bf16[1024,1024]{1,0:T(8,128)(2,1)}, u32[]{:S(2)}, u32[]{:S(2)}) collective-permute-start(bf16[1024,1024]{1,0:T(8,128)(2,1)} %matmul_half.18), channel_id=1, source_target_pairs={{0,1},{1,0},{2,3},{3,2},{4,5},{5,4},{6,7},{7,6},{8,9},{9,8},{10,11... | collective-permute-start | bytes 6291464 | tf_op jit(solution)/shard_map/ppermute | solution.py:703
  330.7 37.6 %collective-permute-start.30 = (bf16[1,352,2048]{2,1,0:T(8,128)(2,1)}, bf16[1,352,2048]{2,1,0:T(8,128)(2,1)}, u32[]{:S(2)}, u32[]{:S(2)}) collective-permute-start(bf16[1,352,2048]{2,1,0:T(8,128)(2,1)} %collective-permute-done.28), channel_id=1, source_target_pairs={{0,8},{8,0},{16,24},{24,16},{1,9},{9,1},{17,25},{25,17},{2,10},{10... | collective-permute-start | bytes 4325384 | tf_op jit(solution)/shard_map/ppermute | solution.py:783
  330.7 63.5 %collective-permute-start.29 = (bf16[1,352,2048]{2,1,0:T(8,128)(2,1)}, bf16[1,352,2048]{2,1,0:T(8,128)(2,1)}, u32[]{:S(2)}, u32[]{:S(2)}) collective-permute-start(bf16[1,352,2048]{2,1,0:T(8,128)(2,1)} %collective-permute-done.27), channel_id=1, source_target_pairs={{0,8},{8,0},{16,24},{24,16},{1,9},{9,1},{17,25},{25,17},{2,10},{10... | collective-permute-start | bytes 4325384 | tf_op jit(solution)/shard_map/ppermute | solution.py:783
  354.0 55.3 %collective-permute-start.24 = (bf16[1024,512]{1,0:T(8,128)(2,1)S(1)}, bf16[1024,512]{1,0:T(8,128)(2,1)}, u32[]{:S(2)}, u32[]{:S(2)}) collective-permute-start(bf16[1024,512]{1,0:T(8,128)(2,1)S(1)} %get-tuple-element.276.refs_0_), channel_id=1, source_target_pairs={{0,4},{1,5},{2,6},{3,7},{4,0},{5,1},{6,2},{7,3},{8,12},{9,13},{10,... | collective-permute-start | bytes 3145736 | tf_op jit(solution)/shard_map/ppermute | solution.py:703
  363.3 52.1 %collective-permute-start.43 = (bf16[1024,512]{1,0:T(8,128)(2,1)}, bf16[1024,512]{1,0:T(8,128)(2,1)}, u32[]{:S(2)}, u32[]{:S(2)}) collective-permute-start(bf16[1024,512]{1,0:T(8,128)(2,1)} %get-tuple-element.145), channel_id=1, source_target_pairs={{0,4},{1,5},{2,6},{3,7},{4,0},{5,1},{6,2},{7,3},{8,12},{9,13},{10,... | collective-permute-start | bytes 3145736 | tf_op jit(solution)/shard_map/ppermute | solution.py:703
  419.1 60.3 %collective-permute-start.51 = (bf16[1024,512]{1,0:T(8,128)(2,1)S(1)}, bf16[1024,512]{1,0:T(8,128)(2,1)}, u32[]{:S(2)}, u32[]{:S(2)}) collective-permute-start(bf16[1024,512]{1,0:T(8,128)(2,1)S(1)} %get-tuple-element.160.refs_0_), channel_id=1, source_target_pairs={{0,4},{1,5},{2,6},{3,7},{4,0},{5,1},{6,2},{7,3},{8,12},{9,13},{10,... | collective-permute-start | bytes 3145736 | tf_op jit(solution)/shard_map/ppermute | solution.py:703
  501.8 95.4 %collective-permute-start.59 = (bf16[1024,512]{1,0:T(8,128)(2,1)}, bf16[1024,512]{1,0:T(8,128)(2,1)}, u32[]{:S(2)}, u32[]{:S(2)}) collective-permute-start(bf16[1024,512]{1,0:T(8,128)(2,1)} %get-tuple-element.180), channel_id=1, source_target_pairs={{0,4},{1,5},{2,6},{3,7},{4,0},{5,1},{6,2},{7,3},{8,12},{9,13},{10,... | collective-permute-start | bytes 3145736 | tf_op jit(solution)/shard_map/ppermute | solution.py:703
  557.6 34.8 %collective-permute-start.55 = (f32[1024]{0:T(1024)}, f32[1024]{0:T(1024)}, u32[]{:S(2)}, u32[]{:S(2)}) collective-permute-start(f32[1024]{0:T(1024)} %slice_reduce_fusion), channel_id=1, source_target_pairs={{0,1},{1,0},{2,3},{3,2},{4,5},{5,4},{6,7},{7,6},{8,9},{9,8},{10,11... | collective-permute-start | bytes 12296 | tf_op jit(solution)/shard_map/ppermute | solution.py:703
  574.7 27.5 %collective-permute-start.54 = (bf16[1024,1024]{1,0:T(8,128)(2,1)}, bf16[1024,1024]{1,0:T(8,128)(2,1)}, u32[]{:S(2)}, u32[]{:S(2)}) collective-permute-start(bf16[1024,1024]{1,0:T(8,128)(2,1)} %matmul_half.22), channel_id=1, source_target_pairs={{0,1},{1,0},{2,3},{3,2},{4,5},{5,4},{6,7},{7,6},{8,9},{9,8},{10,11... | collective-permute-start | bytes 6291464 | tf_op jit(solution)/shard_map/ppermute | solution.py:703
  642.6 65.5 %collective-permute-start.58 = (bf16[1024,1024]{1,0:T(8,128)(2,1)}, bf16[1024,1024]{1,0:T(8,128)(2,1)}, u32[]{:S(2)}, u32[]{:S(2)}) collective-permute-start(bf16[1024,1024]{1,0:T(8,128)(2,1)} %matmul_half.26), channel_id=1, source_target_pairs={{0,1},{1,0},{2,3},{3,2},{4,5},{5,4},{6,7},{7,6},{8,9},{9,8},{10,11... | collective-permute-start | bytes 6291464 | tf_op jit(solution)/shard_map/ppermute | solution.py:703
  656.4 26.0 %collective-permute-start.64 = (bf16[1024,512]{1,0:T(8,128)(2,1)S(1)}, bf16[1024,512]{1,0:T(8,128)(2,1)S(1)}, u32[]{:S(2)}, u32[]{:S(2)}) collective-permute-start(bf16[1024,512]{1,0:T(8,128)(2,1)S(1)} %get-tuple-element.195.refs_0_), channel_id=1, source_target_pairs={{0,4},{1,5},{2,6},{3,7},{4,0},{5,1},{6,2},{7,3},{8,12},{9,13},{10,... | collective-permute-start | bytes 3145736 | tf_op jit(solution)/shard_map/ppermute | solution.py:703
  657.9 46.0 %collective-permute-start.60 = (bf16[1024,512]{1,0:T(8,128)(2,1)S(1)}, bf16[1024,512]{1,0:T(8,128)(2,1)S(1)}, u32[]{:S(2)}, u32[]{:S(2)}) collective-permute-start(bf16[1024,512]{1,0:T(8,128)(2,1)S(1)} %get-tuple-element.191.refs_0_), channel_id=1, source_target_pairs={{0,4},{1,5},{2,6},{3,7},{4,0},{5,1},{6,2},{7,3},{8,12},{9,13},{10,... | collective-permute-start | bytes 3145736 | tf_op jit(solution)/shard_map/ppermute | solution.py:703
  664.5 57.8 %collective-permute-start.65 = (bf16[1024,512]{1,0:T(8,128)(2,1)S(1)}, bf16[1024,512]{1,0:T(8,128)(2,1)}, u32[]{:S(2)}, u32[]{:S(2)}) collective-permute-start(bf16[1024,512]{1,0:T(8,128)(2,1)S(1)} %get-tuple-element.195.refs_0_), channel_id=1, source_target_pairs={{0,1},{1,0},{2,3},{3,2},{4,5},{5,4},{6,7},{7,6},{8,9},{9,8},{10,11... | collective-permute-start | bytes 3145736 | tf_op jit(solution)/shard_map/ppermute | solution.py:703
  664.5 57.8 %collective-permute-start.61 = (bf16[1024,512]{1,0:T(8,128)(2,1)S(1)}, bf16[1024,512]{1,0:T(8,128)(2,1)S(1)}, u32[]{:S(2)}, u32[]{:S(2)}) collective-permute-start(bf16[1024,512]{1,0:T(8,128)(2,1)S(1)} %get-tuple-element.191.refs_0_), channel_id=1, source_target_pairs={{0,1},{1,0},{2,3},{3,2},{4,5},{5,4},{6,7},{7,6},{8,9},{9,8},{10,11... | collective-permute-start | bytes 3145736 | tf_op jit(solution)/shard_map/ppermute | solution.py:703
  682.4 40.0 %collective-permute-start.66 = (bf16[1024,512]{1,0:T(8,128)(2,1)S(1)}, bf16[1024,512]{1,0:T(8,128)(2,1)S(1)}, u32[]{:S(2)}, u32[]{:S(2)}) collective-permute-start(bf16[1024,512]{1,0:T(8,128)(2,1)S(1)} %collective-permute-done.64.refs_1_), channel_id=1, source_target_pairs={{0,1},{1,0},{2,3},{3,2},{4,5},{5,4},{6,7},{7,6},{8,9},{9,8},{10,11... | collective-permute-start | bytes 3145736 | tf_op jit(solution)/shard_map/ppermute | solution.py:703
  807.8 30.5 %collective-permute-start.72 = (f32[2048]{0:T(1024)S(1)}, f32[2048]{0:T(1024)S(1)}, u32[]{:S(2)}, u32[]{:S(2)}) collective-permute-start(f32[2048]{0:T(1024)S(1)} %reduce_sum.138), channel_id=1, source_target_pairs={{0,1},{1,0},{2,3},{3,2},{4,5},{5,4},{6,7},{7,6},{8,9},{9,8},{10,11... | collective-permute-start | bytes 24584 | tf_op jit(solution)/shard_map/ppermute | solution.py:703
  808.0 48.9 %collective-permute-start.67 = (bf16[1024,512]{1,0:T(8,128)(2,1)}, bf16[1024,512]{1,0:T(8,128)(2,1)}, u32[]{:S(2)}, u32[]{:S(2)}) collective-permute-start(bf16[1024,512]{1,0:T(8,128)(2,1)} %get-tuple-element.186), channel_id=1, source_target_pairs={{0,4},{1,5},{2,6},{3,7},{4,0},{5,1},{6,2},{7,3},{8,12},{9,13},{10,... | collective-permute-start | bytes 3145736 | tf_op jit(solution)/shard_map/ppermute | solution.py:703
  809.5 47.4 %collective-permute-start.68 = (bf16[1024,512]{1,0:T(8,128)(2,1)}, bf16[1024,512]{1,0:T(8,128)(2,1)}, u32[]{:S(2)}, u32[]{:S(2)}) collective-permute-start(bf16[1024,512]{1,0:T(8,128)(2,1)} %get-tuple-element.188), channel_id=1, source_target_pairs={{0,4},{1,5},{2,6},{3,7},{4,0},{5,1},{6,2},{7,3},{8,12},{9,13},{10,... | collective-permute-start | bytes 3145736 | tf_op jit(solution)/shard_map/ppermute | solution.py:703
  832.0 85.6 %collective-permute-start.75 = (bf16[1024,1024]{1,0:T(8,128)(2,1)}, bf16[1024,1024]{1,0:T(8,128)(2,1)}, u32[]{:S(2)}, u32[]{:S(2)}) collective-permute-start(bf16[1024,1024]{1,0:T(8,128)(2,1)} %matmul_half.30), channel_id=1, source_target_pairs={{0,1},{1,0},{2,3},{3,2},{4,5},{5,4},{6,7},{7,6},{8,9},{9,8},{10,11... | collective-permute-start | bytes 6291464 | tf_op jit(solution)/shard_map/ppermute | solution.py:703
  832.1 85.5 %collective-permute-start.71 = (bf16[1024,1024]{1,0:T(8,128)(2,1)}, bf16[1024,1024]{1,0:T(8,128)(2,1)}, u32[]{:S(2)}, u32[]{:S(2)}) collective-permute-start(bf16[1024,1024]{1,0:T(8,128)(2,1)} %matmul_half.28), channel_id=1, source_target_pairs={{0,1},{1,0},{2,3},{3,2},{4,5},{5,4},{6,7},{7,6},{8,9},{9,8},{10,11... | collective-permute-start | bytes 6291464 | tf_op jit(solution)/shard_map/ppermute | solution.py:703
  866.4 48.0 %collective-permute-start.69 = (bf16[1024,256]{1,0:T(8,128)(2,1)}, bf16[1024,256]{1,0:T(8,128)(2,1)}, u32[]{:S(2)}, u32[]{:S(2)}) collective-permute-start(bf16[1024,256]{1,0:T(8,128)(2,1)} %get-tuple-element.345), channel_id=1, source_target_pairs={{0,2},{1,3},{2,0},{3,1},{4,6},{5,7},{6,4},{7,5},{8,10},{9,11},{10,... | collective-permute-start | bytes 1572872 | tf_op jit(solution)/shard_map/ppermute | solution.py:703
  868.5 45.8 %collective-permute-start.70 = (bf16[1024,256]{1,0:T(8,128)(2,1)}, bf16[1024,256]{1,0:T(8,128)(2,1)}, u32[]{:S(2)}, u32[]{:S(2)}) collective-permute-start(bf16[1024,256]{1,0:T(8,128)(2,1)} %get-tuple-element.347), channel_id=1, source_target_pairs={{0,2},{1,3},{2,0},{3,1},{4,6},{5,7},{6,4},{7,5},{8,10},{9,11},{10,... | collective-permute-start | bytes 1572872 | tf_op jit(solution)/shard_map/ppermute | solution.py:703
  959.5 26.4 %collective-permute-start.76 = (bf16[1024,512]{1,0:T(8,128)(2,1)}, bf16[1024,512]{1,0:T(8,128)(2,1)}, u32[]{:S(2)}, u32[]{:S(2)}) collective-permute-start(bf16[1024,512]{1,0:T(8,128)(2,1)} %get-tuple-element.211), channel_id=1, source_target_pairs={{0,4},{1,5},{2,6},{3,7},{4,0},{5,1},{6,2},{7,3},{8,12},{9,13},{10,... | collective-permute-start | bytes 3145736 | tf_op jit(solution)/shard_map/ppermute | solution.py:703
  969.0 37.3 %collective-permute-start.74 = (bf16[1024,512]{1,0:T(8,128)(2,1)}, bf16[1024,512]{1,0:T(8,128)(2,1)}, u32[]{:S(2)}, u32[]{:S(2)}) collective-permute-start(bf16[1024,512]{1,0:T(8,128)(2,1)} %get-tuple-element.205), channel_id=1, source_target_pairs={{0,4},{1,5},{2,6},{3,7},{4,0},{5,1},{6,2},{7,3},{8,12},{9,13},{10,... | collective-permute-start | bytes 3145736 | tf_op jit(solution)/shard_map/ppermute | solution.py:703
  983.8 25.0 %collective-permute-start.87 = (f32[181,64]{0,1:T(8,128)S(1)}, f32[181,64]{0,1:T(8,128)S(1)}, u32[]{:S(2)}, u32[]{:S(2)}) collective-permute-start(f32[181,64]{0,1:T(8,128)S(1)} %add_bitcast_fusion), channel_id=1, source_target_pairs={{0,0},{1,4},{2,8},{3,12},{4,16},{5,20},{6,24},{7,28},{8,1},{9,5},{... | collective-permute-start | bytes 139016 | tf_op jit(solution)/shard_map/ppermute | solution.py:1020
  (252 other events, 4333.1 us)

commit v3 on v2

--- a/solution.py
+++ b/solution.py
@@ -21,7 +21,7 @@
 BK = 256
 HEADS_FORWARD = 2
 HEADS_BACKWARD = 2
-COST = 0.15
+COST = 0.07
 F32 = jnp.float32
 BF16 = jnp.bfloat16
 

time: 1040 us -> 1040 us (level); the launches traced: 1020 us -> 1040 us
  Pallas kernels: 380 us -> 393 us
    ppermute x5, waiting for transfers between devices: 47.3 us -> 70.6 us  [fetch(): lax.ppermute(v, 'dp', [(i, i ^ 1) for i in range(n_dp)])]
    ppermute x71, waiting for transfers between devices: 172 us -> 149 us  [flip(): return lax.ppermute(values, 'mp', [(i, i ^ mask) for i in range(n_mp)])]
  transfers between devices with their start and end apart: 92 -> 92, of which waited for: 31 -> 32; matrix products, arithmetic and copies ran while one was open for 22% -> 23% of each run, Pallas kernels for 29% -> 29%
where the time goes in v3:
time: 1040 us
  Pallas kernels  393 us (38%)
  waiting for transfers between devices  278 us (27%)
  matrix products  110 us (11%)
  other arithmetic  108 us (10%)
  local copies, waits for them, and re-layouts  73 us (7%)
  starting transfers between devices  70.4 us (7%)
    ppermute x71, waiting for transfers between devices, flip(): return lax.ppermute(values, 'mp', [(i, i ^ mask) for i in range(n_mp)])  149 us
    pallas_call x16, Pallas kernels, matmul(): pl.pallas_call(body, out_shape=outs, grid=(rows // bm, count), in_specs=s...  127 us
    dot_general x72, matrix products, dot(): return lax.dot_general(a, b, dims, preferred_element_type=F32)  110 us
    ppermute x5, waiting for transfers between devices, fetch(): lax.ppermute(v, 'dp', [(i, i ^ 1) for i in range(n_dp)])  70.6 us
    pallas_call x1, Pallas kernels, attention_backward(): pl.pallas_call(body, out_shape=outs, grid_spec=pltpu.PrefetchScalarGridSp...  58.6 us
    ppermute x71, starting transfers between devices, flip(): return lax.ppermute(values, 'mp', [(i, i ^ mask) for i in range(n_mp)])  53.1 us
    pallas_call x2, Pallas kernels, project_hidden(): pl.pallas_call(body, out_shape=outs, grid=(rows // bm,), in_specs=[pl.Blo...  46.1 us
    ppermute x10, waiting for transfers between devices, spread_step(): theirs = lax.ppermute(values, axis, [(i, i ^ 1 << k) for i in range(count)])  45.9 us
  transfers between devices with their start and end apart: 92, of which 32 were waited for; matrix products, arithmetic and copies ran while one was open for 23% of the time, Pallas kernels for 29%

profile of v3, /device:TPU:0, one launch (start us, length us, event | category | flops | bytes accessed | tf_op | source)
XLA Modules:
  0.0 1037.1 jit_solution(15259371773947922261)
XLA Ops:
  13.9 5.2 subtract_convert_fusion
  40.7 19.5 %collective-permute-done.31 = bf16[2,50,176]{2,1,0:T(8,128)(2,1)S(1)} collective-permute-done((bf16[2,50,176]{2,1,0:T(8,128)(2,1)S(1)}, bf16[2,50,176]{2,1,0:T(8,128)(2,1)S(1)}, u32[]{:S(2)}, u32[]{:S(2)}) %collective-permute-start.31) | collective-permute-done | bytes 35232 | tf_op jit(solution)/shard_map/ppermute | solution.py:753
  74.0 8.6 collective-permute-done.33
  82.8 10.7 %collective-permute-done.13 = bf16[2,2,2,96,128]{4,3,2,1,0:T(8,128)(2,1)S(1)} collective-permute-done((bf16[2,2,2,96,128]{4,3,2,1,0:T(8,128)(2,1)S(1)}, bf16[2,2,2,96,128]{4,3,2,1,0:T(8,128)(2,1)S(1)}, u32[]{:S(2)}, u32[]{:S(2)}) %collective-permute-start.13) | collective-permute-done | bytes 196640 | tf_op jit(solution)/shard_map/ppermute | solution.py:753
  132.0 10.4 %collective-permute-done.10.rest_3_ = bf16[3,512,256]{2,1,0:T(8,128)(2,1)} collective-permute-done((bf16[3,512,256]{2,1,0:T(8,128)(2,1)}, bf16[3,512,256]{2,1,0:T(8,128)(2,1)}, u32[]{:S(2)}, u32[]{:S(2)}) %collective-permute-start.10) | collective-permute-done | bytes 786464 | tf_op jit(solution)/shard_map/ppermute | solution.py:783
  144.1 13.4 %collective-permute-done.9.rest_2_ = bf16[3,512,256]{2,1,0:T(8,128)(2,1)} collective-permute-done((bf16[3,512,256]{2,1,0:T(8,128)(2,1)}, bf16[3,512,256]{2,1,0:T(8,128)(2,1)}, u32[]{:S(2)}, u32[]{:S(2)}) %collective-permute-start.9) | collective-permute-done | bytes 786464 | tf_op jit(solution)/shard_map/ppermute | solution.py:783
  159.1 11.2 %merge_columns.1 = (bf16[3,2048,512]{2,1,0:T(8,128)(2,1)}, f32[3,1,512]{2,1,0:T(1,128)}) custom-call(s32[9]{0:T(128)} %pad_add_fusion.1.perm_ref, bf16[3,2048,256]{2,1,0:T(8,128)(2,1)} %own_ref.1, bf16[3,512,256]{2,1,0:T(8,128)(2,1)} %collective-permute-done.7.rest_0_, bf16[3,512,256]{2,1,0:T(8,128)(2,1)} %collective-permute-done.8.rest_1_, ...), custom_call_target="tpu_custom_call" | custom-call | flops 28185722 | bytes 880803 | tf_op jit(solution)/shard_map/merge_columns/pallas_call | solution.py:92
  172.6 13.5 %project_qkv.2 = (bf16[1024,1536]{1,0:T(8,128)(2,1)}, bf16[1024,128]{1,0:T(8,128)(2,1)}, f32[1024,128]{1,0:T(8,128)}) custom-call(bf16[1024,512]{1,0:T(8,128)(2,1)} %pad_maximum_fusion.6.refs_0_, bf16[1024,512]{1,0:T(8,128)(2,1)} %collective-permute-done.1.refs_1_, bf16[1024,512]{1,0:T(8,128)(2,1)} %copy-done.65, ...), custom_call_target="tpu_custom_call" | custom-call | flops 450971552 | bytes 1009254 | tf_op jit(solution)/shard_map/project_qkv/pallas_call | solution.py:233
  189.1 5.9 collective-permute-done.15
  196.8 7.4 merge_rows.3
  209.5 24.9 %collective-permute-done.38 = bf16[1024,256]{1,0:T(8,128)(2,1)S(1)} collective-permute-done((bf16[1024,256]{1,0:T(8,128)(2,1)}, bf16[1024,256]{1,0:T(8,128)(2,1)S(1)}, u32[]{:S(2)}, u32[]{:S(2)}) %collective-permute-start.38) | collective-permute-done | bytes 524320 | tf_op jit(solution)/shard_map/ppermute | solution.py:703
  244.9 13.5 %project_qkv.3 = (bf16[1024,1536]{1,0:T(8,128)(2,1)}, bf16[1024,128]{1,0:T(8,128)(2,1)}, f32[1024,128]{1,0:T(8,128)}) custom-call(bf16[1024,512]{1,0:T(8,128)(2,1)} %copy-done.5, bf16[1024,512]{1,0:T(8,128)(2,1)} %collective-permute-done.35.refs_1_, bf16[1024,512]{1,0:T(8,128)(2,1)} %collective-permute-done.36.refs_2_, ...), custom_call_target="tpu_custom_call" | custom-call | flops 450971552 | bytes 1009254 | tf_op jit(solution)/shard_map/project_qkv/pallas_call | solution.py:233
  261.4 16.0 %attention_forward.2 = (bf16[1024,512]{1,0:T(8,128)(2,1)}, f32[4,1,1024]{2,1,0:T(1,128)}) custom-call(s32[9]{0:T(128)} %pad_add_fusion.table_ref, bf16[1024,1536]{1,0:T(8,128)(2,1)} %get-tuple-element.190.q_ref, bf16[1024,512]{1,0:T(8,128)(2,1)} %get-tuple-element.323.k_ref, bf16[1024,512]{1,0:T(8,128)(2,1)} %get-tuple-element.322.v_ref, s32[1,2048]{1,0:T(1,128)} %copy-done.156), custom_call_target="tpu_custom_call" | custom-call | flops 75161928 | bytes 221347 | tf_op jit(solution)/shard_map/attention_forward/pallas_call | solution.py:504
  282.5 9.8 merge_rows.5
  307.2 29.6 %attention_forward.3 = (bf16[1024,512]{1,0:T(8,128)(2,1)}, f32[4,1,1024]{2,1,0:T(1,128)}) custom-call(s32[9]{0:T(128)} %pad_add_fusion.table_ref, bf16[1024,1536]{1,0:T(8,128)(2,1)} %get-tuple-element.141.q_ref, bf16[2048,512]{1,0:T(8,128)(2,1)} %pad_maximum_fusion.1.k_ref, bf16[2048,512]{1,0:T(8,128)(2,1)} %pad_maximum_fusion.2.v_ref, s32[1,2048]{1,0:T(1,128)} %copy-done.156), custom_call_target="tpu_custom_call" | custom-call | flops 150323856 | bytes 368148 | tf_op jit(solution)/shard_map/attention_forward/pallas_call | solution.py:504
  360.7 16.5 %collective-permute-done.30 = bf16[1,352,2048]{2,1,0:T(8,128)(2,1)} collective-permute-done((bf16[1,352,2048]{2,1,0:T(8,128)(2,1)}, bf16[1,352,2048]{2,1,0:T(8,128)(2,1)}, u32[]{:S(2)}, u32[]{:S(2)}) %collective-permute-start.30) | collective-permute-done | bytes 1441824 | tf_op jit(solution)/shard_map/ppermute | solution.py:783
  377.3 30.2 %collective-permute-done.29 = bf16[1,352,2048]{2,1,0:T(8,128)(2,1)} collective-permute-done((bf16[1,352,2048]{2,1,0:T(8,128)(2,1)}, bf16[1,352,2048]{2,1,0:T(8,128)(2,1)}, u32[]{:S(2)}, u32[]{:S(2)}) %collective-permute-start.29) | collective-permute-done | bytes 1441824 | tf_op jit(solution)/shard_map/ppermute | solution.py:783
  407.5 15.0 %merge_rows.4 = (bf16[2,1408,2048]{2,1,0:T(8,128)(2,1)}, f32[2,1408,1]{2,1,0:T(8,128)}) custom-call(s32[9]{0:T(128)} %pad_add_fusion.1.perm_ref, bf16[2,704,2048]{2,1,0:T(8,128)(2,1)} %bitcast.401, bf16[352,2048]{1,0:T(8,128)(2,1)} %bitcast.39.rest_0_, bf16[352,2048]{1,0:T(8,128)(2,1)} %bitcast.40.rest_1_, bf16[352,2048]{1,0:T(8,128)(2,1)} %bitcast.41.rest_2_, ...), custom_call_target="tpu_custom_call" | custom-call | flops 51673824 | bytes 1614807 | tf_op jit(solution)/shard_map/merge_rows/pallas_call | solution.py:178
  434.0 23.0 %project_hidden.2 = (bf16[1024,1408]{1,0:T(8,128)(2,1)}, bf16[1024,1408]{1,0:T(8,128)(2,1)}, bf16[1024,1408]{1,0:T(8,128)(2,1)}, bf16[1024,128]{1,0:T(8,128)(2,1...) custom-call(bf16[1024,512]{1,0:T(8,128)(2,1)} %copy-done.39, bf16[1024,512]{1,0:T(8,128)(2,1)} %collective-permute-done.24.refs_1_, ...), custom_call_target="tpu_custom_call" | custom-call | flops 826781184 | bytes 1779957 | tf_op jit(solution)/shard_map/project_hidden/pallas_call | solution.py:288
  457.0 16.5 %hidden_backward.2 = (bf16[2,1024,1408]{2,1,0:T(8,128)(2,1)}, f32[2,1,1408]{2,1,0:T(1,128)}, f32[1024,128]{1,0:T(8,128)}, bf16[1024,128]{1,0:T(8,128)(2,1)}) custom-call(bf16[1024,512]{1,0:T(8,128)(2,1)} %copy-done.27, bf16[1024,512]{1,0:T(8,128)(2,1)} %collective-permute-done.16.refs_1_, bf16[1024,512]{1,0:T(8,128)(2,1)} %collective-permute-done.17.refs_2_, ...), custom_call_target="tpu_custom_call" | custom-call | flops 413390592 | bytes 1560545 | tf_op jit(solution)/shard_map/hidden_backward/pallas_call | solution.py:345
  473.5 12.0 %matmul_half.20 = bf16[1024,1024]{1,0:T(8,128)(2,1)} custom-call(bf16[2,1024,1408]{2,1,0:T(8,128)(2,1)} %get-tuple-element.214.left_ref, bf16[2,1408,2048]{2,1,0:T(8,128)(2,1)} %get-tuple-element.136.refs_4_.right_ref), custom_call_target="tpu_custom_call" | custom-call | flops 413390592 | bytes 954204 | tf_op jit(solution)/shard_map/matmul_half/pallas_call | solution.py:414
  503.6 12.5 %matmul_half.21 = (f32[1024,512]{1,0:T(8,128)}, bf16[1024,512]{1,0:T(8,128)(2,1)}) custom-call(bf16[2,1024,1408]{2,1,0:T(8,128)(2,1)} %get-tuple-element.214.left_ref, bf16[2,1408,2048]{2,1,0:T(8,128)(2,1)} %get-tuple-element.136.refs_4_.right_ref, bf16[1024,1024]{1,0:T(8,128)(2,1)} %collective-permute-done.48.rest_0_), custom_call_target="tpu_custom_call" | custom-call | flops 413390592 | bytes 1027604 | tf_op jit(solution)/shard_map/matmul_half/pallas_call | solution.py:414
  518.7 23.2 %project_hidden.3 = (bf16[1024,1408]{1,0:T(8,128)(2,1)}, bf16[1024,1408]{1,0:T(8,128)(2,1)}, bf16[1024,1408]{1,0:T(8,128)(2,1)}, bf16[1024,128]{1,0:T(8,128)(2,1...) custom-call(bf16[1024,512]{1,0:T(8,128)(2,1)} %copy-done.40, bf16[1024,512]{1,0:T(8,128)(2,1)} %collective-permute-done.51.refs_1_, ...), custom_call_target="tpu_custom_call" | custom-call | flops 826781184 | bytes 1779957 | tf_op jit(solution)/shard_map/project_hidden/pallas_call | solution.py:288
  551.4 16.7 %hidden_backward.3 = (bf16[2,1024,1408]{2,1,0:T(8,128)(2,1)}, f32[2,1,1408]{2,1,0:T(1,128)}, f32[1024,128]{1,0:T(8,128)}, bf16[1024,128]{1,0:T(8,128)(2,1)}) custom-call(bf16[1024,512]{1,0:T(8,128)(2,1)} %pad_maximum_fusion.10.refs_0_, bf16[1024,512]{1,0:T(8,128)(2,1)} %collective-permute-done.39.refs_1_, bf16[1024,512]{1,0:T(8,128)(2,1)} %collective-permute-done.40.refs_2_, ...), custom_call_target="tpu_custom_call" | custom-call | flops 413390592 | bytes 1560545 | tf_op jit(solution)/shard_map/hidden_backward/pallas_call | solution.py:345
  575.6 11.5 %matmul_half.22 = bf16[1024,1024]{1,0:T(8,128)(2,1)} custom-call(bf16[2,1024,1408]{2,1,0:T(8,128)(2,1)} %get-tuple-element.215.left_ref, bf16[2,1408,2048]{2,1,0:T(8,128)(2,1)} %get-tuple-element.136.refs_4_.right_ref), custom_call_target="tpu_custom_call" | custom-call | flops 413390592 | bytes 954204 | tf_op jit(solution)/shard_map/matmul_half/pallas_call | solution.py:414
  594.2 4.9 fusion.55
  609.7 4.9 multiply_reduce_fusion.1
  614.7 13.6 %matmul_half.23 = (f32[1024,512]{1,0:T(8,128)}, bf16[1024,512]{1,0:T(8,128)(2,1)}) custom-call(bf16[2,1024,1408]{2,1,0:T(8,128)(2,1)} %get-tuple-element.215.left_ref, bf16[2,1408,2048]{2,1,0:T(8,128)(2,1)} %get-tuple-element.136.refs_4_.right_ref, bf16[1024,1024]{1,0:T(8,128)(2,1)} %collective-permute-done.54.rest_0_), custom_call_target="tpu_custom_call" | custom-call | flops 413390592 | bytes 1027604 | tf_op jit(solution)/shard_map/matmul_half/pallas_call | solution.py:414
  642.1 7.0 matmul_half.26
  649.1 7.0 matmul_half.24
  678.6 17.3 %collective-permute-done.64.refs_1_ = bf16[1024,512]{1,0:T(8,128)(2,1)S(1)} collective-permute-done((bf16[1024,512]{1,0:T(8,128)(2,1)S(1)}, bf16[1024,512]{1,0:T(8,128)(2,1)S(1)}, u32[]{:S(2)}, u32[]{:S(2)}) %collective-permute-start.64) | collective-permute-done | bytes 1048608 | tf_op jit(solution)/shard_map/ppermute | solution.py:703
  695.8 21.5 %collective-permute-done.60.refs_1_ = bf16[1024,512]{1,0:T(8,128)(2,1)S(1)} collective-permute-done((bf16[1024,512]{1,0:T(8,128)(2,1)S(1)}, bf16[1024,512]{1,0:T(8,128)(2,1)S(1)}, u32[]{:S(2)}, u32[]{:S(2)}) %collective-permute-start.60) | collective-permute-done | bytes 1048608 | tf_op jit(solution)/shard_map/ppermute | solution.py:703
  721.6 7.0 matmul_half.25
  728.6 7.2 matmul_half.27
  741.2 5.8 matmul_parts.3
  747.0 5.9 matmul_parts.2
  755.7 58.6 %attention_backward.1 = (bf16[3,2048,512]{2,1,0:T(8,128)(2,1)}, f32[3,1,512]{2,1,0:T(1,128)}, f32[2048,128]{1,0:T(8,128)}) custom-call(s32[9]{0:T(128)} %pad_add_fusion.table_ref, bf16[2048,1536]{1,0:T(8,128)(2,1)} %pad_maximum_fusion.q_ref.k_ref.v_ref, bf16[2048,1536]{1,0:T(8,128)(2,1)} %pad_maximum_fusion.q_ref.k_ref.v_ref, ...), custom_call_target="tpu_custom_call" | custom-call | flops 751619264 | bytes 1101434 | tf_op jit(solution)/shard_map/attention_backward/pallas_call | solution.py:621
  829.9 6.3 fusion.237
  836.2 7.7 matmul_half.28
  843.9 8.0 matmul_half.30
  860.9 15.3 %collective-permute-done.73 = f32[2048]{0:T(1024)S(1)} collective-permute-done((f32[2048]{0:T(1024)S(1)}, f32[2048]{0:T(1024)S(1)}, u32[]{:S(2)}, u32[]{:S(2)}) %collective-permute-start.73) | collective-permute-done | bytes 8224 | tf_op jit(solution)/shard_map/ppermute | solution.py:703
  876.8 5.3 fusion.72
  895.0 19.4 %collective-permute-done.88 = f32[50,704]{1,0:T(8,128)S(1)} collective-permute-done((f32[50,704]{1,0:T(8,128)S(1)}, f32[50,704]{1,0:T(8,128)S(1)}, u32[]{:S(2)}, u32[]{:S(2)}) %collective-permute-start.88) | collective-permute-done | bytes 140832 | tf_op jit(solution)/shard_map/ppermute | solution.py:703
  933.4 9.0 matmul_half.31
  963.4 5.3 collective-permute-done.83
  976.0 8.8 matmul_half.29
  1004.1 17.7 %collective-permute-done.74 = bf16[1024,512]{1,0:T(8,128)(2,1)} collective-permute-done((bf16[1024,512]{1,0:T(8,128)(2,1)}, bf16[1024,512]{1,0:T(8,128)(2,1)}, u32[]{:S(2)}, u32[]{:S(2)}) %collective-permute-start.74) | collective-permute-done | bytes 1048608 | tf_op jit(solution)/shard_map/ppermute | solution.py:703
  1026.7 8.4 collective-permute-done.77
  (928 shorter events, 384.5 us)
Async XLA Ops:
  3.0 27.6 %collective-permute-start.4 = (bf16[96,128]{1,0:T(8,128)(2,1)S(1)}, bf16[96,128]{1,0:T(8,128)(2,1)S(1)}, u32[]{:S(2)}, u32[]{:S(2)}) collective-permute-start(bf16[96,128]{1,0:T(8,128)(2,1)S(1)} %pad_maximum_fusion.31), channel_id=1, source_target_pairs={{0,2},{1,3},{2,0},{3,1},{4,6},{5,7},{6,4},{7,5},{8,10},{9,11},{10,... | collective-permute-start | bytes 73736 | tf_op jit(solution)/shard_map/ppermute | solution.py:753
  31.8 139.8 %collective-permute-start.2 = (bf16[1024,512]{1,0:T(8,128)(2,1)}, bf16[1024,512]{1,0:T(8,128)(2,1)S(1)}, u32[]{:S(2)}, u32[]{:S(2)}) collective-permute-start(bf16[1024,512]{1,0:T(8,128)(2,1)} %pad_maximum_fusion.6.refs_0_), channel_id=1, source_target_pairs={{0,1},{1,0},{2,3},{3,2},{4,5},{5,4},{6,7},{7,6},{8,9},{9,8},{10,11... | collective-permute-start | bytes 3145736 | tf_op jit(solution)/shard_map/ppermute | solution.py:703
  31.8 91.9 %collective-permute-start.1 = (bf16[1024,512]{1,0:T(8,128)(2,1)}, bf16[1024,512]{1,0:T(8,128)(2,1)}, u32[]{:S(2)}, u32[]{:S(2)}) collective-permute-start(bf16[1024,512]{1,0:T(8,128)(2,1)} %pad_maximum_fusion.6.refs_0_), channel_id=1, source_target_pairs={{0,4},{1,5},{2,6},{3,7},{4,0},{5,1},{6,2},{7,3},{8,12},{9,13},{10,... | collective-permute-start | bytes 3145736 | tf_op jit(solution)/shard_map/ppermute | solution.py:703
  37.3 24.6 %collective-permute-start.11 = (bf16[2,96,128]{2,1,0:T(8,128)(2,1)S(1)}, bf16[2,96,128]{2,1,0:T(8,128)(2,1)S(1)}, u32[]{:S(2)}, u32[]{:S(2)}) collective-permute-start(bf16[2,96,128]{2,1,0:T(8,128)(2,1)S(1)} %pad_maximum_fusion.25), channel_id=1, source_target_pairs={{0,4},{1,5},{2,6},{3,7},{4,0},{5,1},{6,2},{7,3},{8,12},{9,13},{10,... | collective-permute-start | bytes 147464 | tf_op jit(solution)/shard_map/ppermute | solution.py:753
  39.4 203.7 %collective-permute-start.36 = (bf16[1024,512]{1,0:T(8,128)(2,1)S(1)}, bf16[1024,512]{1,0:T(8,128)(2,1)}, u32[]{:S(2)}, u32[]{:S(2)}) collective-permute-start(bf16[1024,512]{1,0:T(8,128)(2,1)S(1)} %pad_maximum_fusion.7.refs_0_), channel_id=1, source_target_pairs={{0,1},{1,0},{2,3},{3,2},{4,5},{5,4},{6,7},{7,6},{8,9},{9,8},{10,11... | collective-permute-start | bytes 3145736 | tf_op jit(solution)/shard_map/ppermute | solution.py:703
  60.1 61.5 %collective-permute-start.8 = (bf16[3,512,256]{2,1,0:T(8,128)(2,1)}, bf16[3,512,256]{2,1,0:T(8,128)(2,1)}, u32[]{:S(2)}, u32[]{:S(2)}) collective-permute-start(bf16[3,512,256]{2,1,0:T(8,128)(2,1)} %get-tuple-element.326), channel_id=1, source_target_pairs={{0,2},{1,3},{2,0},{3,1},{4,6},{5,7},{6,4},{7,5},{8,10},{9,11},{10,... | collective-permute-start | bytes 2359304 | tf_op jit(solution)/shard_map/ppermute | solution.py:703
  121.7 35.8 %collective-permute-start.9 = (bf16[3,512,256]{2,1,0:T(8,128)(2,1)}, bf16[3,512,256]{2,1,0:T(8,128)(2,1)}, u32[]{:S(2)}, u32[]{:S(2)}) collective-permute-start(bf16[3,512,256]{2,1,0:T(8,128)(2,1)} %collective-permute-done.7.rest_0_), channel_id=1, source_target_pairs={{0,8},{8,0},{16,24},{24,16},{1,9},{9,1},{17,25},{25,17},{2,10},{10... | collective-permute-start | bytes 2359304 | tf_op jit(solution)/shard_map/ppermute | solution.py:783
  123.7 48.4 %collective-permute-start.3 = (bf16[1024,512]{1,0:T(8,128)(2,1)}, bf16[1024,512]{1,0:T(8,128)(2,1)}, u32[]{:S(2)}, u32[]{:S(2)}) collective-permute-start(bf16[1024,512]{1,0:T(8,128)(2,1)} %collective-permute-done.1.refs_1_), channel_id=1, source_target_pairs={{0,1},{1,0},{2,3},{3,2},{4,5},{5,4},{6,7},{7,6},{8,9},{9,8},{10,11... | collective-permute-start | bytes 3145736 | tf_op jit(solution)/shard_map/ppermute | solution.py:703
  142.4 63.4 %collective-permute-start.35 = (bf16[1024,512]{1,0:T(8,128)(2,1)S(1)}, bf16[1024,512]{1,0:T(8,128)(2,1)}, u32[]{:S(2)}, u32[]{:S(2)}) collective-permute-start(bf16[1024,512]{1,0:T(8,128)(2,1)S(1)} %pad_maximum_fusion.7.refs_0_), channel_id=1, source_target_pairs={{0,4},{1,5},{2,6},{3,7},{4,0},{5,1},{6,2},{7,3},{8,12},{9,13},{10,... | collective-permute-start | bytes 3145736 | tf_op jit(solution)/shard_map/ppermute | solution.py:703
  157.5 39.3 %collective-permute-start.19 = (bf16[256,2048]{1,0:T(8,128)(2,1)}, bf16[256,2048]{1,0:T(8,128)(2,1)}, u32[]{:S(2)}, u32[]{:S(2)}) collective-permute-start(bf16[256,2048]{1,0:T(8,128)(2,1)} %param.19), channel_id=1, source_target_pairs={{0,2},{1,3},{2,0},{3,1},{4,6},{5,7},{6,4},{7,5},{8,10},{9,11},{10,... | collective-permute-start | bytes 3145736 | tf_op jit(solution)/shard_map/ppermute | solution.py:703
  171.6 23.4 %collective-permute-start.15 = (bf16[1024,256]{1,0:T(8,128)(2,1)S(1)}, bf16[1024,256]{1,0:T(8,128)(2,1)S(1)}, u32[]{:S(2)}, u32[]{:S(2)}) collective-permute-start(bf16[1024,256]{1,0:T(8,128)(2,1)S(1)} %get-tuple-element.331), channel_id=1, source_target_pairs={{0,2},{1,3},{2,0},{3,1},{4,6},{5,7},{6,4},{7,5},{8,10},{9,11},{10,... | collective-permute-start | bytes 1572872 | tf_op jit(solution)/shard_map/ppermute | solution.py:703
  187.4 48.7 %collective-permute-start.44 = (bf16[352,2048]{1,0:T(8,128)(2,1)}, bf16[352,2048]{1,0:T(8,128)(2,1)}, u32[]{:S(2)}, u32[]{:S(2)}) collective-permute-start(bf16[352,2048]{1,0:T(8,128)(2,1)} %constant_dynamic-slice_fusion.2), channel_id=1, source_target_pairs={{0,2},{1,3},{2,0},{3,1},{4,6},{5,7},{6,4},{7,5},{8,10},{9,11},{10,... | collective-permute-start | bytes 4325384 | tf_op jit(solution)/shard_map/ppermute | solution.py:703
  195.1 43.0 %collective-permute-start.16 = (bf16[1024,512]{1,0:T(8,128)(2,1)S(1)}, bf16[1024,512]{1,0:T(8,128)(2,1)}, u32[]{:S(2)}, u32[]{:S(2)}) collective-permute-start(bf16[1024,512]{1,0:T(8,128)(2,1)S(1)} %pad_maximum_fusion.9.refs_0_), channel_id=1, source_target_pairs={{0,4},{1,5},{2,6},{3,7},{4,0},{5,1},{6,2},{7,3},{8,12},{9,13},{10,... | collective-permute-start | bytes 3145736 | tf_op jit(solution)/shard_map/ppermute | solution.py:703
  205.9 28.5 %collective-permute-start.38 = (bf16[1024,256]{1,0:T(8,128)(2,1)}, bf16[1024,256]{1,0:T(8,128)(2,1)S(1)}, u32[]{:S(2)}, u32[]{:S(2)}) collective-permute-start(bf16[1024,256]{1,0:T(8,128)(2,1)} %get-tuple-element.329), channel_id=1, source_target_pairs={{0,2},{1,3},{2,0},{3,1},{4,6},{5,7},{6,4},{7,5},{8,10},{9,11},{10,... | collective-permute-start | bytes 1572872 | tf_op jit(solution)/shard_map/ppermute | solution.py:703
  207.4 35.9 %collective-permute-start.37 = (bf16[1024,512]{1,0:T(8,128)(2,1)}, bf16[1024,512]{1,0:T(8,128)(2,1)}, u32[]{:S(2)}, u32[]{:S(2)}) collective-permute-start(bf16[1024,512]{1,0:T(8,128)(2,1)} %collective-permute-done.35.refs_1_), channel_id=1, source_target_pairs={{0,1},{1,0},{2,3},{3,2},{4,5},{5,4},{6,7},{7,6},{8,9},{9,8},{10,11... | collective-permute-start | bytes 3145736 | tf_op jit(solution)/shard_map/ppermute | solution.py:703
  236.1 46.4 %collective-permute-start.45 = (bf16[352,2048]{1,0:T(8,128)(2,1)}, bf16[352,2048]{1,0:T(8,128)(2,1)}, u32[]{:S(2)}, u32[]{:S(2)}) collective-permute-start(bf16[352,2048]{1,0:T(8,128)(2,1)} %collective-permute-done.44.rest_0_), channel_id=1, source_target_pairs={{0,8},{8,0},{16,24},{24,16},{1,9},{9,1},{17,25},{25,17},{2,10},{10... | collective-permute-start | bytes 4325384 | tf_op jit(solution)/shard_map/ppermute | solution.py:783
  243.1 64.1 %collective-permute-start.40 = (bf16[1024,512]{1,0:T(8,128)(2,1)}, bf16[1024,512]{1,0:T(8,128)(2,1)}, u32[]{:S(2)}, u32[]{:S(2)}) collective-permute-start(bf16[1024,512]{1,0:T(8,128)(2,1)} %pad_maximum_fusion.10.refs_0_), channel_id=1, source_target_pairs={{0,1},{1,0},{2,3},{3,2},{4,5},{5,4},{6,7},{7,6},{8,9},{9,8},{10,11... | collective-permute-start | bytes 3145736 | tf_op jit(solution)/shard_map/ppermute | solution.py:703
  243.2 52.4 %collective-permute-start.39 = (bf16[1024,512]{1,0:T(8,128)(2,1)}, bf16[1024,512]{1,0:T(8,128)(2,1)}, u32[]{:S(2)}, u32[]{:S(2)}) collective-permute-start(bf16[1024,512]{1,0:T(8,128)(2,1)} %pad_maximum_fusion.10.refs_0_), channel_id=1, source_target_pairs={{0,4},{1,5},{2,6},{3,7},{4,0},{5,1},{6,2},{7,3},{8,12},{9,13},{10,... | collective-permute-start | bytes 3145736 | tf_op jit(solution)/shard_map/ppermute | solution.py:703
  259.9 82.6 %collective-permute-start.28 = (bf16[1,352,2048]{2,1,0:T(8,128)(2,1)}, bf16[1,352,2048]{2,1,0:T(8,128)(2,1)}, u32[]{:S(2)}, u32[]{:S(2)}) collective-permute-start(bf16[1,352,2048]{2,1,0:T(8,128)(2,1)} %get-tuple-element.318), channel_id=1, source_target_pairs={{0,2},{1,3},{2,0},{3,1},{4,6},{5,7},{6,4},{7,5},{8,10},{9,11},{10,... | collective-permute-start | bytes 4325384 | tf_op jit(solution)/shard_map/ppermute | solution.py:703
  295.6 46.9 %collective-permute-start.27 = (bf16[1,352,2048]{2,1,0:T(8,128)(2,1)}, bf16[1,352,2048]{2,1,0:T(8,128)(2,1)}, u32[]{:S(2)}, u32[]{:S(2)}) collective-permute-start(bf16[1,352,2048]{2,1,0:T(8,128)(2,1)} %get-tuple-element.319), channel_id=1, source_target_pairs={{0,2},{1,3},{2,0},{3,1},{4,6},{5,7},{6,4},{7,5},{8,10},{9,11},{10,... | collective-permute-start | bytes 4325384 | tf_op jit(solution)/shard_map/ppermute | solution.py:703
  305.2 39.4 %collective-permute-start.23 = (bf16[1024,512]{1,0:T(8,128)(2,1)}, bf16[1024,512]{1,0:T(8,128)(2,1)S(1)}, u32[]{:S(2)}, u32[]{:S(2)}) collective-permute-start(bf16[1024,512]{1,0:T(8,128)(2,1)} %get-tuple-element.132), channel_id=1, source_target_pairs={{0,4},{1,5},{2,6},{3,7},{4,0},{5,1},{6,2},{7,3},{8,12},{9,13},{10,... | collective-permute-start | bytes 3145736 | tf_op jit(solution)/shard_map/ppermute | solution.py:703
  342.5 34.7 %collective-permute-start.30 = (bf16[1,352,2048]{2,1,0:T(8,128)(2,1)}, bf16[1,352,2048]{2,1,0:T(8,128)(2,1)}, u32[]{:S(2)}, u32[]{:S(2)}) collective-permute-start(bf16[1,352,2048]{2,1,0:T(8,128)(2,1)} %collective-permute-done.28), channel_id=1, source_target_pairs={{0,8},{8,0},{16,24},{24,16},{1,9},{9,1},{17,25},{25,17},{2,10},{10... | collective-permute-start | bytes 4325384 | tf_op jit(solution)/shard_map/ppermute | solution.py:783
  342.5 65.0 %collective-permute-start.29 = (bf16[1,352,2048]{2,1,0:T(8,128)(2,1)}, bf16[1,352,2048]{2,1,0:T(8,128)(2,1)}, u32[]{:S(2)}, u32[]{:S(2)}) collective-permute-start(bf16[1,352,2048]{2,1,0:T(8,128)(2,1)} %collective-permute-done.27), channel_id=1, source_target_pairs={{0,8},{8,0},{16,24},{24,16},{1,9},{9,1},{17,25},{25,17},{2,10},{10... | collective-permute-start | bytes 4325384 | tf_op jit(solution)/shard_map/ppermute | solution.py:783
  346.5 76.2 %collective-permute-start.24 = (bf16[1024,512]{1,0:T(8,128)(2,1)S(1)}, bf16[1024,512]{1,0:T(8,128)(2,1)}, u32[]{:S(2)}, u32[]{:S(2)}) collective-permute-start(bf16[1024,512]{1,0:T(8,128)(2,1)S(1)} %get-tuple-element.276.refs_0_), channel_id=1, source_target_pairs={{0,4},{1,5},{2,6},{3,7},{4,0},{5,1},{6,2},{7,3},{8,12},{9,13},{10,... | collective-permute-start | bytes 3145736 | tf_op jit(solution)/shard_map/ppermute | solution.py:703
  359.2 69.7 %collective-permute-start.43 = (bf16[1024,512]{1,0:T(8,128)(2,1)}, bf16[1024,512]{1,0:T(8,128)(2,1)}, u32[]{:S(2)}, u32[]{:S(2)}) collective-permute-start(bf16[1024,512]{1,0:T(8,128)(2,1)} %get-tuple-element.145), channel_id=1, source_target_pairs={{0,4},{1,5},{2,6},{3,7},{4,0},{5,1},{6,2},{7,3},{8,12},{9,13},{10,... | collective-permute-start | bytes 3145736 | tf_op jit(solution)/shard_map/ppermute | solution.py:703
  432.5 61.2 %collective-permute-start.51 = (bf16[1024,512]{1,0:T(8,128)(2,1)S(1)}, bf16[1024,512]{1,0:T(8,128)(2,1)}, u32[]{:S(2)}, u32[]{:S(2)}) collective-permute-start(bf16[1024,512]{1,0:T(8,128)(2,1)S(1)} %get-tuple-element.160.refs_0_), channel_id=1, source_target_pairs={{0,4},{1,5},{2,6},{3,7},{4,0},{5,1},{6,2},{7,3},{8,12},{9,13},{10,... | collective-permute-start | bytes 3145736 | tf_op jit(solution)/shard_map/ppermute | solution.py:703
  493.2 23.4 %collective-permute-start.52 = (bf16[1024,512]{1,0:T(8,128)(2,1)S(1)}, bf16[1024,512]{1,0:T(8,128)(2,1)S(1)}, u32[]{:S(2)}, u32[]{:S(2)}) collective-permute-start(bf16[1024,512]{1,0:T(8,128)(2,1)S(1)} %get-tuple-element.160.refs_0_), channel_id=1, source_target_pairs={{0,1},{1,0},{2,3},{3,2},{4,5},{5,4},{6,7},{7,6},{8,9},{9,8},{10,11... | collective-permute-start | bytes 3145736 | tf_op jit(solution)/shard_map/ppermute | solution.py:703
  516.1 93.6 %collective-permute-start.59 = (bf16[1024,512]{1,0:T(8,128)(2,1)}, bf16[1024,512]{1,0:T(8,128)(2,1)}, u32[]{:S(2)}, u32[]{:S(2)}) collective-permute-start(bf16[1024,512]{1,0:T(8,128)(2,1)} %get-tuple-element.180), channel_id=1, source_target_pairs={{0,4},{1,5},{2,6},{3,7},{4,0},{5,1},{6,2},{7,3},{8,12},{9,13},{10,... | collective-permute-start | bytes 3145736 | tf_op jit(solution)/shard_map/ppermute | solution.py:703
  570.0 34.8 %collective-permute-start.55 = (f32[1024]{0:T(1024)}, f32[1024]{0:T(1024)}, u32[]{:S(2)}, u32[]{:S(2)}) collective-permute-start(f32[1024]{0:T(1024)} %slice_reduce_fusion), channel_id=1, source_target_pairs={{0,1},{1,0},{2,3},{3,2},{4,5},{5,4},{6,7},{7,6},{8,9},{9,8},{10,11... | collective-permute-start | bytes 12296 | tf_op jit(solution)/shard_map/ppermute | solution.py:703
  587.1 27.6 %collective-permute-start.54 = (bf16[1024,1024]{1,0:T(8,128)(2,1)}, bf16[1024,1024]{1,0:T(8,128)(2,1)}, u32[]{:S(2)}, u32[]{:S(2)}) collective-permute-start(bf16[1024,1024]{1,0:T(8,128)(2,1)} %matmul_half.22), channel_id=1, source_target_pairs={{0,1},{1,0},{2,3},{3,2},{4,5},{5,4},{6,7},{7,6},{8,9},{9,8},{10,11... | collective-permute-start | bytes 6291464 | tf_op jit(solution)/shard_map/ppermute | solution.py:703
  640.5 25.2 %collective-permute-start.63 = (bf16[1024,512]{1,0:T(8,128)(2,1)}, bf16[1024,512]{1,0:T(8,128)(2,1)}, u32[]{:S(2)}, u32[]{:S(2)}) collective-permute-start(bf16[1024,512]{1,0:T(8,128)(2,1)} %get-tuple-element.183), channel_id=1, source_target_pairs={{0,4},{1,5},{2,6},{3,7},{4,0},{5,1},{6,2},{7,3},{8,12},{9,13},{10,... | collective-permute-start | bytes 3145736 | tf_op jit(solution)/shard_map/ppermute | solution.py:703
  656.0 65.5 %collective-permute-start.58 = (bf16[1024,1024]{1,0:T(8,128)(2,1)}, bf16[1024,1024]{1,0:T(8,128)(2,1)}, u32[]{:S(2)}, u32[]{:S(2)}) collective-permute-start(bf16[1024,1024]{1,0:T(8,128)(2,1)} %matmul_half.26), channel_id=1, source_target_pairs={{0,1},{1,0},{2,3},{3,2},{4,5},{5,4},{6,7},{7,6},{8,9},{9,8},{10,11... | collective-permute-start | bytes 6291464 | tf_op jit(solution)/shard_map/ppermute | solution.py:703
  669.8 26.0 %collective-permute-start.64 = (bf16[1024,512]{1,0:T(8,128)(2,1)S(1)}, bf16[1024,512]{1,0:T(8,128)(2,1)S(1)}, u32[]{:S(2)}, u32[]{:S(2)}) collective-permute-start(bf16[1024,512]{1,0:T(8,128)(2,1)S(1)} %get-tuple-element.195.refs_0_), channel_id=1, source_target_pairs={{0,4},{1,5},{2,6},{3,7},{4,0},{5,1},{6,2},{7,3},{8,12},{9,13},{10,... | collective-permute-start | bytes 3145736 | tf_op jit(solution)/shard_map/ppermute | solution.py:703
  670.3 47.0 %collective-permute-start.60 = (bf16[1024,512]{1,0:T(8,128)(2,1)S(1)}, bf16[1024,512]{1,0:T(8,128)(2,1)S(1)}, u32[]{:S(2)}, u32[]{:S(2)}) collective-permute-start(bf16[1024,512]{1,0:T(8,128)(2,1)S(1)} %get-tuple-element.191.refs_0_), channel_id=1, source_target_pairs={{0,4},{1,5},{2,6},{3,7},{4,0},{5,1},{6,2},{7,3},{8,12},{9,13},{10,... | collective-permute-start | bytes 3145736 | tf_op jit(solution)/shard_map/ppermute | solution.py:703
  678.0 57.8 %collective-permute-start.65 = (bf16[1024,512]{1,0:T(8,128)(2,1)S(1)}, bf16[1024,512]{1,0:T(8,128)(2,1)}, u32[]{:S(2)}, u32[]{:S(2)}) collective-permute-start(bf16[1024,512]{1,0:T(8,128)(2,1)S(1)} %get-tuple-element.195.refs_0_), channel_id=1, source_target_pairs={{0,1},{1,0},{2,3},{3,2},{4,5},{5,4},{6,7},{7,6},{8,9},{9,8},{10,11... | collective-permute-start | bytes 3145736 | tf_op jit(solution)/shard_map/ppermute | solution.py:703
  678.0 57.8 %collective-permute-start.61 = (bf16[1024,512]{1,0:T(8,128)(2,1)S(1)}, bf16[1024,512]{1,0:T(8,128)(2,1)S(1)}, u32[]{:S(2)}, u32[]{:S(2)}) collective-permute-start(bf16[1024,512]{1,0:T(8,128)(2,1)S(1)} %get-tuple-element.191.refs_0_), channel_id=1, source_target_pairs={{0,1},{1,0},{2,3},{3,2},{4,5},{5,4},{6,7},{7,6},{8,9},{9,8},{10,11... | collective-permute-start | bytes 3145736 | tf_op jit(solution)/shard_map/ppermute | solution.py:703
  695.8 40.0 %collective-permute-start.66 = (bf16[1024,512]{1,0:T(8,128)(2,1)S(1)}, bf16[1024,512]{1,0:T(8,128)(2,1)S(1)}, u32[]{:S(2)}, u32[]{:S(2)}) collective-permute-start(bf16[1024,512]{1,0:T(8,128)(2,1)S(1)} %collective-permute-done.64.refs_1_), channel_id=1, source_target_pairs={{0,1},{1,0},{2,3},{3,2},{4,5},{5,4},{6,7},{7,6},{8,9},{9,8},{10,11... | collective-permute-start | bytes 3145736 | tf_op jit(solution)/shard_map/ppermute | solution.py:703
  827.7 30.5 %collective-permute-start.72 = (f32[2048]{0:T(1024)S(1)}, f32[2048]{0:T(1024)S(1)}, u32[]{:S(2)}, u32[]{:S(2)}) collective-permute-start(f32[2048]{0:T(1024)S(1)} %reduce_sum.138), channel_id=1, source_target_pairs={{0,1},{1,0},{2,3},{3,2},{4,5},{5,4},{6,7},{7,6},{8,9},{9,8},{10,11... | collective-permute-start | bytes 24584 | tf_op jit(solution)/shard_map/ppermute | solution.py:703
  827.9 48.9 %collective-permute-start.67 = (bf16[1024,512]{1,0:T(8,128)(2,1)}, bf16[1024,512]{1,0:T(8,128)(2,1)}, u32[]{:S(2)}, u32[]{:S(2)}) collective-permute-start(bf16[1024,512]{1,0:T(8,128)(2,1)} %get-tuple-element.186), channel_id=1, source_target_pairs={{0,4},{1,5},{2,6},{3,7},{4,0},{5,1},{6,2},{7,3},{8,12},{9,13},{10,... | collective-permute-start | bytes 3145736 | tf_op jit(solution)/shard_map/ppermute | solution.py:703
  828.4 48.4 %collective-permute-start.68 = (bf16[1024,512]{1,0:T(8,128)(2,1)}, bf16[1024,512]{1,0:T(8,128)(2,1)}, u32[]{:S(2)}, u32[]{:S(2)}) collective-permute-start(bf16[1024,512]{1,0:T(8,128)(2,1)} %get-tuple-element.188), channel_id=1, source_target_pairs={{0,4},{1,5},{2,6},{3,7},{4,0},{5,1},{6,2},{7,3},{8,12},{9,13},{10,... | collective-permute-start | bytes 3145736 | tf_op jit(solution)/shard_map/ppermute | solution.py:703
  851.9 81.6 %collective-permute-start.75 = (bf16[1024,1024]{1,0:T(8,128)(2,1)}, bf16[1024,1024]{1,0:T(8,128)(2,1)}, u32[]{:S(2)}, u32[]{:S(2)}) collective-permute-start(bf16[1024,1024]{1,0:T(8,128)(2,1)} %matmul_half.30), channel_id=1, source_target_pairs={{0,1},{1,0},{2,3},{3,2},{4,5},{5,4},{6,7},{7,6},{8,9},{9,8},{10,11... | collective-permute-start | bytes 6291464 | tf_op jit(solution)/shard_map/ppermute | solution.py:703
  851.9 81.5 %collective-permute-start.71 = (bf16[1024,1024]{1,0:T(8,128)(2,1)}, bf16[1024,1024]{1,0:T(8,128)(2,1)}, u32[]{:S(2)}, u32[]{:S(2)}) collective-permute-start(bf16[1024,1024]{1,0:T(8,128)(2,1)} %matmul_half.28), channel_id=1, source_target_pairs={{0,1},{1,0},{2,3},{3,2},{4,5},{5,4},{6,7},{7,6},{8,9},{9,8},{10,11... | collective-permute-start | bytes 6291464 | tf_op jit(solution)/shard_map/ppermute | solution.py:703
  885.3 44.9 %collective-permute-start.69 = (bf16[1024,256]{1,0:T(8,128)(2,1)}, bf16[1024,256]{1,0:T(8,128)(2,1)}, u32[]{:S(2)}, u32[]{:S(2)}) collective-permute-start(bf16[1024,256]{1,0:T(8,128)(2,1)} %get-tuple-element.345), channel_id=1, source_target_pairs={{0,2},{1,3},{2,0},{3,1},{4,6},{5,7},{6,4},{7,5},{8,10},{9,11},{10,... | collective-permute-start | bytes 1572872 | tf_op jit(solution)/shard_map/ppermute | solution.py:703
  888.4 41.8 %collective-permute-start.70 = (bf16[1024,256]{1,0:T(8,128)(2,1)}, bf16[1024,256]{1,0:T(8,128)(2,1)}, u32[]{:S(2)}, u32[]{:S(2)}) collective-permute-start(bf16[1024,256]{1,0:T(8,128)(2,1)} %get-tuple-element.347), channel_id=1, source_target_pairs={{0,2},{1,3},{2,0},{3,1},{4,6},{5,7},{6,4},{7,5},{8,10},{9,11},{10,... | collective-permute-start | bytes 1572872 | tf_op jit(solution)/shard_map/ppermute | solution.py:703
  974.2 26.4 %collective-permute-start.76 = (bf16[1024,512]{1,0:T(8,128)(2,1)}, bf16[1024,512]{1,0:T(8,128)(2,1)}, u32[]{:S(2)}, u32[]{:S(2)}) collective-permute-start(bf16[1024,512]{1,0:T(8,128)(2,1)} %get-tuple-element.211), channel_id=1, source_target_pairs={{0,4},{1,5},{2,6},{3,7},{4,0},{5,1},{6,2},{7,3},{8,12},{9,13},{10,... | collective-permute-start | bytes 3145736 | tf_op jit(solution)/shard_map/ppermute | solution.py:703
  984.8 37.0 %collective-permute-start.74 = (bf16[1024,512]{1,0:T(8,128)(2,1)}, bf16[1024,512]{1,0:T(8,128)(2,1)}, u32[]{:S(2)}, u32[]{:S(2)}) collective-permute-start(bf16[1024,512]{1,0:T(8,128)(2,1)} %get-tuple-element.205), channel_id=1, source_target_pairs={{0,4},{1,5},{2,6},{3,7},{4,0},{5,1},{6,2},{7,3},{8,12},{9,13},{10,... | collective-permute-start | bytes 3145736 | tf_op jit(solution)/shard_map/ppermute | solution.py:703
  997.7 26.3 %collective-permute-start.87 = (f32[181,64]{0,1:T(8,128)S(1)}, f32[181,64]{0,1:T(8,128)S(1)}, u32[]{:S(2)}, u32[]{:S(2)}) collective-permute-start(f32[181,64]{0,1:T(8,128)S(1)} %add_bitcast_fusion), channel_id=1, source_target_pairs={{0,0},{1,4},{2,8},{3,12},{4,16},{5,20},{6,24},{7,28},{8,1},{9,5},{... | collective-permute-start | bytes 139016 | tf_op jit(solution)/shard_map/ppermute | solution.py:1020
  1003.3 23.3 %collective-permute-start.78 = (bf16[1024,256]{1,0:T(8,128)(2,1)S(1)}, bf16[1024,256]{1,0:T(8,128)(2,1)S(1)}, u32[]{:S(2)}, u32[]{:S(2)}) collective-permute-start(bf16[1024,256]{1,0:T(8,128)(2,1)S(1)} %get-tuple-element.343), channel_id=1, source_target_pairs={{0,2},{1,3},{2,0},{3,1},{4,6},{5,7},{6,4},{7,5},{8,10},{9,11},{10,... | collective-permute-start | bytes 1572872 | tf_op jit(solution)/shard_map/ppermute | solution.py:703
  (258 other events, 4021.7 us)
